TPU v7x, 256 devices: a whole 4x4x8 slice. The times are simulated.
256 devices in a mesh: gx: 8 (over x, core), gy: 4 (over y), gz: 8 (over z).
Axes of the slice: x: 4, y: 4, z: 8, core: 2. Of those that a mesh axis runs over, the one named last changes fastest.
Arguments:
- charges: float32 [256, 1024, 1024], P('gz', 'gy', 'gx'), may hold values from -8 to 8
- fine_taps: float32 [2, 3, 17], replicated, may hold values from 0.05 to 0.45
- coarse_taps: float32 [2, 3, 17], replicated, may hold values from 0.05 to 0.45
Outputs:
- potential: float32 [256, 1024, 1024], P('gz', 'gy', 'gx')
All inputs are finite; a program needn't handle non-finite values.
Results may differ from a plain program's by a relative error of at most 0.0003.
Values sent between devices are 32-bit elements; how exact they have to be, the bound alone decides.
No kernel may reach another device: no remote copies, remote signals or barrier semaphores. Data moves between devices by JAX's collectives and lax.ppermute only.
A program may use at most 128 MiB of HBM per device.

v0:
```python
import functools
import itertools

import jax
import jax.numpy as jnp
from jax import lax
from jax.experimental import pallas as pl
from jax.experimental.pallas import tpu as pltpu
from jax.sharding import PartitionSpec as P

f32 = jnp.float32
bf16 = jnp.bfloat16
AXES = ("gx", "gy", "gz")
NB = 45
NT = 149
R = 8
TAPS = 17

VM = pl.BlockSpec(memory_space=pltpu.VMEM)
SM = pl.BlockSpec(memory_space=pltpu.SMEM)
PARAMS = pltpu.CompilerParams(vmem_limit_bytes=60 * 1024 * 1024)


def shift(value, axis, step):
    count = lax.axis_size(axis)
    return lax.ppermute(value, axis, [(i, (i + step) % count) for i in range(count)])


def split(a):
    hi = a.astype(bf16)
    lo = (a - hi.astype(f32)).astype(bf16)
    return hi, lo


def mm(a, b):
    return jnp.dot(a, b, preferred_element_type=f32)


def iota(shape, dim):
    return lax.broadcasted_iota(jnp.int32, shape, dim)


def banded(taps, base, delta):
    out = jnp.zeros(delta.shape, f32)
    for k in range(TAPS):
        out = jnp.where(delta == k, taps[base + k], out)
    return out


def tap_base(t, axis):
    return (t * 3 + axis) * TAPS


def x_weights(taps, coarse):
    sh = 1 if coarse else 0
    scale = 0.125 if coarse else 1.0
    edge = 128 >> sh

    def halves(rows, source):
        cols = iota((rows, 128), 1) >> sh
        return jnp.concatenate(
            [banded(taps, tap_base(t, 0), source - cols + R) * scale for t in range(2)], axis=1
        )

    hi, lo = split(halves(128, iota((128, 128), 0) >> sh))
    h = iota((16, 128), 0)
    hhi, hlo = split(halves(16, jnp.where(h < 8, h - 8, h - 8 + edge)))
    return (
        jnp.concatenate([hi, hi], axis=0),
        lo,
        jnp.concatenate([hhi, hhi, hlo], axis=0),
    )


def y_weights(taps, t, coarse):
    seg = 48 if coarse else 80
    c = iota((64, 256), 1)
    i = iota((64, 256), 0) >> (1 if coarse else 0)
    j = c - jnp.where(c >= seg, seg, 0) - jnp.where(c >= 2 * seg, seg, 0)
    m = jnp.where(c < 3 * seg, banded(taps, tap_base(t, 1), j - i), 0.0)
    hi = m.astype(bf16).astype(f32)
    return jnp.where(c < 2 * seg, hi, m - hi).astype(bf16)


def stack(hi, lo):
    pad = jnp.zeros((256 - 3 * hi.shape[0], hi.shape[1]), bf16)
    return jnp.concatenate([hi, lo, hi, pad], axis=0)


def x_block(a, xt, w1, w2, wh):
    hi, lo = split(a)
    xhi, xlo = split(xt)
    x3 = jnp.concatenate([xhi, xlo, xhi], axis=0)
    return (
        mm(jnp.concatenate([hi, lo], axis=1), w1)
        + mm(hi, w2)
        + lax.dot_general(x3, wh, (((0,), (0,)), ((), ())), preferred_element_type=f32)
    )


def pool(ref, z):
    def half(p):
        return ref[p, pl.ds(0, 128, stride=2), :] + ref[p, pl.ds(1, 128, stride=2), :]

    return half(2 * z) + half(2 * z + 1)


def prep_kernel(d, g, ylo, yhi):
    def step(z, acc):
        v = pool(d, z)
        g[z] = v
        return acc + v

    total = lax.fori_loop(0, 16, step, jnp.zeros((128, 128), f32))
    rows = jnp.sum(total.reshape(8, 16, 128), axis=1)
    group = jnp.where((iota((128, 128), 0) >> 5) == iota((128, 128), 1), 0.125, 0.0)
    q = jnp.dot(rows, group, precision=lax.Precision.HIGHEST, preferred_element_type=f32)
    ylo[0:32] = d[:, 0:8, :]
    yhi[0:32] = d[:, 248:256, :]
    ylo[32:48] = g[:, 0:8, :]
    yhi[32:48] = g[:, 120:128, :]
    ylo[48] = q
    yhi[48] = q


def strip_kernel(d, g, yl, yh, q2, xlo, xhi):
    h = iota((16, 256), 0)
    x = iota((16, 256), 1) & 127
    sel = jnp.where(x == jnp.where(h < 8, h, h + 112), 1.0, 0.0).astype(bf16)
    selc = jnp.where((x >> 1) == jnp.where(h < 8, h, h + 48), 1.0, 0.0).astype(bf16)

    def put(i, rows, s):
        hi, lo = split(rows)
        v = lax.dot_general(
            s, jnp.concatenate([hi, lo], axis=1), (((1,), (1,)), ((), ())),
            preferred_element_type=f32,
        )
        xlo[i] = v[0:8]
        xhi[i] = v[8:16]

    @pl.loop(0, 32)
    def _(z):
        put(z, d[z], sel)

    put(32, yl[0:32].reshape(256, 128), sel)
    put(33, yh[0:32].reshape(256, 128), sel)

    @pl.loop(0, 8)
    def _(b):
        put(34 + b, g[pl.ds(2 * b, 2)].reshape(256, 128), selc)

    put(
        42,
        jnp.concatenate([yl[32:48].reshape(128, 128), yh[32:48].reshape(128, 128)], axis=0),
        selc,
    )
    mine = xlo.at[43]
    own = jnp.concatenate([yl[48], yh[48]], axis=1)
    rest = jnp.concatenate([q2[0], q2[1]], axis=1)
    mine[...] = own
    xlo[44] = rest
    xhi[43] = own
    xhi[44] = rest


def zstrip_kernel(g, yl, yh, xl, xr, qt, zlo, zhi):
    packed = jnp.concatenate([qt[i][:, 0:4] for i in range(32)], axis=1)
    for out, p0, far in ((zlo, 0, 4), (zhi, 24, 8)):
        for p in range(8):
            for s, src in ((0, xl), (1, xr)):
                for half in range(2):
                    out[p * 4 + s * 2 + half] = src[p0 + p, :, half * 128 : half * 128 + 128]
        out[32:40] = yl[p0 : p0 + 8]
        out[40:48] = yh[p0 : p0 + 8]
        for s, src in ((0, xl), (1, xr)):
            a, b = src[32], src[33]
            out[48 + s] = jnp.concatenate([a[:, p0 * 8 : p0 * 8 + 64], b[:, p0 * 8 : p0 * 8 + 64]], axis=1)
        for i in range(4):
            out[50 + 16 * i : 66 + 16 * i] = g[far + i].reshape(16, 8, 128)
        c0 = 0 if p0 == 0 else 8
        out[114:122] = yl[32 + c0 : 40 + c0]
        out[122:130] = yh[32 + c0 : 40 + c0]
        for b in range(4):
            for s, src in ((0, xl), (1, xr)):
                for half in range(2):
                    out[130 + b * 4 + s * 2 + half] = src[34 + c0 // 2 + b, :, half * 128 : half * 128 + 128]
        for s, src in ((0, xl), (1, xr)):
            a = src[42]
            out[146 + s] = jnp.concatenate(
                [a[:, c0 * 8 : c0 * 8 + 64], a[:, 128 + c0 * 8 : 128 + c0 * 8 + 64]], axis=1
            )
        out[148] = packed


def own_kernel(ft, ct, d, g, yl, yh, xl, xr, e, ec):
    w = x_weights(ft, False)

    def strip(i):
        return jnp.concatenate([xl[i], xr[i]], axis=0)

    @pl.loop(0, 32)
    def _(z):
        r = x_block(d[z], strip(z), *w)
        for t in range(2):
            e[t, z, 8:264, :] = r[:, t * 128 : t * 128 + 128]

    for i, src, row in ((32, yl, 0), (33, yh, 264)):
        r = x_block(src[0:32].reshape(256, 128), strip(i), *w).reshape(32, 8, 256)
        for t in range(2):
            e[t, :, row : row + 8, :] = r[:, :, t * 128 : t * 128 + 128]

    wc = x_weights(ct, True)

    @pl.loop(0, 8)
    def _(b):
        r = x_block(g[pl.ds(2 * b, 2)].reshape(256, 128), strip(34 + b), *wc).reshape(2, 128, 256)
        for t in range(2):
            ec[t, pl.ds(2 * b, 2), 8:136, :] = r[:, :, t * 128 : t * 128 + 128]

    r = x_block(
        jnp.concatenate([yl[32:48].reshape(128, 128), yh[32:48].reshape(128, 128)], axis=0),
        strip(42), *wc,
    ).reshape(2, 16, 8, 256)
    for t in range(2):
        ec[t, :, 0:8, :] = r[0, :, :, t * 128 : t * 128 + 128]
        ec[t, :, 136:144, :] = r[1, :, :, t * 128 : t * 128 + 128]


def z_group(planes, taps, base, count):
    w = [jnp.full((8, 128), taps[base + k], f32) for k in range(TAPS)]
    w = [jnp.concatenate([v, v], axis=0) for v in w]
    acc = [None] * count
    for i in range(count + 2 * R):
        v = planes(i)
        for o in range(count):
            k = i - o
            if 0 <= k < TAPS:
                acc[o] = w[k] * v if acc[o] is None else acc[o] + w[k] * v
    return acc


def final_kernel(ft, ct, e, ec, zl, zh, sl, sh, tp, out, eh, ech, gn, fh, fl, fch, fcl):
    w = x_weights(ft, False)

    def strip(ref, i):
        return jnp.concatenate(
            [
                jnp.concatenate([ref[i], ref[i + 1]], axis=1),
                jnp.concatenate([ref[i + 2], ref[i + 3]], axis=1),
            ],
            axis=0,
        )

    for n, (m, s) in enumerate(((zl, sl), (zh, sh))):

        @pl.loop(0, 8)
        def _(p, n=n, m=m, s=s):
            r = x_block(m[p], strip(s, 4 * p), *w)
            for t in range(2):
                eh[t, 8 * n + p, 8:264, :] = r[:, t * 128 : t * 128 + 128]

        @pl.loop(0, 4)
        def _(p, n=n, m=m):
            gn[4 * n + p] = pool(m, p)

    def sides(lo, hi):
        return jnp.concatenate([lo, hi], axis=0)

    def pair(i):
        return jnp.concatenate(
            [jnp.concatenate([sl[i], sh[i]], axis=1), jnp.concatenate([sl[i + 1], sh[i + 1]], axis=1)],
            axis=0,
        )

    r = x_block(
        sides(sl[32:48].reshape(128, 128), sh[32:48].reshape(128, 128)), pair(48), *w
    ).reshape(2, 2, 8, 8, 256)
    for n in range(2):
        for t in range(2):
            eh[t, 8 * n : 8 * n + 8, 0:8, :] = r[n, 0, :, :, t * 128 : t * 128 + 128]
            eh[t, 8 * n : 8 * n + 8, 264:272, :] = r[n, 1, :, :, t * 128 : t * 128 + 128]

    wc = x_weights(ct, True)
    for n, s in enumerate((sl, sh)):
        for b in range(4):
            near = b >= 2 if n == 0 else b < 2
            if near:
                first = 2 * (b - 2) if n == 0 else 4 + 2 * b
                rows = gn[first : first + 2].reshape(256, 128)
            else:
                first = 50 + 32 * (b if n == 0 else b - 2)
                rows = s[first : first + 32].reshape(256, 128)
            r = x_block(rows, strip(s, 130 + 4 * b), *wc).reshape(2, 128, 256)
            for t in range(2):
                ech[t, 8 * n + 2 * b : 8 * n + 2 * b + 2, 8:136, :] = r[:, :, t * 128 : t * 128 + 128]
    r = x_block(
        sides(sl[114:130].reshape(128, 128), sh[114:130].reshape(128, 128)), pair(146), *wc
    ).reshape(2, 2, 8, 8, 256)
    for n in range(2):
        for t in range(2):
            ech[t, 8 * n : 8 * n + 8, 0:8, :] = r[n, 0, :, :, t * 128 : t * 128 + 128]
            ech[t, 8 * n : 8 * n + 8, 136:144, :] = r[n, 1, :, :, t * 128 : t * 128 + 128]

    @pl.loop(0, 17)
    def _(y):
        rows = pl.ds(pl.multiple_of(y * 16, 16), 16)
        for t in range(2):
            for zb in range(4):

                def plane(i, t=t, zb=zb):
                    i = i + 8 * zb
                    if i < 8:
                        return eh[t, i, rows, :]
                    if i < 40:
                        return e[t, i - 8, rows, :]
                    return eh[t, i - 32, rows, :]

                for o, v in enumerate(z_group(plane, ft, tap_base(t, 2), 8)):
                    z = 8 * zb + o
                    q, l, r = z // 4, z // 2 % 2, z % 2
                    hi, lo = split(v)
                    fh[t, 2 * q + r, rows, l * 128 : l * 128 + 128] = hi
                    fl[t, 2 * q + r, rows, l * 128 : l * 128 + 128] = lo

    @pl.loop(0, 9)
    def _(y):
        rows = pl.ds(pl.multiple_of(y * 16, 16), 16)
        for t in range(2):
            for zb in range(2):

                def plane(i, t=t, zb=zb):
                    i = i + 8 * zb
                    if i < 8:
                        return ech[t, i, rows, :]
                    if i < 24:
                        return ec[t, i - 8, rows, :]
                    return ech[t, i - 16, rows, :]

                for o, v in enumerate(z_group(plane, ct, tap_base(t, 2), 8)):
                    z = 8 * zb + o
                    hi, lo = split(v)
                    fch[t, z // 2, rows, (z % 2) * 128 : (z % 2) * 128 + 128] = hi
                    fcl[t, z // 2, rows, (z % 2) * 128 : (z % 2) * 128 + 128] = lo

    wy, wyc = (
        jnp.concatenate([y_weights(taps, t, coarse) for t in range(2)], axis=1)
        for taps, coarse in ((ft, False), (ct, True))
    )

    def stacked(h, l, index, first, size):
        rows = slice(first, first + size)
        return jnp.concatenate([stack(h[t, index, rows, :], l[t, index, rows, :]) for t in range(2)], axis=0)

    @pl.loop(0, 8)
    def _(q):
        for b in range(4):
            top = jnp.concatenate(
                [jnp.broadcast_to(tp[2 * b + k : 2 * b + k + 1, :], (32, 128)) for k in range(2)], axis=0
            )
            common = mm(wyc, stacked(fch, fcl, q, 32 * b, 48))
            even, odd = common[:, 0:128] + top, common[:, 128:256] + top
            for r in range(2):
                res = mm(wy, stacked(fh, fl, 2 * q + r, 64 * b, 80))
                out[4 * q + r, 64 * b : 64 * b + 64, :] = res[:, 0:128] + even
                out[4 * q + 2 + r, 64 * b : 64 * b + 64, :] = res[:, 128:256] + odd


def sds(*shape):
    return jax.ShapeDtypeStruct(shape, f32)


def call(kernel, outs, n_smem, args, scratch=(), flops=0, nbytes=0):
    return pl.pallas_call(
        kernel,
        out_shape=outs,
        in_specs=[SM] * n_smem + [VM] * (len(args) - n_smem),
        out_specs=jax.tree.map(lambda _: VM, outs),
        scratch_shapes=scratch,
        compiler_params=PARAMS,
        cost_estimate=pl.CostEstimate(flops=flops, bytes_accessed=nbytes, transcendentals=0),
    )(*args)


OFFSETS = {"gx": (0, -1, 1, -4, -3, -2, 2, 3), "gy": (0, -1, 1, 2), "gz": (0, -1, 1, -4, -3, -2, 2, 3)}


def wrapped(d, period):
    d = jnp.abs(d) % period
    return jnp.minimum(d, period - d).astype(f32)


def top_kernel_matrix():
    shape = (8, 4, 8, 8, 8, 4, 4)
    ids = [lax.broadcasted_iota(jnp.int32, shape, i) for i in range(7)]
    return ids


def top_potential(parts):
    lane = jnp.arange(128, dtype=jnp.int32)
    offx = sum(jnp.where(lane // 16 == i, v, 0) for i, v in enumerate(OFFSETS["gx"]))
    offy = sum(jnp.where(lane // 4 % 4 == i, v, 0) for i, v in enumerate(OFFSETS["gy"]))
    zi = jnp.arange(8, dtype=jnp.int32)
    dz = wrapped(sum(jnp.where(zi == i, v, 0) for i, v in enumerate(OFFSETS["gz"])), 8)
    ys = offy[None, :] * 8 + jnp.arange(8, dtype=jnp.int32)[:, None]
    xs = offx * 4 + lane % 4
    own = jnp.arange(32, dtype=jnp.int32)
    dy = wrapped((own // 4)[:, None, None] - ys[None], 32)
    dx = wrapped((own % 4)[:, None, None] - xs[None, None, :], 32)
    r2 = 1.0 + (dz * dz)[None, :, None, None] + (dy * dy + dx * dx)[:, None]
    kernel = 1.0 / (256.0 * jnp.sqrt(r2))
    return jnp.sum(kernel * parts[None], axis=(1, 2, 3)).reshape(8, 4)


def on_device(charges, fine_taps, coarse_taps):
    ft = fine_taps.reshape(-1)
    ct = coarse_taps.reshape(-1)
    zl = shift(charges[24:32], "gz", 1)
    zh = shift(charges[0:8], "gz", -1)

    g, ylo, yhi = call(
        prep_kernel, (sds(16, 128, 128), sds(49, 8, 128), sds(49, 8, 128)), 0, (charges,),
        flops=1 << 22, nbytes=6 << 20,
    )
    q2 = shift(ylo[48], "gy", 2)
    yl = shift(yhi, "gy", 1)
    yh = shift(ylo, "gy", -1)
    q2 = jnp.stack([ylo[48], q2])

    xlo, xhi = call(
        strip_kernel, (sds(NB, 8, 256), sds(NB, 8, 256)), 0, (charges, g, yl, yh, q2),
        flops=1 << 27, nbytes=6 << 20,
    )
    xl = shift(xhi, "gx", 1)
    xr = shift(xlo, "gx", -1)

    def quarters(v):
        v = v[43:45]
        return jnp.stack([v[1, :, 0:128], v[0, :, 0:128], v[0, :, 128:256], v[1, :, 128:256]])

    q3 = jnp.concatenate([quarters(v) for v in (xlo, xl, xr)], axis=0)
    qm = shift(q3, "gx", 3)
    qp = shift(q3, "gx", -3)
    qt = jnp.concatenate([q3, qm[4:8], qm[0:4], qm[8:12], qp[4:8], qp[0:4]], axis=0)

    zlo, zhi = call(
        zstrip_kernel, (sds(NT, 8, 128), sds(NT, 8, 128)), 0, (g, yl, yh, xl, xr, qt),
        flops=1 << 20, nbytes=4 << 20,
    )
    sl = shift(zhi, "gz", 1)
    sh = shift(zlo, "gz", -1)

    e, ec = call(
        own_kernel, (sds(2, 32, 272, 128), sds(2, 16, 144, 128)), 2,
        (ft, ct, charges, g, yl, yh, xl, xr), flops=5 << 30, nbytes=16 << 20,
    )

    p3 = jnp.stack([zlo[148], sl[148], sh[148]])
    pm = shift(p3, "gz", 3)
    pp = shift(p3, "gz", -3)
    parts = jnp.stack([p3[0], p3[1], p3[2], pm[1], pm[0], pm[2], pp[1], pp[0]])
    tp = jnp.repeat(top_potential(parts), 32, axis=1)

    return call(
        final_kernel, sds(32, 256, 128), 2, (ft, ct, e, ec, zl, zh, sl, sh, tp),
        scratch=[
            pltpu.VMEM((2, 16, 272, 128), f32),
            pltpu.VMEM((2, 16, 144, 128), f32),
            pltpu.VMEM((8, 128, 128), f32),
            pltpu.VMEM((2, 16, 272, 256), bf16),
            pltpu.VMEM((2, 16, 272, 256), bf16),
            pltpu.VMEM((2, 8, 144, 256), bf16),
            pltpu.VMEM((2, 8, 144, 256), bf16),
        ],
        flops=8 << 30, nbytes=20 << 20,
    )


def solution(mesh):
    return jax.shard_map(
        on_device,
        mesh=mesh,
        in_specs=(P("gz", "gy", "gx"), P(), P()),
        out_specs=P("gz", "gy", "gx"),
        check_vma=False,
    )
```

profile of v0, /device:TPU:1, one launch (start us, length us, event | category | flops | bytes accessed | tf_op | source)
XLA Modules:
  0.0 130.3 jit_solution(14828660762748802726)
XLA Ops:
  0.0 3.6 %shard_map.37 = (f32[16,128,128]{2,1,0:T(8,128)}, f32[49,8,128]{2,1,0:T(8,128)}, f32[49,8,128]{2,1,0:T(8,128)}) custom-call(f32[32,256,128]{2,1,0:T(8,128)} %d.5), custom_call_target="tpu_custom_call" | custom-call | flops 4194304 | bytes 6291456 | tf_op jit(solution)/shard_map/pallas_call | solution.py:373
  3.6 3.6 %collective-permute-start.1 = (f32[49,8,128]{2,1,0:T(8,128)}, f32[49,8,128]{2,1,0:T(8,128)S(1)}, u32[]{:S(2)}, u32[]{:S(2)}) collective-permute-start(f32[49,8,128]{2,1,0:T(8,128)} %get-tuple-element.16), channel_id=1, source_target_pairs={{0,24},{8,0},{16,8},{24,16},{1,25},{9,1},{17,9},{25,17},{2,26},{10... | collective-permute-start | bytes 602120 | tf_op jit(solution)/shard_map/ppermute | solution.py:26
  7.1 0.7 fusion.41
  8.2 0.7 collective-permute-start
  8.9 1.7 %fusion.37 = (f32[8,256,128]{2,1,0:T(8,128)S(1)}, f32[8,256,128]{2,1,0:T(8,128)S(1)}) fusion(f32[32,256,128]{2,1,0:T(8,128)} %d.5), kind=kLoop, calls=%fused_computation.118 | loop fusion | bytes 4194304 | tf_op jit(solution)/shard_map/slice | solution.py:418
  10.6 5.7 %collective-permute-start.6 = (f32[8,256,128]{2,1,0:T(8,128)S(1)}, f32[8,256,128]{2,1,0:T(8,128)}, u32[]{:S(2)}, u32[]{:S(2)}) collective-permute-start(f32[8,256,128]{2,1,0:T(8,128)S(1)} %get-tuple-element.23), channel_id=1, source_target_pairs={{0,7},{1,0},{2,1},{3,2},{4,3},{5,4},{6,5},{7,6},{8,15},{9,8},{10,9... | collective-permute-start | bytes 3145736 | tf_op jit(solution)/shard_map/ppermute | solution.py:26
  17.7 11.3 %shard_map.38 = (f32[45,8,256]{2,1,0:T(8,128)}, f32[45,8,256]{2,1,0:T(8,128)}) custom-call(f32[32,256,128]{2,1,0:T(8,128)} %d.5, f32[16,128,128]{2,1,0:T(8,128)} %get-tuple-element.14.g, f32[49,8,128]{2,1,0:T(8,128)} %copy-done.1, f32[49,8,128]{2,1,0:T(8,128)} %copy-done, f32[2,8,128]{2,1,0:T(8,128)} %pad_maximum_fusion.1.q2), custom_call_target="tpu_custom_call" | custom-call | flops 134217728 | bytes 6291456 | tf_op jit(solution)/shard_map/pallas_call | solution.py:373
  29.7 1.8 %collective-permute-start.4 = (f32[45,8,256]{2,1,0:T(8,128)}, f32[45,8,256]{2,1,0:T(8,128)S(1)}, u32[]{:S(2)}, u32[]{:S(2)}) collective-permute-start(f32[45,8,256]{2,1,0:T(8,128)} %get-tuple-element.18), channel_id=1, source_target_pairs={{0,224},{32,0},{64,32},{96,64},{128,96},{160,128},{192,160},{224,1... | collective-permute-start | bytes 1105928 | tf_op jit(solution)/shard_map/ppermute | solution.py:26
  31.5 0.7 constant_dynamic-update-slice_fusion.7
  32.3 1.1 collective-permute-start.3
  34.0 0.7 constant_dynamic-update-slice_fusion.6
  34.7 3.4 %collective-permute-done.3.xl = f32[45,8,256]{2,1,0:T(8,128)S(1)} collective-permute-done((f32[45,8,256]{2,1,0:T(8,128)}, f32[45,8,256]{2,1,0:T(8,128)S(1)}, u32[]{:S(2)}, u32[]{:S(2)}) %collective-permute-start.3) | collective-permute-done | bytes 368672 | tf_op jit(solution)/shard_map/ppermute | solution.py:26
  38.5 3.7 %collective-permute-start.7 = (f32[12,8,128]{2,1,0:T(8,128)S(1)}, f32[12,8,128]{2,1,0:T(8,128)S(1)}, u32[]{:S(2)}, u32[]{:S(2)}) collective-permute-start(f32[12,8,128]{2,1,0:T(8,128)S(1)} %get-tuple-element.31), channel_id=1, source_target_pairs={{0,96},{32,128},{64,160},{96,192},{128,224},{160,0},{192,32},{224,... | collective-permute-start | bytes 147464 | tf_op jit(solution)/shard_map/ppermute | solution.py:26
  42.2 1.5 %collective-permute-done.7 = f32[12,8,128]{2,1,0:T(8,128)S(1)} collective-permute-done((f32[12,8,128]{2,1,0:T(8,128)S(1)}, f32[12,8,128]{2,1,0:T(8,128)S(1)}, u32[]{:S(2)}, u32[]{:S(2)}) %collective-permute-start.7) | collective-permute-done | bytes 49184 | tf_op jit(solution)/shard_map/ppermute | solution.py:26
  43.7 3.5 %collective-permute-done.8 = f32[12,8,128]{2,1,0:T(8,128)S(1)} collective-permute-done((f32[12,8,128]{2,1,0:T(8,128)S(1)}, f32[12,8,128]{2,1,0:T(8,128)S(1)}, u32[]{:S(2)}, u32[]{:S(2)}) %collective-permute-start.8) | collective-permute-done | bytes 49184 | tf_op jit(solution)/shard_map/ppermute | solution.py:26
  47.9 2.7 %shard_map.40 = (f32[149,8,128]{2,1,0:T(8,128)}, f32[149,8,128]{2,1,0:T(8,128)}) custom-call(f32[16,128,128]{2,1,0:T(8,128)} %get-tuple-element.14.g, f32[49,8,128]{2,1,0:T(8,128)} %copy-done.1, f32[49,8,128]{2,1,0:T(8,128)} %copy-done, f32[45,8,256]{2,1,0:T(8,128)} %copy-done.3, f32[45,8,256]{2,1,0:T(8,128)} %copy-done.2, f32[32,8,128]{2,1,0:T(8,128)} %copy-done.4), custom_call_target="tpu_custom_call" | custom-call | flops 1048576 | bytes 4194304 | tf_op jit(solution)/shard_map/pallas_call | solution.py:373
  50.7 3.9 %collective-permute-start.10 = (f32[149,8,128]{2,1,0:T(8,128)}, f32[149,8,128]{2,1,0:T(8,128)}, u32[]{:S(2)}, u32[]{:S(2)}) collective-permute-start(f32[149,8,128]{2,1,0:T(8,128)} %get-tuple-element.22), channel_id=1, source_target_pairs={{0,7},{1,0},{2,1},{3,2},{4,3},{5,4},{6,5},{7,6},{8,15},{9,8},{10,9... | collective-permute-start | bytes 1830920 | tf_op jit(solution)/shard_map/ppermute | solution.py:26
  56.7 11.7 %collective-permute-done.9.sl = f32[149,8,128]{2,1,0:T(8,128)S(1)} collective-permute-done((f32[149,8,128]{2,1,0:T(8,128)}, f32[149,8,128]{2,1,0:T(8,128)S(1)}, u32[]{:S(2)}, u32[]{:S(2)}) %collective-permute-start.9) | collective-permute-done | bytes 610336 | tf_op jit(solution)/shard_map/ppermute | solution.py:26
  68.4 0.7 fusion.40
  69.1 4.9 %collective-permute-start.11 = (f32[3,8,128]{2,1,0:T(8,128)S(1)}, f32[3,8,128]{2,1,0:T(8,128)S(1)}, u32[]{:S(2)}, u32[]{:S(2)}) collective-permute-start(f32[3,8,128]{2,1,0:T(8,128)S(1)} %pad_maximum_fusion), channel_id=1, source_target_pairs={{0,3},{1,4},{2,5},{3,6},{4,7},{5,0},{6,1},{7,2},{8,11},{9,12},{10,... | collective-permute-start | bytes 36872 | tf_op jit(solution)/shard_map/ppermute | solution.py:26
  73.9 18.0 %shard_map.39 = (f32[2,32,272,128]{3,2,1,0:T(8,128)}, f32[2,16,144,128]{3,2,1,0:T(8,128)}) custom-call(f32[102]{0:T(128)} %reshape.253.ft, f32[102]{0:T(128)} %reshape.254.ct, f32[32,256,128]{2,1,0:T(8,128)} %d.5, f32[16,128,128]{2,1,0:T(8,128)} %get-tuple-element.14.g, f32[49,8,128]{2,1,0:T(8,128)} %copy-done.1, f32[49,8,128]{2,1,0:T(8,128)} %copy-done, ...), custom_call_target="tpu_custom_call" | custom-call | flops 5368709120 | bytes 16777216 | tf_op jit(solution)/shard_map/pallas_call | solution.py:373
  92.0 4.4 %collective-permute-done.12 = f32[3,8,128]{2,1,0:T(8,128)S(1)} collective-permute-done((f32[3,8,128]{2,1,0:T(8,128)S(1)}, f32[3,8,128]{2,1,0:T(8,128)S(1)}, u32[]{:S(2)}, u32[]{:S(2)}) %collective-permute-start.12) | collective-permute-done | bytes 12320 | tf_op jit(solution)/shard_map/ppermute | solution.py:26
  96.3 0.7 multiply_reduce_fusion
  97.9 32.4 %shard_map.41 = f32[32,256,128]{2,1,0:T(8,128)} custom-call(f32[102]{0:T(128)} %reshape.253.ft, f32[102]{0:T(128)} %reshape.254.ct, f32[2,32,272,128]{3,2,1,0:T(8,128)} %get-tuple-element.19.e, f32[2,16,144,128]{3,2,1,0:T(8,128)} %get-tuple-element.20.ec, f32[8,256,128]{2,1,0:T(8,128)} %collective-permute-done.5.zl, ...), custom_call_target="tpu_custom_call" | custom-call | flops 8589934592 | bytes 20971520 | tf_op jit(solution)/shard_map/pallas_call | solution.py:373
  (68 shorter events, 7.1 us)
Async XLA Ops:
  3.6 13.4 %collective-permute-start.1 = (f32[49,8,128]{2,1,0:T(8,128)}, f32[49,8,128]{2,1,0:T(8,128)S(1)}, u32[]{:S(2)}, u32[]{:S(2)}) collective-permute-start(f32[49,8,128]{2,1,0:T(8,128)} %get-tuple-element.16), channel_id=1, source_target_pairs={{0,24},{8,0},{16,8},{24,16},{1,25},{9,1},{17,9},{25,17},{2,26},{10... | collective-permute-start | bytes 602120 | tf_op jit(solution)/shard_map/ppermute | solution.py:26
  7.8 8.5 %collective-permute-start.2 = (f32[8,128]{1,0:T(8,128)S(1)}, f32[8,128]{1,0:T(8,128)S(1)}, u32[]{:S(2)}, u32[]{:S(2)}) collective-permute-start(f32[8,128]{1,0:T(8,128)S(1)} %get-tuple-element.44), channel_id=1, source_target_pairs={{0,16},{8,24},{16,0},{24,8},{1,17},{9,25},{17,1},{25,9},{2,18},{10... | collective-permute-start | bytes 12296 | tf_op jit(solution)/shard_map/ppermute | solution.py:26
  8.2 8.8 %collective-permute-start = (f32[49,8,128]{2,1,0:T(8,128)}, f32[49,8,128]{2,1,0:T(8,128)S(1)}, u32[]{:S(2)}, u32[]{:S(2)}) collective-permute-start(f32[49,8,128]{2,1,0:T(8,128)} %get-tuple-element.15), channel_id=1, source_target_pairs={{0,8},{8,16},{16,24},{24,0},{1,9},{9,17},{17,25},{25,1},{2,10},{10... | collective-permute-start | bytes 602120 | tf_op jit(solution)/shard_map/ppermute | solution.py:26
  10.6 87.3 %collective-permute-start.6 = (f32[8,256,128]{2,1,0:T(8,128)S(1)}, f32[8,256,128]{2,1,0:T(8,128)}, u32[]{:S(2)}, u32[]{:S(2)}) collective-permute-start(f32[8,256,128]{2,1,0:T(8,128)S(1)} %get-tuple-element.23), channel_id=1, source_target_pairs={{0,7},{1,0},{2,1},{3,2},{4,3},{5,4},{6,5},{7,6},{8,15},{9,8},{10,9... | collective-permute-start | bytes 3145736 | tf_op jit(solution)/shard_map/ppermute | solution.py:26
  16.2 81.7 %collective-permute-start.5 = (f32[8,256,128]{2,1,0:T(8,128)S(1)}, f32[8,256,128]{2,1,0:T(8,128)}, u32[]{:S(2)}, u32[]{:S(2)}) collective-permute-start(f32[8,256,128]{2,1,0:T(8,128)S(1)} %get-tuple-element.24), channel_id=1, source_target_pairs={{0,1},{1,2},{2,3},{3,4},{4,5},{5,6},{6,7},{7,0},{8,9},{9,10},{10,1... | collective-permute-start | bytes 3145736 | tf_op jit(solution)/shard_map/ppermute | solution.py:26
  17.0 0.7 copy-start.1
  17.0 0.7 copy-start
  17.7 37.0 %copy-start.5 = (f32[2,3,17]{2,0,1:T(2,128)S(1)}, f32[2,3,17]{2,0,1:T(2,128)}, u32[]{:S(2)}) copy-start(f32[2,3,17]{2,0,1:T(2,128)} %param.4) | copy-start | bytes 1228
  17.7 37.7 %copy-start.6 = (f32[2,3,17]{2,0,1:T(2,128)S(1)}, f32[2,3,17]{2,0,1:T(2,128)}, u32[]{:S(2)}) copy-start(f32[2,3,17]{2,0,1:T(2,128)} %param.5) | copy-start | bytes 1228
  29.7 8.7 %collective-permute-start.4 = (f32[45,8,256]{2,1,0:T(8,128)}, f32[45,8,256]{2,1,0:T(8,128)S(1)}, u32[]{:S(2)}, u32[]{:S(2)}) collective-permute-start(f32[45,8,256]{2,1,0:T(8,128)} %get-tuple-element.18), channel_id=1, source_target_pairs={{0,224},{32,0},{64,32},{96,64},{128,96},{160,128},{192,160},{224,1... | collective-permute-start | bytes 1105928 | tf_op jit(solution)/shard_map/ppermute | solution.py:26
  32.3 5.9 %collective-permute-start.3 = (f32[45,8,256]{2,1,0:T(8,128)}, f32[45,8,256]{2,1,0:T(8,128)S(1)}, u32[]{:S(2)}, u32[]{:S(2)}) collective-permute-start(f32[45,8,256]{2,1,0:T(8,128)} %get-tuple-element.17), channel_id=1, source_target_pairs={{0,32},{32,64},{64,96},{96,128},{128,160},{160,192},{192,224},{224... | collective-permute-start | bytes 1105928 | tf_op jit(solution)/shard_map/ppermute | solution.py:26
  38.1 9.1 %copy-start.3 = (f32[45,8,256]{2,1,0:T(8,128)}, f32[45,8,256]{2,1,0:T(8,128)S(1)}, u32[]{:S(2)}) copy-start(f32[45,8,256]{2,1,0:T(8,128)S(1)} %collective-permute-done.3.xl) | copy-start | bytes 1105924
  38.4 8.8 %copy-start.2 = (f32[45,8,256]{2,1,0:T(8,128)}, f32[45,8,256]{2,1,0:T(8,128)S(1)}, u32[]{:S(2)}) copy-start(f32[45,8,256]{2,1,0:T(8,128)S(1)} %collective-permute-done.4.xr) | copy-start | bytes 1105924
  38.5 5.2 %collective-permute-start.7 = (f32[12,8,128]{2,1,0:T(8,128)S(1)}, f32[12,8,128]{2,1,0:T(8,128)S(1)}, u32[]{:S(2)}, u32[]{:S(2)}) collective-permute-start(f32[12,8,128]{2,1,0:T(8,128)S(1)} %get-tuple-element.31), channel_id=1, source_target_pairs={{0,96},{32,128},{64,160},{96,192},{128,224},{160,0},{192,32},{224,... | collective-permute-start | bytes 147464 | tf_op jit(solution)/shard_map/ppermute | solution.py:26
  42.2 5.0 %collective-permute-start.8 = (f32[12,8,128]{2,1,0:T(8,128)S(1)}, f32[12,8,128]{2,1,0:T(8,128)S(1)}, u32[]{:S(2)}, u32[]{:S(2)}) collective-permute-start(f32[12,8,128]{2,1,0:T(8,128)S(1)} %get-tuple-element.31), channel_id=1, source_target_pairs={{0,160},{32,192},{64,224},{96,0},{128,32},{160,64},{192,96},{224,1... | collective-permute-start | bytes 147464 | tf_op jit(solution)/shard_map/ppermute | solution.py:26
  47.2 0.6 copy-start.4
  50.6 17.7 %collective-permute-start.9 = (f32[149,8,128]{2,1,0:T(8,128)}, f32[149,8,128]{2,1,0:T(8,128)S(1)}, u32[]{:S(2)}, u32[]{:S(2)}) collective-permute-start(f32[149,8,128]{2,1,0:T(8,128)} %get-tuple-element.21), channel_id=1, source_target_pairs={{0,1},{1,2},{2,3},{3,4},{4,5},{5,6},{6,7},{7,0},{8,9},{9,10},{10,1... | collective-permute-start | bytes 1830920 | tf_op jit(solution)/shard_map/ppermute | solution.py:26
  50.7 17.7 %collective-permute-start.10 = (f32[149,8,128]{2,1,0:T(8,128)}, f32[149,8,128]{2,1,0:T(8,128)}, u32[]{:S(2)}, u32[]{:S(2)}) collective-permute-start(f32[149,8,128]{2,1,0:T(8,128)} %get-tuple-element.22), channel_id=1, source_target_pairs={{0,7},{1,0},{2,1},{3,2},{4,3},{5,4},{6,5},{7,6},{8,15},{9,8},{10,9... | collective-permute-start | bytes 1830920 | tf_op jit(solution)/shard_map/ppermute | solution.py:26
  68.4 23.6 %copy-start.7 = (f32[149,8,128]{2,1,0:T(8,128)}, f32[149,8,128]{2,1,0:T(8,128)S(1)}, u32[]{:S(2)}) copy-start(f32[149,8,128]{2,1,0:T(8,128)S(1)} %collective-permute-done.9.sl) | copy-start | bytes 1830916
  69.1 22.8 %collective-permute-start.11 = (f32[3,8,128]{2,1,0:T(8,128)S(1)}, f32[3,8,128]{2,1,0:T(8,128)S(1)}, u32[]{:S(2)}, u32[]{:S(2)}) collective-permute-start(f32[3,8,128]{2,1,0:T(8,128)S(1)} %pad_maximum_fusion), channel_id=1, source_target_pairs={{0,3},{1,4},{2,5},{3,6},{4,7},{5,0},{6,1},{7,2},{8,11},{9,12},{10,... | collective-permute-start | bytes 36872 | tf_op jit(solution)/shard_map/ppermute | solution.py:26
  91.9 4.4 %collective-permute-start.12 = (f32[3,8,128]{2,1,0:T(8,128)S(1)}, f32[3,8,128]{2,1,0:T(8,128)S(1)}, u32[]{:S(2)}, u32[]{:S(2)}) collective-permute-start(f32[3,8,128]{2,1,0:T(8,128)S(1)} %pad_maximum_fusion), channel_id=1, source_target_pairs={{0,5},{1,6},{2,7},{3,0},{4,1},{5,2},{6,3},{7,4},{8,13},{9,14},{10,... | collective-permute-start | bytes 36872 | tf_op jit(solution)/shard_map/ppermute | solution.py:26
where the time goes:
time: 131 us; the launch traced here: 130 us
  Pallas kernels  68 us (52%)
  starting transfers between devices  25.7 us (20%)
  waiting for transfers between devices  24.8 us (19%)
  local copies, waits for them, and re-layouts  10 us (8%)
  other arithmetic  1.63 us (1%)
    pallas_call x5, Pallas kernels, call(): pl.pallas_call(kernel, out_shape=outs, in_specs=[SM] * n_smem + [VM] * (l...  68 us
    ppermute x13, starting transfers between devices, shift(): lax.ppermute(value, axis, [(i, (i + step) % count) for i in range(count)])  25.7 us
    ppermute x13, waiting for transfers between devices, shift(): lax.ppermute(value, axis, [(i, (i + step) % count) for i in range(count)])  24.8 us
    unnamed x37, local copies, waits for them, and re-layouts  4.19 us
  transfers between devices with their start and end apart: 13, of which 6 were waited for; matrix products, arithmetic and copies ran while one was open for 8% of the time, Pallas kernels for 25%

commit v1 on v0

--- a/solution.py
+++ b/solution.py
@@ -1,6 +1,3 @@
-import functools
-import itertools
-
 import jax
 import jax.numpy as jnp
 from jax import lax
@@ -8,11 +5,11 @@
 from jax.experimental.pallas import tpu as pltpu
 from jax.sharding import PartitionSpec as P
 
+
 f32 = jnp.float32
 bf16 = jnp.bfloat16
-AXES = ("gx", "gy", "gz")
 NB = 45
-NT = 149
+NT = 148
 R = 8
 TAPS = 17
 
@@ -65,11 +62,7 @@
     hi, lo = split(halves(128, iota((128, 128), 0) >> sh))
     h = iota((16, 128), 0)
     hhi, hlo = split(halves(16, jnp.where(h < 8, h - 8, h - 8 + edge)))
-    return (
-        jnp.concatenate([hi, hi], axis=0),
-        lo,
-        jnp.concatenate([hhi, hhi, hlo], axis=0),
-    )
+    return jnp.concatenate([hi, hi, lo, hhi, hhi, hlo, jnp.zeros((80, 256), bf16)], axis=0)
 
 
 def y_weights(taps, t, coarse):
@@ -87,15 +80,11 @@
     return jnp.concatenate([hi, lo, hi, pad], axis=0)
 
 
-def x_block(a, xt, w1, w2, wh):
+def x_block(a, xt, w):
     hi, lo = split(a)
     xhi, xlo = split(xt)
-    x3 = jnp.concatenate([xhi, xlo, xhi], axis=0)
-    return (
-        mm(jnp.concatenate([hi, lo], axis=1), w1)
-        + mm(hi, w2)
-        + lax.dot_general(x3, wh, (((0,), (0,)), ((), ())), preferred_element_type=f32)
-    )
+    x3 = jnp.concatenate([xhi, xlo, xhi, jnp.zeros((80, 256), bf16)], axis=0)
+    return mm(jnp.concatenate([hi, lo, hi, x3.T], axis=1), w)
 
 
 def pool(ref, z):
@@ -124,47 +113,55 @@
 
 
 def strip_kernel(d, g, yl, yh, q2, xlo, xhi):
-    h = iota((16, 256), 0)
-    x = iota((16, 256), 1) & 127
-    sel = jnp.where(x == jnp.where(h < 8, h, h + 112), 1.0, 0.0).astype(bf16)
-    selc = jnp.where((x >> 1) == jnp.where(h < 8, h, h + 48), 1.0, 0.0).astype(bf16)
-
-    def put(i, rows, s):
-        hi, lo = split(rows)
-        v = lax.dot_general(
-            s, jnp.concatenate([hi, lo], axis=1), (((1,), (1,)), ((), ())),
-            preferred_element_type=f32,
-        )
-        xlo[i] = v[0:8]
-        xhi[i] = v[8:16]
-
-    @pl.loop(0, 32)
-    def _(z):
-        put(z, d[z], sel)
-
-    put(32, yl[0:32].reshape(256, 128), sel)
-    put(33, yh[0:32].reshape(256, 128), sel)
-
-    @pl.loop(0, 8)
-    def _(b):
-        put(34 + b, g[pl.ds(2 * b, 2)].reshape(256, 128), selc)
-
-    put(
+    lane = iota((256, 128), 1)
+
+    def put(first, sources):
+        tile = None
+        for p, v in enumerate(sources):
+            v = pltpu.roll(v, (16 * p + 8) % 128, 1)
+            tile = v if tile is None else jnp.where(lane >= 16 * p, v, tile)
+        tile = tile.T
+        for p in range(len(sources)):
+            xhi[first + p] = tile[16 * p : 16 * p + 8]
+            xlo[first + p] = tile[16 * p + 8 : 16 * p + 16]
+
+    for k in range(4):
+        put(8 * k, [d[8 * k + p] for p in range(8)])
+    put(32, [yl[0:32].reshape(256, 128), yh[0:32].reshape(256, 128)])
+
+    def putc(first, sources):
+        tile = None
+        for p, v in enumerate(sources):
+            v = v + pltpu.roll(v, 127, 1)
+            v = pltpu.roll(v, (32 * p + 16) % 128, 1)
+            tile = v if tile is None else jnp.where(lane >= 32 * p, v, tile)
+        tile = tile.T
+        for p in range(len(sources)):
+            rows = [tile[32 * p + 2 * i : 32 * p + 2 * i + 1] for i in range(16)]
+            xhi[first + p] = jnp.concatenate(rows[0:8], axis=0)
+            xlo[first + p] = jnp.concatenate(rows[8:16], axis=0)
+
+    for k in range(2):
+        putc(34 + 4 * k, [g[8 * k + 2 * p : 8 * k + 2 * p + 2].reshape(256, 128) for p in range(4)])
+    putc(
         42,
-        jnp.concatenate([yl[32:48].reshape(128, 128), yh[32:48].reshape(128, 128)], axis=0),
-        selc,
-    )
-    mine = xlo.at[43]
+        [jnp.concatenate([yl[32:48].reshape(128, 128), yh[32:48].reshape(128, 128)], axis=0)],
+    )
     own = jnp.concatenate([yl[48], yh[48]], axis=1)
     rest = jnp.concatenate([q2[0], q2[1]], axis=1)
-    mine[...] = own
+    xlo[43] = own
     xlo[44] = rest
     xhi[43] = own
     xhi[44] = rest
 
 
-def zstrip_kernel(g, yl, yh, xl, xr, qt, zlo, zhi):
-    packed = jnp.concatenate([qt[i][:, 0:4] for i in range(32)], axis=1)
+def zstrip_kernel(g, yl, yh, xl, xr, own, zlo, zhi, q3):
+    for i, src in enumerate((own, xl, xr)):
+        a, b = src[43], src[44]
+        q3[4 * i] = b[:, 0:128]
+        q3[4 * i + 1] = a[:, 0:128]
+        q3[4 * i + 2] = a[:, 128:256]
+        q3[4 * i + 3] = b[:, 128:256]
     for out, p0, far in ((zlo, 0, 4), (zhi, 24, 8)):
         for p in range(8):
             for s, src in ((0, xl), (1, xr)):
@@ -189,37 +186,48 @@
             out[146 + s] = jnp.concatenate(
                 [a[:, c0 * 8 : c0 * 8 + 64], a[:, 128 + c0 * 8 : 128 + c0 * 8 + 64]], axis=1
             )
-        out[148] = packed
-
-
-def own_kernel(ft, ct, d, g, yl, yh, xl, xr, e, ec):
+
+
+def pack_kernel(q3, qm, qp, packed):
+    tiles = [q3[i] for i in range(12)]
+    tiles += [qm[i] for i in (4, 5, 6, 7, 0, 1, 2, 3, 8, 9, 10, 11)]
+    tiles += [qp[i] for i in (4, 5, 6, 7, 0, 1, 2, 3)]
+    packed[...] = jnp.concatenate([v[:, 0:4] for v in tiles], axis=1)
+
+
+def own_fine_kernel(ft, d, yl, yh, xl, xr, e):
     w = x_weights(ft, False)
 
     def strip(i):
         return jnp.concatenate([xl[i], xr[i]], axis=0)
 
-    @pl.loop(0, 32)
+    @pl.loop(0, 32, unroll=4)
     def _(z):
-        r = x_block(d[z], strip(z), *w)
+        r = x_block(d[z], strip(z), w)
         for t in range(2):
             e[t, z, 8:264, :] = r[:, t * 128 : t * 128 + 128]
 
     for i, src, row in ((32, yl, 0), (33, yh, 264)):
-        r = x_block(src[0:32].reshape(256, 128), strip(i), *w).reshape(32, 8, 256)
+        r = x_block(src[0:32].reshape(256, 128), strip(i), w).reshape(32, 8, 256)
         for t in range(2):
             e[t, :, row : row + 8, :] = r[:, :, t * 128 : t * 128 + 128]
 
+
+def own_coarse_kernel(ct, g, yl, yh, xl, xr, ec):
+    def strip(i):
+        return jnp.concatenate([xl[i], xr[i]], axis=0)
+
     wc = x_weights(ct, True)
 
-    @pl.loop(0, 8)
+    @pl.loop(0, 8, unroll=4)
     def _(b):
-        r = x_block(g[pl.ds(2 * b, 2)].reshape(256, 128), strip(34 + b), *wc).reshape(2, 128, 256)
+        r = x_block(g[pl.ds(2 * b, 2)].reshape(256, 128), strip(34 + b), wc).reshape(2, 128, 256)
         for t in range(2):
             ec[t, pl.ds(2 * b, 2), 8:136, :] = r[:, :, t * 128 : t * 128 + 128]
 
     r = x_block(
         jnp.concatenate([yl[32:48].reshape(128, 128), yh[32:48].reshape(128, 128)], axis=0),
-        strip(42), *wc,
+        strip(42), wc,
     ).reshape(2, 16, 8, 256)
     for t in range(2):
         ec[t, :, 0:8, :] = r[0, :, :, t * 128 : t * 128 + 128]
@@ -239,7 +247,7 @@
     return acc
 
 
-def final_kernel(ft, ct, e, ec, zl, zh, sl, sh, tp, out, eh, ech, gn, fh, fl, fch, fcl):
+def final_kernel(ft, ct, e, ec, zl, zh, sl, sh, out, eh, ech, gn, fh, fl, fch, fcl):
     w = x_weights(ft, False)
 
     def strip(ref, i):
@@ -253,9 +261,9 @@
 
     for n, (m, s) in enumerate(((zl, sl), (zh, sh))):
 
-        @pl.loop(0, 8)
+        @pl.loop(0, 8, unroll=4)
         def _(p, n=n, m=m, s=s):
-            r = x_block(m[p], strip(s, 4 * p), *w)
+            r = x_block(m[p], strip(s, 4 * p), w)
             for t in range(2):
                 eh[t, 8 * n + p, 8:264, :] = r[:, t * 128 : t * 128 + 128]
 
@@ -273,7 +281,7 @@
         )
 
     r = x_block(
-        sides(sl[32:48].reshape(128, 128), sh[32:48].reshape(128, 128)), pair(48), *w
+        sides(sl[32:48].reshape(128, 128), sh[32:48].reshape(128, 128)), pair(48), w
     ).reshape(2, 2, 8, 8, 256)
     for n in range(2):
         for t in range(2):
@@ -290,11 +298,11 @@
             else:
                 first = 50 + 32 * (b if n == 0 else b - 2)
                 rows = s[first : first + 32].reshape(256, 128)
-            r = x_block(rows, strip(s, 130 + 4 * b), *wc).reshape(2, 128, 256)
+            r = x_block(rows, strip(s, 130 + 4 * b), wc).reshape(2, 128, 256)
             for t in range(2):
                 ech[t, 8 * n + 2 * b : 8 * n + 2 * b + 2, 8:136, :] = r[:, :, t * 128 : t * 128 + 128]
     r = x_block(
-        sides(sl[114:130].reshape(128, 128), sh[114:130].reshape(128, 128)), pair(146), *wc
+        sides(sl[114:130].reshape(128, 128), sh[114:130].reshape(128, 128)), pair(146), wc
     ).reshape(2, 2, 8, 8, 256)
     for n in range(2):
         for t in range(2):
@@ -354,11 +362,8 @@
     @pl.loop(0, 8)
     def _(q):
         for b in range(4):
-            top = jnp.concatenate(
-                [jnp.broadcast_to(tp[2 * b + k : 2 * b + k + 1, :], (32, 128)) for k in range(2)], axis=0
-            )
             common = mm(wyc, stacked(fch, fcl, q, 32 * b, 48))
-            even, odd = common[:, 0:128] + top, common[:, 128:256] + top
+            even, odd = common[:, 0:128], common[:, 128:256]
             for r in range(2):
                 res = mm(wy, stacked(fh, fl, 2 * q + r, 64 * b, 80))
                 out[4 * q + r, 64 * b : 64 * b + 64, :] = res[:, 0:128] + even
@@ -387,12 +392,6 @@
 def wrapped(d, period):
     d = jnp.abs(d) % period
     return jnp.minimum(d, period - d).astype(f32)
-
-
-def top_kernel_matrix():
-    shape = (8, 4, 8, 8, 8, 4, 4)
-    ids = [lax.broadcasted_iota(jnp.int32, shape, i) for i in range(7)]
-    return ids
 
 
 def top_potential(parts):
@@ -411,7 +410,7 @@
     return jnp.sum(kernel * parts[None], axis=(1, 2, 3)).reshape(8, 4)
 
 
-def on_device(charges, fine_taps, coarse_taps):
+def body(charges, fine_taps, coarse_taps):
     ft = fine_taps.reshape(-1)
     ct = coarse_taps.reshape(-1)
     zl = shift(charges[24:32], "gz", 1)
@@ -433,35 +432,35 @@
     xl = shift(xhi, "gx", 1)
     xr = shift(xlo, "gx", -1)
 
-    def quarters(v):
-        v = v[43:45]
-        return jnp.stack([v[1, :, 0:128], v[0, :, 0:128], v[0, :, 128:256], v[1, :, 128:256]])
-
-    q3 = jnp.concatenate([quarters(v) for v in (xlo, xl, xr)], axis=0)
+    zlo, zhi, q3 = call(
+        zstrip_kernel, (sds(NT, 8, 128), sds(NT, 8, 128), sds(12, 8, 128)), 0,
+        (g, yl, yh, xl, xr, xlo), flops=1 << 20, nbytes=4 << 20,
+    )
+    sl = shift(zhi, "gz", 1)
+    sh = shift(zlo, "gz", -1)
     qm = shift(q3, "gx", 3)
     qp = shift(q3, "gx", -3)
-    qt = jnp.concatenate([q3, qm[4:8], qm[0:4], qm[8:12], qp[4:8], qp[0:4]], axis=0)
-
-    zlo, zhi = call(
-        zstrip_kernel, (sds(NT, 8, 128), sds(NT, 8, 128)), 0, (g, yl, yh, xl, xr, qt),
-        flops=1 << 20, nbytes=4 << 20,
-    )
-    sl = shift(zhi, "gz", 1)
-    sh = shift(zlo, "gz", -1)
-
-    e, ec = call(
-        own_kernel, (sds(2, 32, 272, 128), sds(2, 16, 144, 128)), 2,
-        (ft, ct, charges, g, yl, yh, xl, xr), flops=5 << 30, nbytes=16 << 20,
-    )
-
-    p3 = jnp.stack([zlo[148], sl[148], sh[148]])
+
+    e = call(
+        own_fine_kernel, sds(2, 32, 272, 128), 1,
+        (ft, charges, yl, yh, xl, xr), flops=5 << 30, nbytes=16 << 20,
+    )
+
+    qm, qp, e = lax.optimization_barrier((qm, qp, e))
+    p0 = call(pack_kernel, sds(8, 128), 0, (q3, qm, qp))
+    pl1 = shift(p0, "gz", 1)
+    pr1 = shift(p0, "gz", -1)
+    p0, g = lax.optimization_barrier((p0, g))
+    ec = call(
+        own_coarse_kernel, sds(2, 16, 144, 128), 1,
+        (ct, g, yl, yh, xl, xr), flops=1 << 30, nbytes=4 << 20,
+    )
+    p3, ec = lax.optimization_barrier((jnp.stack([p0, pl1, pr1]), ec))
     pm = shift(p3, "gz", 3)
     pp = shift(p3, "gz", -3)
-    parts = jnp.stack([p3[0], p3[1], p3[2], pm[1], pm[0], pm[2], pp[1], pp[0]])
-    tp = jnp.repeat(top_potential(parts), 32, axis=1)
-
-    return call(
-        final_kernel, sds(32, 256, 128), 2, (ft, ct, e, ec, zl, zh, sl, sh, tp),
+
+    out = call(
+        final_kernel, sds(32, 256, 128), 2, (ft, ct, e, ec, zl, zh, sl, sh),
         scratch=[
             pltpu.VMEM((2, 16, 272, 128), f32),
             pltpu.VMEM((2, 16, 144, 128), f32),
@@ -473,11 +472,15 @@
         ],
         flops=8 << 30, nbytes=20 << 20,
     )
+    pm, pp, out = lax.optimization_barrier((pm, pp, out))
+    parts = jnp.stack([p3[0], p3[1], p3[2], pm[1], pm[0], pm[2], pp[1], pp[0]])
+    tp = jnp.repeat(top_potential(parts), 32, axis=1)
+    return (out.reshape(32, 8, 32, 128) + tp[None, :, None, :]).reshape(32, 256, 128)
 
 
 def solution(mesh):
     return jax.shard_map(
-        on_device,
+        body,
         mesh=mesh,
         in_specs=(P("gz", "gy", "gx"), P(), P()),
         out_specs=P("gz", "gy", "gx"),

time: 131 us -> 109 us (0.83)
  the two profiles are of different devices: /device:TPU:1 before, /device:TPU:32 now
where the time goes in v1:
time: 109 us
  Pallas kernels  58 us (53%)
  starting transfers between devices  23.3 us (21%)
  waiting for transfers between devices  15 us (14%)
  other arithmetic  6.28 us (6%)
  local copies, waits for them, and re-layouts  6.02 us (6%)
    pallas_call x7, Pallas kernels, call(): pl.pallas_call(kernel, out_shape=outs, in_specs=[SM] * n_smem + [VM] * (l...  58 us
    ppermute x15, starting transfers between devices, shift(): lax.ppermute(value, axis, [(i, (i + step) % count) for i in range(count)])  23.3 us
    ppermute x15, waiting for transfers between devices, shift(): lax.ppermute(value, axis, [(i, (i + step) % count) for i in range(count)])  15 us
    add x1, other arithmetic, body(): out.reshape(32, 8, 32, 128) + tp[None, :, None, :]  4.65 us
  transfers between devices with their start and end apart: 15, of which 4 were waited for; matrix products, arithmetic and copies ran while one was open for 4% of the time, Pallas kernels for 50%

profile of v1, /device:TPU:32, one launch (start us, length us, event | category | flops | bytes accessed | tf_op | source)
XLA Modules:
  0.0 108.8 jit_solution(1309480908121898851)
XLA Ops:
  0.0 3.6 %shard_map.37 = (f32[16,128,128]{2,1,0:T(8,128)}, f32[49,8,128]{2,1,0:T(8,128)}, f32[49,8,128]{2,1,0:T(8,128)}) custom-call(f32[32,256,128]{2,1,0:T(8,128)} %d.5), custom_call_target="tpu_custom_call" | custom-call | flops 4194304 | bytes 6291456 | tf_op jit(solution)/shard_map/pallas_call | solution.py:378
  3.6 3.0 %collective-permute-start.1 = (f32[49,8,128]{2,1,0:T(8,128)}, f32[49,8,128]{2,1,0:T(8,128)S(1)}, u32[]{:S(2)}, u32[]{:S(2)}) collective-permute-start(f32[49,8,128]{2,1,0:T(8,128)} %get-tuple-element.25), channel_id=1, source_target_pairs={{0,24},{8,0},{16,8},{24,16},{1,25},{9,1},{17,9},{25,17},{2,26},{10... | collective-permute-start | bytes 602120 | tf_op jit(solution)/shard_map/ppermute | solution.py:23
  7.9 1.0 collective-permute-start
  8.9 1.7 %fusion.37 = (f32[8,256,128]{2,1,0:T(8,128)S(1)}, f32[8,256,128]{2,1,0:T(8,128)S(1)}) fusion(f32[32,256,128]{2,1,0:T(8,128)} %d.5), kind=kLoop, calls=%fused_computation.94 | loop fusion | bytes 4194304 | tf_op jit(solution)/shard_map/slice | solution.py:417
  10.6 2.0 %collective-permute-start.11 = (f32[8,256,128]{2,1,0:T(8,128)S(1)}, f32[8,256,128]{2,1,0:T(8,128)S(1)}, u32[]{:S(2)}, u32[]{:S(2)}) collective-permute-start(f32[8,256,128]{2,1,0:T(8,128)S(1)} %get-tuple-element.42), channel_id=1, source_target_pairs={{0,1},{1,2},{2,3},{3,4},{4,5},{5,6},{6,7},{7,0},{8,9},{9,10},{10,1... | collective-permute-start | bytes 3145736 | tf_op jit(solution)/shard_map/ppermute | solution.py:23
  13.4 2.2 %collective-permute-done.yl = f32[49,8,128]{2,1,0:T(8,128)S(1)} collective-permute-done((f32[49,8,128]{2,1,0:T(8,128)}, f32[49,8,128]{2,1,0:T(8,128)S(1)}, u32[]{:S(2)}, u32[]{:S(2)}) %collective-permute-start) | collective-permute-done | bytes 200736 | tf_op jit(solution)/shard_map/ppermute | solution.py:23
  16.2 5.9 %shard_map.38 = (f32[45,8,256]{2,1,0:T(8,128)}, f32[45,8,256]{2,1,0:T(8,128)}) custom-call(f32[32,256,128]{2,1,0:T(8,128)} %d.5, f32[16,128,128]{2,1,0:T(8,128)} %get-tuple-element.32.g, f32[49,8,128]{2,1,0:T(8,128)} %copy-done.1, f32[49,8,128]{2,1,0:T(8,128)} %copy-done, f32[2,8,128]{2,1,0:T(8,128)} %pad_maximum_fusion.1.q2), custom_call_target="tpu_custom_call" | custom-call | flops 134217728 | bytes 6291456 | tf_op jit(solution)/shard_map/pallas_call | solution.py:378
  22.1 0.8 collective-permute-start.4
  23.1 5.2 %collective-permute-done.4.xr = f32[45,8,256]{2,1,0:T(8,128)S(1)} collective-permute-done((f32[45,8,256]{2,1,0:T(8,128)}, f32[45,8,256]{2,1,0:T(8,128)S(1)}, u32[]{:S(2)}, u32[]{:S(2)}) %collective-permute-start.4) | collective-permute-done | bytes 368672 | tf_op jit(solution)/shard_map/ppermute | solution.py:23
  28.3 3.0 %collective-permute-done.3.xl = f32[45,8,256]{2,1,0:T(8,128)S(1)} collective-permute-done((f32[45,8,256]{2,1,0:T(8,128)}, f32[45,8,256]{2,1,0:T(8,128)S(1)}, u32[]{:S(2)}, u32[]{:S(2)}) %collective-permute-start.3) | collective-permute-done | bytes 368672 | tf_op jit(solution)/shard_map/ppermute | solution.py:23
  31.3 0.8 copy-done.3
  32.1 2.8 %shard_map.39 = (f32[148,8,128]{2,1,0:T(8,128)}, f32[148,8,128]{2,1,0:T(8,128)}, f32[12,8,128]{2,1,0:T(8,128)}) custom-call(f32[16,128,128]{2,1,0:T(8,128)} %get-tuple-element.32.g, f32[49,8,128]{2,1,0:T(8,128)} %copy-done.1, f32[49,8,128]{2,1,0:T(8,128)} %copy-done, f32[45,8,256]{2,1,0:T(8,128)} %copy-done.3, f32[45,8,256]{2,1,0:T(8,128)} %copy-done.2, ...), custom_call_target="tpu_custom_call" | custom-call | flops 1048576 | bytes 4194304 | tf_op jit(solution)/shard_map/pallas_call | solution.py:378
  35.7 3.2 %collective-permute-start.6 = (f32[12,8,128]{2,1,0:T(8,128)}, f32[12,8,128]{2,1,0:T(8,128)S(1)}, u32[]{:S(2)}, u32[]{:S(2)}) collective-permute-start(f32[12,8,128]{2,1,0:T(8,128)} %get-tuple-element.28.q3), channel_id=1, source_target_pairs={{0,160},{32,192},{64,224},{96,0},{128,32},{160,64},{192,96},{224,1... | collective-permute-start | bytes 147464 | tf_op jit(solution)/shard_map/ppermute | solution.py:23
  38.9 1.9 %collective-permute-start.13 = (f32[148,8,128]{2,1,0:T(8,128)}, f32[148,8,128]{2,1,0:T(8,128)}, u32[]{:S(2)}, u32[]{:S(2)}) collective-permute-start(f32[148,8,128]{2,1,0:T(8,128)} %get-tuple-element.36), channel_id=1, source_target_pairs={{0,1},{1,2},{2,3},{3,4},{4,5},{5,6},{6,7},{7,0},{8,9},{9,10},{10,1... | collective-permute-start | bytes 1818632 | tf_op jit(solution)/shard_map/ppermute | solution.py:23
  40.8 1.6 %collective-permute-start.14 = (f32[148,8,128]{2,1,0:T(8,128)}, f32[148,8,128]{2,1,0:T(8,128)}, u32[]{:S(2)}, u32[]{:S(2)}) collective-permute-start(f32[148,8,128]{2,1,0:T(8,128)} %get-tuple-element.37), channel_id=1, source_target_pairs={{0,7},{1,0},{2,1},{3,2},{4,3},{5,4},{6,5},{7,6},{8,15},{9,8},{10,9... | collective-permute-start | bytes 1818632 | tf_op jit(solution)/shard_map/ppermute | solution.py:23
  42.4 10.2 %shard_map.40.e = f32[2,32,272,128]{3,2,1,0:T(8,128)} custom-call(f32[102]{0:T(128)} %reshape.254.ft, f32[32,256,128]{2,1,0:T(8,128)} %d.5, f32[49,8,128]{2,1,0:T(8,128)} %copy-done.1, f32[49,8,128]{2,1,0:T(8,128)} %copy-done, f32[45,8,256]{2,1,0:T(8,128)} %copy-done.3, f32[45,8,256]{2,1,0:T(8,128)} %copy-done.2), custom_call_target="tpu_custom_call" | custom-call | flops 5368709120 | bytes 16777216 | tf_op jit(solution)/shard_map/pallas_call | solution.py:378
  53.2 1.5 %shard_map.41 = f32[8,128]{1,0:T(8,128)} custom-call(f32[12,8,128]{2,1,0:T(8,128)} %get-tuple-element.28.q3, f32[12,8,128]{2,1,0:T(8,128)} %copy-done.4, f32[12,8,128]{2,1,0:T(8,128)} %copy-done.5), custom_call_target="tpu_custom_call" | custom-call | tf_op jit(solution)/shard_map/pallas_call | solution.py:378
  55.9 4.6 %collective-permute-done.7 = f32[8,128]{1,0:T(8,128)S(1)} collective-permute-done((f32[8,128]{1,0:T(8,128)}, f32[8,128]{1,0:T(8,128)S(1)}, u32[]{:S(2)}, u32[]{:S(2)}) %collective-permute-start.7) | collective-permute-done | bytes 4128 | tf_op jit(solution)/shard_map/ppermute | solution.py:23
  60.5 3.2 %collective-permute-start.8 = (f32[8,128]{1,0:T(8,128)}, f32[8,128]{1,0:T(8,128)S(1)}, u32[]{:S(2)}, u32[]{:S(2)}) collective-permute-start(f32[8,128]{1,0:T(8,128)} %shard_map.41), channel_id=1, source_target_pairs={{0,7},{1,0},{2,1},{3,2},{4,3},{5,4},{6,5},{7,6},{8,15},{9,8},{10,9... | collective-permute-start | bytes 12296 | tf_op jit(solution)/shard_map/ppermute | solution.py:23
  63.6 4.3 %shard_map.42.ec = f32[2,16,144,128]{3,2,1,0:T(8,128)} custom-call(f32[102]{0:T(128)} %reshape.255.ct, f32[16,128,128]{2,1,0:T(8,128)} %get-tuple-element.32.g, f32[49,8,128]{2,1,0:T(8,128)} %copy-done.1, f32[49,8,128]{2,1,0:T(8,128)} %copy-done, f32[45,8,256]{2,1,0:T(8,128)} %copy-done.3, f32[45,8,256]{2,1,0:T(8,128)} %copy-done.2), custom_call_target="tpu_custom_call" | custom-call | flops 1073741824 | bytes 4194304 | tf_op jit(solution)/shard_map/pallas_call | solution.py:378
  68.0 0.8 collective-permute-start.10
  68.8 4.5 %collective-permute-start.9 = (f32[3,8,128]{2,1,0:T(8,128)S(1)}, f32[3,8,128]{2,1,0:T(8,128)S(1)}, u32[]{:S(2)}, u32[]{:S(2)}) collective-permute-start(f32[3,8,128]{2,1,0:T(8,128)S(1)} %pad_maximum_fusion), channel_id=1, source_target_pairs={{0,3},{1,4},{2,5},{3,6},{4,7},{5,0},{6,1},{7,2},{8,11},{9,12},{10,... | collective-permute-start | bytes 36872 | tf_op jit(solution)/shard_map/ppermute | solution.py:23
  73.4 29.7 %shard_map.43 = f32[32,256,128]{2,1,0:T(8,128)} custom-call(f32[102]{0:T(128)} %reshape.254.ft, f32[102]{0:T(128)} %reshape.255.ct, f32[2,32,272,128]{3,2,1,0:T(8,128)} %shard_map.40.e, f32[2,16,144,128]{3,2,1,0:T(8,128)} %shard_map.42.ec, f32[8,256,128]{2,1,0:T(8,128)} %copy-done.9, f32[8,256,128]{2,1,0:T(8,128)} %collective-permute-done.12.zh, ...), custom_call_target="tpu_custom_call" | custom-call | flops 8589934592 | bytes 20971520 | tf_op jit(solution)/shard_map/pallas_call | solution.py:378
  104.1 4.7 %broadcast_add_fusion = f32[32,256,128]{2,1,0:T(8,128)} fusion(f32[32,256,128]{2,1,0:T(8,128)} %shard_map.43, f32[256,128]{1,0:T(8,128)S(1)} %bitcast.7), kind=kLoop, calls=%fused_computation | loop fusion | flops 1048576 | bytes 8519680 | tf_op jit(solution)/shard_map/add | solution.py:478
  (61 shorter events, 6.4 us)
Async XLA Ops:
  3.6 9.8 %collective-permute-start.1 = (f32[49,8,128]{2,1,0:T(8,128)}, f32[49,8,128]{2,1,0:T(8,128)S(1)}, u32[]{:S(2)}, u32[]{:S(2)}) collective-permute-start(f32[49,8,128]{2,1,0:T(8,128)} %get-tuple-element.25), channel_id=1, source_target_pairs={{0,24},{8,0},{16,8},{24,16},{1,25},{9,1},{17,9},{25,17},{2,26},{10... | collective-permute-start | bytes 602120 | tf_op jit(solution)/shard_map/ppermute | solution.py:23
  7.3 5.5 %collective-permute-start.2 = (f32[8,128]{1,0:T(8,128)S(1)}, f32[8,128]{1,0:T(8,128)S(1)}, u32[]{:S(2)}, u32[]{:S(2)}) collective-permute-start(f32[8,128]{1,0:T(8,128)S(1)} %get-tuple-element.44), channel_id=1, source_target_pairs={{0,16},{8,24},{16,0},{24,8},{1,17},{9,25},{17,1},{25,9},{2,18},{10... | collective-permute-start | bytes 12296 | tf_op jit(solution)/shard_map/ppermute | solution.py:23
  7.9 7.6 %collective-permute-start = (f32[49,8,128]{2,1,0:T(8,128)}, f32[49,8,128]{2,1,0:T(8,128)S(1)}, u32[]{:S(2)}, u32[]{:S(2)}) collective-permute-start(f32[49,8,128]{2,1,0:T(8,128)} %get-tuple-element.24), channel_id=1, source_target_pairs={{0,8},{8,16},{16,24},{24,0},{1,9},{9,17},{17,25},{25,1},{2,10},{10... | collective-permute-start | bytes 602120 | tf_op jit(solution)/shard_map/ppermute | solution.py:23
  10.6 58.2 %collective-permute-start.11 = (f32[8,256,128]{2,1,0:T(8,128)S(1)}, f32[8,256,128]{2,1,0:T(8,128)S(1)}, u32[]{:S(2)}, u32[]{:S(2)}) collective-permute-start(f32[8,256,128]{2,1,0:T(8,128)S(1)} %get-tuple-element.42), channel_id=1, source_target_pairs={{0,1},{1,2},{2,3},{3,4},{4,5},{5,6},{6,7},{7,0},{8,9},{9,10},{10,1... | collective-permute-start | bytes 3145736 | tf_op jit(solution)/shard_map/ppermute | solution.py:23
  12.6 60.7 %collective-permute-start.12 = (f32[8,256,128]{2,1,0:T(8,128)S(1)}, f32[8,256,128]{2,1,0:T(8,128)}, u32[]{:S(2)}, u32[]{:S(2)}) collective-permute-start(f32[8,256,128]{2,1,0:T(8,128)S(1)} %get-tuple-element.41), channel_id=1, source_target_pairs={{0,7},{1,0},{2,1},{3,2},{4,3},{5,4},{6,5},{7,6},{8,15},{9,8},{10,9... | collective-permute-start | bytes 3145736 | tf_op jit(solution)/shard_map/ppermute | solution.py:23
  13.4 21.8 %copy-start.7 = (f32[2,3,17]{2,0,1:T(2,128)S(1)}, f32[2,3,17]{2,0,1:T(2,128)}, u32[]{:S(2)}) copy-start(f32[2,3,17]{2,0,1:T(2,128)} %param.4) | copy-start | bytes 1228
  13.4 2.2 %copy-start = (f32[49,8,128]{2,1,0:T(8,128)}, f32[49,8,128]{2,1,0:T(8,128)S(1)}, u32[]{:S(2)}) copy-start(f32[49,8,128]{2,1,0:T(8,128)S(1)} %collective-permute-done.1.yh) | copy-start | bytes 602116
  15.6 0.7 copy-start.1
  22.1 6.2 %collective-permute-start.4 = (f32[45,8,256]{2,1,0:T(8,128)}, f32[45,8,256]{2,1,0:T(8,128)S(1)}, u32[]{:S(2)}, u32[]{:S(2)}) collective-permute-start(f32[45,8,256]{2,1,0:T(8,128)} %get-tuple-element.27.own), channel_id=1, source_target_pairs={{0,224},{32,0},{64,32},{96,64},{128,96},{160,128},{192,160},{224,1... | collective-permute-start | bytes 1105928 | tf_op jit(solution)/shard_map/ppermute | solution.py:23
  22.9 8.4 %collective-permute-start.3 = (f32[45,8,256]{2,1,0:T(8,128)}, f32[45,8,256]{2,1,0:T(8,128)S(1)}, u32[]{:S(2)}, u32[]{:S(2)}) collective-permute-start(f32[45,8,256]{2,1,0:T(8,128)} %get-tuple-element.26), channel_id=1, source_target_pairs={{0,32},{32,64},{64,96},{96,128},{128,160},{160,192},{192,224},{224... | collective-permute-start | bytes 1105928 | tf_op jit(solution)/shard_map/ppermute | solution.py:23
  28.3 3.0 %copy-start.2 = (f32[45,8,256]{2,1,0:T(8,128)}, f32[45,8,256]{2,1,0:T(8,128)S(1)}, u32[]{:S(2)}) copy-start(f32[45,8,256]{2,1,0:T(8,128)S(1)} %collective-permute-done.4.xr) | copy-start | bytes 1105924
  31.3 0.8 copy-start.3
  34.9 5.9 %collective-permute-start.5 = (f32[12,8,128]{2,1,0:T(8,128)}, f32[12,8,128]{2,1,0:T(8,128)S(1)}, u32[]{:S(2)}, u32[]{:S(2)}) collective-permute-start(f32[12,8,128]{2,1,0:T(8,128)} %get-tuple-element.28.q3), channel_id=1, source_target_pairs={{0,96},{32,128},{64,160},{96,192},{128,224},{160,0},{192,32},{224,... | collective-permute-start | bytes 147464 | tf_op jit(solution)/shard_map/ppermute | solution.py:23
  35.7 16.9 %collective-permute-start.6 = (f32[12,8,128]{2,1,0:T(8,128)}, f32[12,8,128]{2,1,0:T(8,128)S(1)}, u32[]{:S(2)}, u32[]{:S(2)}) collective-permute-start(f32[12,8,128]{2,1,0:T(8,128)} %get-tuple-element.28.q3), channel_id=1, source_target_pairs={{0,160},{32,192},{64,224},{96,0},{128,32},{160,64},{192,96},{224,1... | collective-permute-start | bytes 147464 | tf_op jit(solution)/shard_map/ppermute | solution.py:23
  38.9 34.5 %collective-permute-start.13 = (f32[148,8,128]{2,1,0:T(8,128)}, f32[148,8,128]{2,1,0:T(8,128)}, u32[]{:S(2)}, u32[]{:S(2)}) collective-permute-start(f32[148,8,128]{2,1,0:T(8,128)} %get-tuple-element.36), channel_id=1, source_target_pairs={{0,1},{1,2},{2,3},{3,4},{4,5},{5,6},{6,7},{7,0},{8,9},{9,10},{10,1... | collective-permute-start | bytes 1818632 | tf_op jit(solution)/shard_map/ppermute | solution.py:23
  40.8 11.8 %copy-start.4 = (f32[12,8,128]{2,1,0:T(8,128)}, f32[12,8,128]{2,1,0:T(8,128)S(1)}, u32[]{:S(2)}) copy-start(f32[12,8,128]{2,1,0:T(8,128)S(1)} %collective-permute-done.5.qm) | copy-start | bytes 147460
  40.8 14.4 %copy-start.8 = (f32[2,3,17]{2,0,1:T(2,128)S(1)}, f32[2,3,17]{2,0,1:T(2,128)}, u32[]{:S(2)}) copy-start(f32[2,3,17]{2,0,1:T(2,128)} %param.5) | copy-start | bytes 1228
  40.8 32.5 %collective-permute-start.14 = (f32[148,8,128]{2,1,0:T(8,128)}, f32[148,8,128]{2,1,0:T(8,128)}, u32[]{:S(2)}, u32[]{:S(2)}) collective-permute-start(f32[148,8,128]{2,1,0:T(8,128)} %get-tuple-element.37), channel_id=1, source_target_pairs={{0,7},{1,0},{2,1},{3,2},{4,3},{5,4},{6,5},{7,6},{8,15},{9,8},{10,9... | collective-permute-start | bytes 1818632 | tf_op jit(solution)/shard_map/ppermute | solution.py:23
  54.7 13.2 %copy-start.6 = (f32[8,128]{1,0:T(8,128)S(1)}, f32[8,128]{1,0:T(8,128)}, u32[]{:S(2)}) copy-start(f32[8,128]{1,0:T(8,128)} %shard_map.41) | copy-start | bytes 12292
  54.7 5.7 %collective-permute-start.7 = (f32[8,128]{1,0:T(8,128)}, f32[8,128]{1,0:T(8,128)S(1)}, u32[]{:S(2)}, u32[]{:S(2)}) collective-permute-start(f32[8,128]{1,0:T(8,128)} %shard_map.41), channel_id=1, source_target_pairs={{0,1},{1,2},{2,3},{3,4},{4,5},{5,6},{6,7},{7,0},{8,9},{9,10},{10,1... | collective-permute-start | bytes 12296 | tf_op jit(solution)/shard_map/ppermute | solution.py:23
  60.5 7.5 %collective-permute-start.8 = (f32[8,128]{1,0:T(8,128)}, f32[8,128]{1,0:T(8,128)S(1)}, u32[]{:S(2)}, u32[]{:S(2)}) collective-permute-start(f32[8,128]{1,0:T(8,128)} %shard_map.41), channel_id=1, source_target_pairs={{0,7},{1,0},{2,1},{3,2},{4,3},{5,4},{6,5},{7,6},{8,15},{9,8},{10,9... | collective-permute-start | bytes 12296 | tf_op jit(solution)/shard_map/ppermute | solution.py:23
  68.0 35.1 %collective-permute-start.10 = (f32[3,8,128]{2,1,0:T(8,128)S(1)}, f32[3,8,128]{2,1,0:T(8,128)S(1)}, u32[]{:S(2)}, u32[]{:S(2)}) collective-permute-start(f32[3,8,128]{2,1,0:T(8,128)S(1)} %pad_maximum_fusion), channel_id=1, source_target_pairs={{0,5},{1,6},{2,7},{3,0},{4,1},{5,2},{6,3},{7,4},{8,13},{9,14},{10,... | collective-permute-start | bytes 36872 | tf_op jit(solution)/shard_map/ppermute | solution.py:23
  68.8 4.5 %copy-start.9 = (f32[8,256,128]{2,1,0:T(8,128)}, f32[8,256,128]{2,1,0:T(8,128)S(1)}, u32[]{:S(2)}) copy-start(f32[8,256,128]{2,1,0:T(8,128)S(1)} %collective-permute-done.11.zl) | copy-start | bytes 3145732
  68.8 34.2 %collective-permute-start.9 = (f32[3,8,128]{2,1,0:T(8,128)S(1)}, f32[3,8,128]{2,1,0:T(8,128)S(1)}, u32[]{:S(2)}, u32[]{:S(2)}) collective-permute-start(f32[3,8,128]{2,1,0:T(8,128)S(1)} %pad_maximum_fusion), channel_id=1, source_target_pairs={{0,3},{1,4},{2,5},{3,6},{4,7},{5,0},{6,1},{7,2},{8,11},{9,12},{10,... | collective-permute-start | bytes 36872 | tf_op jit(solution)/shard_map/ppermute | solution.py:23
  (1 other events, 0.6 us)

commit v2 on v1

--- a/solution.py
+++ b/solution.py
@@ -9,13 +9,12 @@
 f32 = jnp.float32
 bf16 = jnp.bfloat16
 NB = 45
-NT = 148
+NT = 149
 R = 8
 TAPS = 17
 
 VM = pl.BlockSpec(memory_space=pltpu.VMEM)
 SM = pl.BlockSpec(memory_space=pltpu.SMEM)
-PARAMS = pltpu.CompilerParams(vmem_limit_bytes=60 * 1024 * 1024)
 
 
 def shift(value, axis, step):
@@ -37,15 +36,11 @@
     return lax.broadcasted_iota(jnp.int32, shape, dim)
 
 
-def banded(taps, base, delta):
+def banded(taps, t, axis, delta):
     out = jnp.zeros(delta.shape, f32)
     for k in range(TAPS):
-        out = jnp.where(delta == k, taps[base + k], out)
+        out = jnp.where(delta == k, taps[t, axis, k], out)
     return out
-
-
-def tap_base(t, axis):
-    return (t * 3 + axis) * TAPS
 
 
 def x_weights(taps, coarse):
@@ -56,7 +51,7 @@
     def halves(rows, source):
         cols = iota((rows, 128), 1) >> sh
         return jnp.concatenate(
-            [banded(taps, tap_base(t, 0), source - cols + R) * scale for t in range(2)], axis=1
+            [banded(taps, t, 0, source - cols + R) * scale for t in range(2)], axis=1
         )
 
     hi, lo = split(halves(128, iota((128, 128), 0) >> sh))
@@ -70,7 +65,7 @@
     c = iota((64, 256), 1)
     i = iota((64, 256), 0) >> (1 if coarse else 0)
     j = c - jnp.where(c >= seg, seg, 0) - jnp.where(c >= 2 * seg, seg, 0)
-    m = jnp.where(c < 3 * seg, banded(taps, tap_base(t, 1), j - i), 0.0)
+    m = jnp.where(c < 3 * seg, banded(taps, t, 1, j - i), 0.0)
     hi = m.astype(bf16).astype(f32)
     return jnp.where(c < 2 * seg, hi, m - hi).astype(bf16)
 
@@ -94,7 +89,7 @@
     return half(2 * z) + half(2 * z + 1)
 
 
-def prep_kernel(d, g, ylo, yhi):
+def prep_kernel(d, g, ylo, yhi, own):
     def step(z, acc):
         v = pool(d, z)
         g[z] = v
@@ -110,58 +105,62 @@
     yhi[32:48] = g[:, 120:128, :]
     ylo[48] = q
     yhi[48] = q
-
-
-def strip_kernel(d, g, yl, yh, q2, xlo, xhi):
+    own[...] = q
+
+
+def put(xlo, xhi, first, sources, coarse):
+    width = 32 if coarse else 16
     lane = iota((256, 128), 1)
-
-    def put(first, sources):
-        tile = None
-        for p, v in enumerate(sources):
-            v = pltpu.roll(v, (16 * p + 8) % 128, 1)
-            tile = v if tile is None else jnp.where(lane >= 16 * p, v, tile)
-        tile = tile.T
-        for p in range(len(sources)):
-            xhi[first + p] = tile[16 * p : 16 * p + 8]
-            xlo[first + p] = tile[16 * p + 8 : 16 * p + 16]
-
-    for k in range(4):
-        put(8 * k, [d[8 * k + p] for p in range(8)])
-    put(32, [yl[0:32].reshape(256, 128), yh[0:32].reshape(256, 128)])
-
-    def putc(first, sources):
-        tile = None
-        for p, v in enumerate(sources):
+    tile = None
+    for p, v in enumerate(sources):
+        if coarse:
             v = v + pltpu.roll(v, 127, 1)
-            v = pltpu.roll(v, (32 * p + 16) % 128, 1)
-            tile = v if tile is None else jnp.where(lane >= 32 * p, v, tile)
-        tile = tile.T
-        for p in range(len(sources)):
+        v = pltpu.roll(v, (width * p + width // 2) % 128, 1)
+        tile = v if tile is None else jnp.where(lane >= width * p, v, tile)
+    tile = tile.T
+    for p in range(len(sources)):
+        if coarse:
             rows = [tile[32 * p + 2 * i : 32 * p + 2 * i + 1] for i in range(16)]
             xhi[first + p] = jnp.concatenate(rows[0:8], axis=0)
             xlo[first + p] = jnp.concatenate(rows[8:16], axis=0)
-
+        else:
+            xhi[first + p] = tile[16 * p : 16 * p + 8]
+            xlo[first + p] = tile[16 * p + 8 : 16 * p + 16]
+
+
+def strip_kernel(d, g, xlo, xhi):
+    for k in range(4):
+        put(xlo, xhi, 8 * k, [d[8 * k + p] for p in range(8)], False)
     for k in range(2):
-        putc(34 + 4 * k, [g[8 * k + 2 * p : 8 * k + 2 * p + 2].reshape(256, 128) for p in range(4)])
-    putc(
-        42,
-        [jnp.concatenate([yl[32:48].reshape(128, 128), yh[32:48].reshape(128, 128)], axis=0)],
-    )
-    own = jnp.concatenate([yl[48], yh[48]], axis=1)
-    rest = jnp.concatenate([q2[0], q2[1]], axis=1)
-    xlo[43] = own
+        sources = [g[8 * k + 2 * p : 8 * k + 2 * p + 2].reshape(256, 128) for p in range(4)]
+        put(xlo, xhi, 34 + 4 * k, sources, True)
+
+
+def strip_y_kernel(xlo_in, xhi_in, yl, yh, q, q2, xlo, xhi):
+    put(xlo, xhi, 32, [yl[0:32].reshape(256, 128), yh[0:32].reshape(256, 128)], False)
+    coarse = jnp.concatenate([yl[32:48].reshape(128, 128), yh[32:48].reshape(128, 128)], axis=0)
+    put(xlo, xhi, 42, [coarse], True)
+    sides = jnp.concatenate([yl[48], yh[48]], axis=1)
+    rest = jnp.concatenate([q[...], q2[...]], axis=1)
+    xlo[43] = sides
     xlo[44] = rest
-    xhi[43] = own
+    xhi[43] = sides
     xhi[44] = rest
 
 
-def zstrip_kernel(g, yl, yh, xl, xr, own, zlo, zhi, q3):
-    for i, src in enumerate((own, xl, xr)):
-        a, b = src[43], src[44]
-        q3[4 * i] = b[:, 0:128]
-        q3[4 * i + 1] = a[:, 0:128]
-        q3[4 * i + 2] = a[:, 128:256]
-        q3[4 * i + 3] = b[:, 128:256]
+def zstrip_kernel(g, yl, yh, xl, xr, q3, qm, qp, zlo, zhi, own):
+    def quarters(ref, i):
+        a, b = ref[2 * i], ref[2 * i + 1]
+        return [b[:, 0:4], a[:, 0:4], a[:, 128:132], b[:, 128:132]]
+
+    packed = jnp.concatenate(
+        sum((quarters(q3, i) for i in range(3)), [])
+        + quarters(qm, 1) + quarters(qm, 0) + quarters(qm, 2) + quarters(qp, 1) + quarters(qp, 0),
+        axis=1,
+    )
+    own[...] = packed
+    zlo[148] = packed
+    zhi[148] = packed
     for out, p0, far in ((zlo, 0, 4), (zhi, 24, 8)):
         for p in range(8):
             for s, src in ((0, xl), (1, xr)):
@@ -188,13 +187,6 @@
             )
 
 
-def pack_kernel(q3, qm, qp, packed):
-    tiles = [q3[i] for i in range(12)]
-    tiles += [qm[i] for i in (4, 5, 6, 7, 0, 1, 2, 3, 8, 9, 10, 11)]
-    tiles += [qp[i] for i in (4, 5, 6, 7, 0, 1, 2, 3)]
-    packed[...] = jnp.concatenate([v[:, 0:4] for v in tiles], axis=1)
-
-
 def own_fine_kernel(ft, d, yl, yh, xl, xr, e):
     w = x_weights(ft, False)
 
@@ -234,8 +226,8 @@
         ec[t, :, 136:144, :] = r[1, :, :, t * 128 : t * 128 + 128]
 
 
-def z_group(planes, taps, base, count):
-    w = [jnp.full((8, 128), taps[base + k], f32) for k in range(TAPS)]
+def z_group(planes, taps, t, count):
+    w = [jnp.full((8, 128), taps[t, 2, k], f32) for k in range(TAPS)]
     w = [jnp.concatenate([v, v], axis=0) for v in w]
     acc = [None] * count
     for i in range(count + 2 * R):
@@ -247,7 +239,7 @@
     return acc
 
 
-def final_kernel(ft, ct, e, ec, zl, zh, sl, sh, out, eh, ech, gn, fh, fl, fch, fcl):
+def final_kernel(ft, ct, e, ec, zl, zh, sl, sh, tp, out, eh, ech, gn, fh, fl, fch, fcl):
     w = x_weights(ft, False)
 
     def strip(ref, i):
@@ -323,7 +315,7 @@
                         return e[t, i - 8, rows, :]
                     return eh[t, i - 32, rows, :]
 
-                for o, v in enumerate(z_group(plane, ft, tap_base(t, 2), 8)):
+                for o, v in enumerate(z_group(plane, ft, t, 8)):
                     z = 8 * zb + o
                     q, l, r = z // 4, z // 2 % 2, z % 2
                     hi, lo = split(v)
@@ -344,7 +336,7 @@
                         return ec[t, i - 8, rows, :]
                     return ech[t, i - 16, rows, :]
 
-                for o, v in enumerate(z_group(plane, ct, tap_base(t, 2), 8)):
+                for o, v in enumerate(z_group(plane, ct, t, 8)):
                     z = 8 * zb + o
                     hi, lo = split(v)
                     fch[t, z // 2, rows, (z % 2) * 128 : (z % 2) * 128 + 128] = hi
@@ -362,8 +354,11 @@
     @pl.loop(0, 8)
     def _(q):
         for b in range(4):
+            top = jnp.concatenate(
+                [jnp.broadcast_to(tp[2 * b + k : 2 * b + k + 1, :], (32, 128)) for k in range(2)], axis=0
+            )
             common = mm(wyc, stacked(fch, fcl, q, 32 * b, 48))
-            even, odd = common[:, 0:128], common[:, 128:256]
+            even, odd = common[:, 0:128] + top, common[:, 128:256] + top
             for r in range(2):
                 res = mm(wy, stacked(fh, fl, 2 * q + r, 64 * b, 80))
                 out[4 * q + r, 64 * b : 64 * b + 64, :] = res[:, 0:128] + even
@@ -374,14 +369,15 @@
     return jax.ShapeDtypeStruct(shape, f32)
 
 
-def call(kernel, outs, n_smem, args, scratch=(), flops=0, nbytes=0):
+def call(kernel, outs, n_smem, args, scratch=(), flops=0, nbytes=0, grant=12, alias=None):
     return pl.pallas_call(
         kernel,
         out_shape=outs,
         in_specs=[SM] * n_smem + [VM] * (len(args) - n_smem),
         out_specs=jax.tree.map(lambda _: VM, outs),
         scratch_shapes=scratch,
-        compiler_params=PARAMS,
+        compiler_params=pltpu.CompilerParams(vmem_limit_bytes=grant * 1024 * 1024),
+        input_output_aliases=alias or {},
         cost_estimate=pl.CostEstimate(flops=flops, bytes_accessed=nbytes, transcendentals=0),
     )(*args)
 
@@ -390,77 +386,113 @@
 
 
 def wrapped(d, period):
-    d = jnp.abs(d) % period
+    d = jnp.abs(d) & (period - 1)
     return jnp.minimum(d, period - d).astype(f32)
 
 
-def top_potential(parts):
-    lane = jnp.arange(128, dtype=jnp.int32)
-    offx = sum(jnp.where(lane // 16 == i, v, 0) for i, v in enumerate(OFFSETS["gx"]))
-    offy = sum(jnp.where(lane // 4 % 4 == i, v, 0) for i, v in enumerate(OFFSETS["gy"]))
-    zi = jnp.arange(8, dtype=jnp.int32)
-    dz = wrapped(sum(jnp.where(zi == i, v, 0) for i, v in enumerate(OFFSETS["gz"])), 8)
-    ys = offy[None, :] * 8 + jnp.arange(8, dtype=jnp.int32)[:, None]
-    xs = offx * 4 + lane % 4
-    own = jnp.arange(32, dtype=jnp.int32)
-    dy = wrapped((own // 4)[:, None, None] - ys[None], 32)
-    dx = wrapped((own % 4)[:, None, None] - xs[None, None, :], 32)
-    r2 = 1.0 + (dz * dz)[None, :, None, None] + (dy * dy + dx * dx)[:, None]
-    kernel = 1.0 / (256.0 * jnp.sqrt(r2))
-    return jnp.sum(kernel * parts[None], axis=(1, 2, 3)).reshape(8, 4)
+def pick(index, values):
+    out = jnp.zeros(index.shape, jnp.int32)
+    for i, v in enumerate(values):
+        out = jnp.where(index == i, v, out)
+    return out
+
+
+def matrix_kernel(k):
+    lane = iota((8, 128), 1)
+    ys = pick((lane >> 2) & 3, OFFSETS["gy"]) * 8 + iota((8, 128), 0)
+    xs = pick(lane >> 4, OFFSETS["gx"]) * 4 + (lane & 3)
+
+    @pl.loop(0, 8)
+    def _(y):
+        dy = wrapped(y - ys, 32)
+        for x in range(4):
+            dx = wrapped(x - xs, 32)
+            r2 = 1.0 + dy * dy + dx * dx
+            for i, off in enumerate(OFFSETS["gz"]):
+                dz = float(min(abs(off), 8 - abs(off)))
+                k[x, y, i] = 1.0 / (256.0 * jnp.sqrt(r2 + dz * dz))
+
+
+def top_kernel(k, p3, pm, pp, tp):
+    tiles = [p3[0], p3[1], p3[2], pm[1], pm[0], pm[2], pp[1], pp[0]]
+    lane = iota((8, 128), 1) >> 5
+    out = jnp.zeros((8, 128), f32)
+    for x in range(4):
+        rows = []
+        for y in range(8):
+            v = k[x, y, 0] * tiles[0]
+            for i in range(1, 8):
+                v = v + k[x, y, i] * tiles[i]
+            rows.append(jnp.sum(v, axis=0, keepdims=True))
+        total = jnp.sum(jnp.concatenate(rows, axis=0), axis=1, keepdims=True)
+        out = jnp.where(lane == x, jnp.broadcast_to(total, (8, 128)), out)
+    tp[...] = out
+
+
+def q3_kernel(xlo, xl, xr, q3):
+    q3[0:2] = xlo[43:45]
+    q3[2:4] = xl[43:45]
+    q3[4:6] = xr[43:45]
+
+
+def p3_kernel(p0, sl, sh, p3):
+    p3[0] = p0[...]
+    p3[1] = sl[148]
+    p3[2] = sh[148]
 
 
 def body(charges, fine_taps, coarse_taps):
-    ft = fine_taps.reshape(-1)
-    ct = coarse_taps.reshape(-1)
+    ft, ct = fine_taps, coarse_taps
     zl = shift(charges[24:32], "gz", 1)
     zh = shift(charges[0:8], "gz", -1)
 
-    g, ylo, yhi = call(
-        prep_kernel, (sds(16, 128, 128), sds(49, 8, 128), sds(49, 8, 128)), 0, (charges,),
+    g, ylo, yhi, q = call(
+        prep_kernel, (sds(16, 128, 128), sds(49, 8, 128), sds(49, 8, 128), sds(8, 128)), 0, (charges,),
         flops=1 << 22, nbytes=6 << 20,
     )
-    q2 = shift(ylo[48], "gy", 2)
+    q2 = shift(q, "gy", 2)
     yl = shift(yhi, "gy", 1)
     yh = shift(ylo, "gy", -1)
-    q2 = jnp.stack([ylo[48], q2])
 
     xlo, xhi = call(
-        strip_kernel, (sds(NB, 8, 256), sds(NB, 8, 256)), 0, (charges, g, yl, yh, q2),
+        strip_kernel, (sds(NB, 8, 256), sds(NB, 8, 256)), 0, (charges, g),
         flops=1 << 27, nbytes=6 << 20,
+    )
+    xlo, xhi = call(
+        strip_y_kernel, (sds(NB, 8, 256), sds(NB, 8, 256)), 0, (xlo, xhi, yl, yh, q, q2),
+        flops=1 << 24, nbytes=1 << 20, alias={0: 0, 1: 1},
     )
     xl = shift(xhi, "gx", 1)
     xr = shift(xlo, "gx", -1)
 
-    zlo, zhi, q3 = call(
-        zstrip_kernel, (sds(NT, 8, 128), sds(NT, 8, 128), sds(12, 8, 128)), 0,
-        (g, yl, yh, xl, xr, xlo), flops=1 << 20, nbytes=4 << 20,
+    k = call(matrix_kernel, sds(4, 8, 8, 8, 128), 0, (), flops=1 << 24, nbytes=1 << 20)
+    q3 = call(q3_kernel, sds(6, 8, 256), 0, (xlo, xl, xr))
+    qm = shift(q3, "gx", 3)
+    qp = shift(q3, "gx", -3)
+
+    zlo, zhi, p0 = call(
+        zstrip_kernel, (sds(NT, 8, 128), sds(NT, 8, 128), sds(8, 128)), 0,
+        (g, yl, yh, xl, xr, q3, qm, qp), flops=1 << 20, nbytes=4 << 20,
     )
     sl = shift(zhi, "gz", 1)
     sh = shift(zlo, "gz", -1)
-    qm = shift(q3, "gx", 3)
-    qp = shift(q3, "gx", -3)
 
     e = call(
         own_fine_kernel, sds(2, 32, 272, 128), 1,
         (ft, charges, yl, yh, xl, xr), flops=5 << 30, nbytes=16 << 20,
     )
 
-    qm, qp, e = lax.optimization_barrier((qm, qp, e))
-    p0 = call(pack_kernel, sds(8, 128), 0, (q3, qm, qp))
-    pl1 = shift(p0, "gz", 1)
-    pr1 = shift(p0, "gz", -1)
-    p0, g = lax.optimization_barrier((p0, g))
+    p3 = call(p3_kernel, sds(3, 8, 128), 0, (p0, sl, sh))
+    pm = shift(p3, "gz", 3)
+    pp = shift(p3, "gz", -3)
     ec = call(
         own_coarse_kernel, sds(2, 16, 144, 128), 1,
         (ct, g, yl, yh, xl, xr), flops=1 << 30, nbytes=4 << 20,
     )
-    p3, ec = lax.optimization_barrier((jnp.stack([p0, pl1, pr1]), ec))
-    pm = shift(p3, "gz", 3)
-    pp = shift(p3, "gz", -3)
+    tp = call(top_kernel, sds(8, 128), 0, (k, p3, pm, pp))
 
     out = call(
-        final_kernel, sds(32, 256, 128), 2, (ft, ct, e, ec, zl, zh, sl, sh),
+        final_kernel, sds(32, 256, 128), 2, (ft, ct, e, ec, zl, zh, sl, sh, tp),
         scratch=[
             pltpu.VMEM((2, 16, 272, 128), f32),
             pltpu.VMEM((2, 16, 144, 128), f32),
@@ -470,12 +502,9 @@
             pltpu.VMEM((2, 8, 144, 256), bf16),
             pltpu.VMEM((2, 8, 144, 256), bf16),
         ],
-        flops=8 << 30, nbytes=20 << 20,
-    )
-    pm, pp, out = lax.optimization_barrier((pm, pp, out))
-    parts = jnp.stack([p3[0], p3[1], p3[2], pm[1], pm[0], pm[2], pp[1], pp[0]])
-    tp = jnp.repeat(top_potential(parts), 32, axis=1)
-    return (out.reshape(32, 8, 32, 128) + tp[None, :, None, :]).reshape(32, 256, 128)
+        flops=8 << 30, nbytes=20 << 20, grant=30,
+    )
+    return out
 
 
 def solution(mesh):

time: 109 us -> 92 us (0.84)
  the two profiles are of different devices: /device:TPU:32 before, /device:TPU:2 now
where the time goes in v2:
time: 92 us; the launch traced here: 91.9 us
  Pallas kernels  35.7 us (39%)
  waiting for transfers between devices  28.1 us (31%)
  starting transfers between devices  25.7 us (28%)
  local copies, waits for them, and re-layouts  2.34 us (3%)
    pallas_call x11, Pallas kernels, call(): pl.pallas_call(kernel, out_shape=outs, in_specs=[SM] * n_smem + [VM] * (l...  35.7 us
    ppermute x13, waiting for transfers between devices, shift(): lax.ppermute(value, axis, [(i, (i + step) % count) for i in range(count)])  28.1 us
    ppermute x13, starting transfers between devices, shift(): lax.ppermute(value, axis, [(i, (i + step) % count) for i in range(count)])  25.7 us
    unnamed x10, local copies, waits for them, and re-layouts  2.2 us
  transfers between devices with their start and end apart: 13, of which 5 were waited for; matrix products, arithmetic and copies ran while one was open for 0% of the time, Pallas kernels for 10%

profile of v2, /device:TPU:2, one launch (start us, length us, event | category | flops | bytes accessed | tf_op | source)
XLA Modules:
  0.0 91.9 jit_solution(7192990860107352960)
XLA Ops:
  0.0 2.2 %copy-done = f32[32,256,128]{2,1,0:T(8,128)S(1)} copy-done((f32[32,256,128]{2,1,0:T(8,128)S(1)}, f32[32,256,128]{2,1,0:T(8,128)}, u32[]{:S(2)}) %copy-start) | copy-done | bytes 4194328
  2.2 0.5 shard_map.37
  2.7 1.6 %collective-permute-start = (f32[49,8,128]{2,1,0:T(8,128)S(1)}, f32[49,8,128]{2,1,0:T(8,128)S(1)}, u32[]{:S(2)}, u32[]{:S(2)}) collective-permute-start(f32[49,8,128]{2,1,0:T(8,128)S(1)} %get-tuple-element.16), channel_id=1, source_target_pairs={{0,8},{8,16},{16,24},{24,0},{1,9},{9,17},{17,25},{25,1},{2,10},{10... | collective-permute-start | bytes 602120 | tf_op jit(solution)/shard_map/ppermute | solution.py:22
  4.2 1.7 %collective-permute-start.1 = (f32[49,8,128]{2,1,0:T(8,128)S(1)}, f32[49,8,128]{2,1,0:T(8,128)S(1)}, u32[]{:S(2)}, u32[]{:S(2)}) collective-permute-start(f32[49,8,128]{2,1,0:T(8,128)S(1)} %get-tuple-element.17), channel_id=1, source_target_pairs={{0,24},{8,0},{16,8},{24,16},{1,25},{9,1},{17,9},{25,17},{2,26},{10... | collective-permute-start | bytes 602120 | tf_op jit(solution)/shard_map/ppermute | solution.py:22
  5.9 2.0 %collective-permute-start.2 = (f32[8,128]{1,0:T(8,128)S(1)}, f32[8,128]{1,0:T(8,128)S(1)}, u32[]{:S(2)}, u32[]{:S(2)}) collective-permute-start(f32[8,128]{1,0:T(8,128)S(1)} %get-tuple-element.21.q), channel_id=1, source_target_pairs={{0,16},{8,24},{16,0},{24,8},{1,17},{9,25},{17,1},{25,9},{2,18},{10... | collective-permute-start | bytes 12296 | tf_op jit(solution)/shard_map/ppermute | solution.py:22
  7.9 2.2 %shard_map.38 = (f32[45,8,256]{2,1,0:T(8,128)S(1)}, f32[45,8,256]{2,1,0:T(8,128)S(1)}) custom-call(f32[32,256,128]{2,1,0:T(8,128)S(1)} %copy-done, f32[16,128,128]{2,1,0:T(8,128)S(1)} %get-tuple-element.18.g), custom_call_target="tpu_custom_call" | custom-call | flops 134217728 | bytes 6291456 | tf_op jit(solution)/shard_map/pallas_call | solution.py:373
  10.1 1.8 %collective-permute-done.2.q2 = f32[8,128]{1,0:T(8,128)S(1)} collective-permute-done((f32[8,128]{1,0:T(8,128)S(1)}, f32[8,128]{1,0:T(8,128)S(1)}, u32[]{:S(2)}, u32[]{:S(2)}) %collective-permute-start.2) | collective-permute-done | bytes 4128 | tf_op jit(solution)/shard_map/ppermute | solution.py:22
  12.0 0.3 shard_map.39
  12.3 1.7 %collective-permute-start.4 = (f32[45,8,256]{2,1,0:T(8,128)S(1)}, f32[45,8,256]{2,1,0:T(8,128)S(1)}, u32[]{:S(2)}, u32[]{:S(2)}) collective-permute-start(f32[45,8,256]{2,1,0:T(8,128)S(1)} %get-tuple-element.23.xlo), channel_id=1, source_target_pairs={{0,224},{32,0},{64,32},{96,64},{128,96},{160,128},{192,160},{224,1... | collective-permute-start | bytes 1105928 | tf_op jit(solution)/shard_map/ppermute | solution.py:22
  14.2 5.9 %collective-permute-start.6 = (f32[8,256,128]{2,1,0:T(8,128)S(1)}, f32[8,256,128]{2,1,0:T(8,128)S(1)}, u32[]{:S(2)}, u32[]{:S(2)}) collective-permute-start(f32[8,256,128]{2,1,0:T(8,128)S(1)} %get-tuple-element.27), channel_id=1, source_target_pairs={{0,7},{1,0},{2,1},{3,2},{4,3},{5,4},{6,5},{7,6},{8,15},{9,8},{10,9... | collective-permute-start | bytes 3145736 | tf_op jit(solution)/shard_map/ppermute | solution.py:22
  20.1 3.4 %collective-permute-start.8 = (f32[6,8,256]{2,1,0:T(8,128)S(1)}, f32[6,8,256]{2,1,0:T(8,128)S(1)}, u32[]{:S(2)}, u32[]{:S(2)}) collective-permute-start(f32[6,8,256]{2,1,0:T(8,128)S(1)} %shard_map.42.q3), channel_id=1, source_target_pairs={{0,160},{32,192},{64,224},{96,0},{128,32},{160,64},{192,96},{224,1... | collective-permute-start | bytes 147464 | tf_op jit(solution)/shard_map/ppermute | solution.py:22
  23.5 2.0 %collective-permute-done.8.qp = f32[6,8,256]{2,1,0:T(8,128)S(1)} collective-permute-done((f32[6,8,256]{2,1,0:T(8,128)S(1)}, f32[6,8,256]{2,1,0:T(8,128)S(1)}, u32[]{:S(2)}, u32[]{:S(2)}) %collective-permute-start.8) | collective-permute-done | bytes 49184 | tf_op jit(solution)/shard_map/ppermute | solution.py:22
  25.5 3.0 %collective-permute-done.7.qm = f32[6,8,256]{2,1,0:T(8,128)S(1)} collective-permute-done((f32[6,8,256]{2,1,0:T(8,128)S(1)}, f32[6,8,256]{2,1,0:T(8,128)S(1)}, u32[]{:S(2)}, u32[]{:S(2)}) %collective-permute-start.7) | collective-permute-done | bytes 49184 | tf_op jit(solution)/shard_map/ppermute | solution.py:22
  28.7 1.2 %collective-permute-start.9 = (f32[149,8,128]{2,1,0:T(8,128)S(1)}, f32[149,8,128]{2,1,0:T(8,128)S(1)}, u32[]{:S(2)}, u32[]{:S(2)}) collective-permute-start(f32[149,8,128]{2,1,0:T(8,128)S(1)} %get-tuple-element.24), channel_id=1, source_target_pairs={{0,1},{1,2},{2,3},{3,4},{4,5},{5,6},{6,7},{7,0},{8,9},{9,10},{10,1... | collective-permute-start | bytes 1830920 | tf_op jit(solution)/shard_map/ppermute | solution.py:22
  29.9 4.3 %collective-permute-start.10 = (f32[149,8,128]{2,1,0:T(8,128)S(1)}, f32[149,8,128]{2,1,0:T(8,128)S(1)}, u32[]{:S(2)}, u32[]{:S(2)}) collective-permute-start(f32[149,8,128]{2,1,0:T(8,128)S(1)} %get-tuple-element.25), channel_id=1, source_target_pairs={{0,7},{1,0},{2,1},{3,2},{4,3},{5,4},{6,5},{7,6},{8,15},{9,8},{10,9... | collective-permute-start | bytes 1830920 | tf_op jit(solution)/shard_map/ppermute | solution.py:22
  34.2 0.4 shard_map.44.k
  34.6 4.8 %shard_map.40.e = f32[2,32,272,128]{3,2,1,0:T(8,128)S(1)} custom-call(f32[2,3,17]{2,1,0:T(4,128)S(1)} %copy.8.ft, f32[32,256,128]{2,1,0:T(8,128)S(1)} %copy-done.1, f32[49,8,128]{2,1,0:T(8,128)S(1)} %collective-permute-done.yl, f32[49,8,128]{2,1,0:T(8,128)S(1)} %collective-permute-done.1.yh, f32[45,8,256]{2,1,0:T(8,128)S(1)} %collective-permute-done.3.xl, ...), custom_call_target="tpu_custom_call" | custom-call | flops 5368709120 | bytes 16777216 | tf_op jit(solution)/shard_map/pallas_call | solution.py:373
  39.4 19.6 %collective-permute-done.9.sl = f32[149,8,128]{2,1,0:T(8,128)S(1)} collective-permute-done((f32[149,8,128]{2,1,0:T(8,128)S(1)}, f32[149,8,128]{2,1,0:T(8,128)S(1)}, u32[]{:S(2)}, u32[]{:S(2)}) %collective-permute-start.9) | collective-permute-done | bytes 610336 | tf_op jit(solution)/shard_map/ppermute | solution.py:22
  59.0 0.7 collective-permute-start.12
  59.7 3.1 %collective-permute-start.11 = (f32[3,8,128]{2,1,0:T(8,128)S(1)}, f32[3,8,128]{2,1,0:T(8,128)S(1)}, u32[]{:S(2)}, u32[]{:S(2)}) collective-permute-start(f32[3,8,128]{2,1,0:T(8,128)S(1)} %shard_map.45.p3), channel_id=1, source_target_pairs={{0,3},{1,4},{2,5},{3,6},{4,7},{5,0},{6,1},{7,2},{8,11},{9,12},{10,... | collective-permute-start | bytes 36872 | tf_op jit(solution)/shard_map/ppermute | solution.py:22
  62.9 1.9 %shard_map.41.ec = f32[2,16,144,128]{3,2,1,0:T(8,128)S(1)} custom-call(f32[2,3,17]{2,1,0:T(4,128)S(1)} %copy.9.ct, f32[16,128,128]{2,1,0:T(8,128)S(1)} %get-tuple-element.18.g, f32[49,8,128]{2,1,0:T(8,128)S(1)} %collective-permute-done.yl, f32[49,8,128]{2,1,0:T(8,128)S(1)} %collective-permute-done.1.yh, f32[45,8,256]{2,1,0:T(8,128)S(1)} %collective-permute-done.3.xl, ...), custom_call_target="tpu_custom_call" | custom-call | flops 1073741824 | bytes 4194304 | tf_op jit(solution)/shard_map/pallas_call | solution.py:373
  64.8 1.6 %collective-permute-done.11.pm = f32[3,8,128]{2,1,0:T(8,128)S(1)} collective-permute-done((f32[3,8,128]{2,1,0:T(8,128)S(1)}, f32[3,8,128]{2,1,0:T(8,128)S(1)}, u32[]{:S(2)}, u32[]{:S(2)}) %collective-permute-start.11) | collective-permute-done | bytes 12320 | tf_op jit(solution)/shard_map/ppermute | solution.py:22
  66.4 0.2 shard_map.46.tp
  66.6 25.3 %shard_map.47 = f32[32,256,128]{2,1,0:T(8,128)} custom-call(f32[2,3,17]{2,1,0:T(4,128)S(1)} %copy.8.ft, f32[2,3,17]{2,1,0:T(4,128)S(1)} %copy.9.ct, f32[2,32,272,128]{3,2,1,0:T(8,128)S(1)} %shard_map.40.e, f32[2,16,144,128]{3,2,1,0:T(8,128)S(1)} %shard_map.41.ec, f32[8,256,128]{2,1,0:T(8,128)S(1)} %collective-permute-done.5.zl, ...), custom_call_target="tpu_custom_call" | custom-call | flops 8589934592 | bytes 20971520 | tf_op jit(solution)/shard_map/pallas_call | solution.py:373
  (24 shorter events, 0.3 us)
Async XLA Ops:
  0.0 2.2 %copy-start = (f32[32,256,128]{2,1,0:T(8,128)S(1)}, f32[32,256,128]{2,1,0:T(8,128)}, u32[]{:S(2)}) copy-start(f32[32,256,128]{2,1,0:T(8,128)} %d.5) | copy-start | bytes 12582916
  2.7 11.4 %copy-start.1 = (f32[32,256,128]{2,1,0:T(8,128)S(1)}, f32[32,256,128]{2,1,0:T(8,128)}, u32[]{:S(2)}) copy-start(f32[32,256,128]{2,1,0:T(8,128)} %d.5) | copy-start | bytes 12582916
  2.7 9.3 %collective-permute-start = (f32[49,8,128]{2,1,0:T(8,128)S(1)}, f32[49,8,128]{2,1,0:T(8,128)S(1)}, u32[]{:S(2)}, u32[]{:S(2)}) collective-permute-start(f32[49,8,128]{2,1,0:T(8,128)S(1)} %get-tuple-element.16), channel_id=1, source_target_pairs={{0,8},{8,16},{16,24},{24,0},{1,9},{9,17},{17,25},{25,1},{2,10},{10... | collective-permute-start | bytes 602120 | tf_op jit(solution)/shard_map/ppermute | solution.py:22
  4.2 7.7 %collective-permute-start.1 = (f32[49,8,128]{2,1,0:T(8,128)S(1)}, f32[49,8,128]{2,1,0:T(8,128)S(1)}, u32[]{:S(2)}, u32[]{:S(2)}) collective-permute-start(f32[49,8,128]{2,1,0:T(8,128)S(1)} %get-tuple-element.17), channel_id=1, source_target_pairs={{0,24},{8,0},{16,8},{24,16},{1,25},{9,1},{17,9},{25,17},{2,26},{10... | collective-permute-start | bytes 602120 | tf_op jit(solution)/shard_map/ppermute | solution.py:22
  5.9 6.0 %collective-permute-start.2 = (f32[8,128]{1,0:T(8,128)S(1)}, f32[8,128]{1,0:T(8,128)S(1)}, u32[]{:S(2)}, u32[]{:S(2)}) collective-permute-start(f32[8,128]{1,0:T(8,128)S(1)} %get-tuple-element.21.q), channel_id=1, source_target_pairs={{0,16},{8,24},{16,0},{24,8},{1,17},{9,25},{17,1},{25,9},{2,18},{10... | collective-permute-start | bytes 12296 | tf_op jit(solution)/shard_map/ppermute | solution.py:22
  11.9 22.3 %copy-start.2 = (f32[2,3,17]{2,0,1:T(2,128)S(1)}, f32[2,3,17]{2,0,1:T(2,128)}, u32[]{:S(2)}) copy-start(f32[2,3,17]{2,0,1:T(2,128)} %param.4) | copy-start | bytes 1228
  11.9 22.3 %copy-start.3 = (f32[2,3,17]{2,0,1:T(2,128)S(1)}, f32[2,3,17]{2,0,1:T(2,128)}, u32[]{:S(2)}) copy-start(f32[2,3,17]{2,0,1:T(2,128)} %param.5) | copy-start | bytes 1228
  12.3 7.8 %collective-permute-start.3 = (f32[45,8,256]{2,1,0:T(8,128)S(1)}, f32[45,8,256]{2,1,0:T(8,128)S(1)}, u32[]{:S(2)}, u32[]{:S(2)}) collective-permute-start(f32[45,8,256]{2,1,0:T(8,128)S(1)} %get-tuple-element.22), channel_id=1, source_target_pairs={{0,32},{32,64},{64,96},{96,128},{128,160},{160,192},{192,224},{224... | collective-permute-start | bytes 1105928 | tf_op jit(solution)/shard_map/ppermute | solution.py:22
  12.3 7.8 %collective-permute-start.4 = (f32[45,8,256]{2,1,0:T(8,128)S(1)}, f32[45,8,256]{2,1,0:T(8,128)S(1)}, u32[]{:S(2)}, u32[]{:S(2)}) collective-permute-start(f32[45,8,256]{2,1,0:T(8,128)S(1)} %get-tuple-element.23.xlo), channel_id=1, source_target_pairs={{0,224},{32,0},{64,32},{96,64},{128,96},{160,128},{192,160},{224,1... | collective-permute-start | bytes 1105928 | tf_op jit(solution)/shard_map/ppermute | solution.py:22
  14.2 52.4 %collective-permute-start.6 = (f32[8,256,128]{2,1,0:T(8,128)S(1)}, f32[8,256,128]{2,1,0:T(8,128)S(1)}, u32[]{:S(2)}, u32[]{:S(2)}) collective-permute-start(f32[8,256,128]{2,1,0:T(8,128)S(1)} %get-tuple-element.27), channel_id=1, source_target_pairs={{0,7},{1,0},{2,1},{3,2},{4,3},{5,4},{6,5},{7,6},{8,15},{9,8},{10,9... | collective-permute-start | bytes 3145736 | tf_op jit(solution)/shard_map/ppermute | solution.py:22
  20.1 46.5 %collective-permute-start.5 = (f32[8,256,128]{2,1,0:T(8,128)S(1)}, f32[8,256,128]{2,1,0:T(8,128)S(1)}, u32[]{:S(2)}, u32[]{:S(2)}) collective-permute-start(f32[8,256,128]{2,1,0:T(8,128)S(1)} %get-tuple-element.28), channel_id=1, source_target_pairs={{0,1},{1,2},{2,3},{3,4},{4,5},{5,6},{6,7},{7,0},{8,9},{9,10},{10,1... | collective-permute-start | bytes 3145736 | tf_op jit(solution)/shard_map/ppermute | solution.py:22
  20.1 5.4 %collective-permute-start.8 = (f32[6,8,256]{2,1,0:T(8,128)S(1)}, f32[6,8,256]{2,1,0:T(8,128)S(1)}, u32[]{:S(2)}, u32[]{:S(2)}) collective-permute-start(f32[6,8,256]{2,1,0:T(8,128)S(1)} %shard_map.42.q3), channel_id=1, source_target_pairs={{0,160},{32,192},{64,224},{96,0},{128,32},{160,64},{192,96},{224,1... | collective-permute-start | bytes 147464 | tf_op jit(solution)/shard_map/ppermute | solution.py:22
  23.5 5.0 %collective-permute-start.7 = (f32[6,8,256]{2,1,0:T(8,128)S(1)}, f32[6,8,256]{2,1,0:T(8,128)S(1)}, u32[]{:S(2)}, u32[]{:S(2)}) collective-permute-start(f32[6,8,256]{2,1,0:T(8,128)S(1)} %shard_map.42.q3), channel_id=1, source_target_pairs={{0,96},{32,128},{64,160},{96,192},{128,224},{160,0},{192,32},{224,... | collective-permute-start | bytes 147464 | tf_op jit(solution)/shard_map/ppermute | solution.py:22
  28.7 30.4 %collective-permute-start.9 = (f32[149,8,128]{2,1,0:T(8,128)S(1)}, f32[149,8,128]{2,1,0:T(8,128)S(1)}, u32[]{:S(2)}, u32[]{:S(2)}) collective-permute-start(f32[149,8,128]{2,1,0:T(8,128)S(1)} %get-tuple-element.24), channel_id=1, source_target_pairs={{0,1},{1,2},{2,3},{3,4},{4,5},{5,6},{6,7},{7,0},{8,9},{9,10},{10,1... | collective-permute-start | bytes 1830920 | tf_op jit(solution)/shard_map/ppermute | solution.py:22
  29.9 29.2 %collective-permute-start.10 = (f32[149,8,128]{2,1,0:T(8,128)S(1)}, f32[149,8,128]{2,1,0:T(8,128)S(1)}, u32[]{:S(2)}, u32[]{:S(2)}) collective-permute-start(f32[149,8,128]{2,1,0:T(8,128)S(1)} %get-tuple-element.25), channel_id=1, source_target_pairs={{0,7},{1,0},{2,1},{3,2},{4,3},{5,4},{6,5},{7,6},{8,15},{9,8},{10,9... | collective-permute-start | bytes 1830920 | tf_op jit(solution)/shard_map/ppermute | solution.py:22
  59.0 5.8 %collective-permute-start.12 = (f32[3,8,128]{2,1,0:T(8,128)S(1)}, f32[3,8,128]{2,1,0:T(8,128)S(1)}, u32[]{:S(2)}, u32[]{:S(2)}) collective-permute-start(f32[3,8,128]{2,1,0:T(8,128)S(1)} %shard_map.45.p3), channel_id=1, source_target_pairs={{0,5},{1,6},{2,7},{3,0},{4,1},{5,2},{6,3},{7,4},{8,13},{9,14},{10,... | collective-permute-start | bytes 36872 | tf_op jit(solution)/shard_map/ppermute | solution.py:22
  59.7 6.7 %collective-permute-start.11 = (f32[3,8,128]{2,1,0:T(8,128)S(1)}, f32[3,8,128]{2,1,0:T(8,128)S(1)}, u32[]{:S(2)}, u32[]{:S(2)}) collective-permute-start(f32[3,8,128]{2,1,0:T(8,128)S(1)} %shard_map.45.p3), channel_id=1, source_target_pairs={{0,3},{1,4},{2,5},{3,6},{4,7},{5,0},{6,1},{7,2},{8,11},{9,12},{10,... | collective-permute-start | bytes 36872 | tf_op jit(solution)/shard_map/ppermute | solution.py:22

commit v3 on v2

--- a/solution.py
+++ b/solution.py
@@ -9,7 +9,7 @@
 f32 = jnp.float32
 bf16 = jnp.bfloat16
 NB = 45
-NT = 149
+NT = 148
 R = 8
 TAPS = 17
 
@@ -148,19 +148,19 @@
     xhi[44] = rest
 
 
-def zstrip_kernel(g, yl, yh, xl, xr, q3, qm, qp, zlo, zhi, own):
+def pack_kernel(q3, qm, qp, own):
     def quarters(ref, i):
         a, b = ref[2 * i], ref[2 * i + 1]
         return [b[:, 0:4], a[:, 0:4], a[:, 128:132], b[:, 128:132]]
 
-    packed = jnp.concatenate(
+    own[...] = jnp.concatenate(
         sum((quarters(q3, i) for i in range(3)), [])
         + quarters(qm, 1) + quarters(qm, 0) + quarters(qm, 2) + quarters(qp, 1) + quarters(qp, 0),
         axis=1,
     )
-    own[...] = packed
-    zlo[148] = packed
-    zhi[148] = packed
+
+
+def zstrip_kernel(g, yl, yh, xl, xr, zlo, zhi):
     for out, p0, far in ((zlo, 0, 4), (zhi, 24, 8)):
         for p in range(8):
             for s, src in ((0, xl), (1, xr)):
@@ -205,7 +205,7 @@
             e[t, :, row : row + 8, :] = r[:, :, t * 128 : t * 128 + 128]
 
 
-def own_coarse_kernel(ct, g, yl, yh, xl, xr, ec):
+def own_coarse(ct, g, yl, yh, xl, xr, ec):
     def strip(i):
         return jnp.concatenate([xl[i], xr[i]], axis=0)
 
@@ -226,20 +226,56 @@
         ec[t, :, 136:144, :] = r[1, :, :, t * 128 : t * 128 + 128]
 
 
-def z_group(planes, taps, t, count):
+def z_group(planes, taps, t, first, last, acc=None):
     w = [jnp.full((8, 128), taps[t, 2, k], f32) for k in range(TAPS)]
     w = [jnp.concatenate([v, v], axis=0) for v in w]
-    acc = [None] * count
-    for i in range(count + 2 * R):
+    acc = [None] * 8 if acc is None else list(acc)
+    for i in range(first, last):
         v = planes(i)
-        for o in range(count):
+        for o in range(8):
             k = i - o
             if 0 <= k < TAPS:
                 acc[o] = w[k] * v if acc[o] is None else acc[o] + w[k] * v
     return acc
 
 
-def final_kernel(ft, ct, e, ec, zl, zh, sl, sh, tp, out, eh, ech, gn, fh, fl, fch, fcl):
+def put_pair(hi_ref, lo_ref, t, first, rows, values):
+    for z, v in enumerate(values):
+        q, l, r = z // 4, z // 2 % 2, z % 2
+        hi, lo = split(v)
+        hi_ref[t, first + 2 * q + r, rows, l * 128 : l * 128 + 128] = hi
+        lo_ref[t, first + 2 * q + r, rows, l * 128 : l * 128 + 128] = lo
+
+
+def inner_kernel(ft, ct, e, g, yl, yh, xl, xr, fih, fil, pa, pc, ec):
+    own_coarse(ct, g, yl, yh, xl, xr, ec)
+
+    @pl.loop(0, 17)
+    def _(y):
+        rows = pl.ds(pl.multiple_of(y * 16, 16), 16)
+        for t in range(2):
+            for n in range(2):
+
+                def plane(i, t=t, n=n):
+                    return e[t, i + 8 * n, rows, :]
+
+                put_pair(fih, fil, t, 4 * n, rows, z_group(plane, ft, t, 0, 24))
+            for o, v in enumerate(z_group(lambda i, t=t: e[t, i - 8, rows, :], ft, t, 8, 24)):
+                pa[t, 0, o, rows, :] = v
+            for o, v in enumerate(z_group(lambda i, t=t: e[t, i + 16, rows, :], ft, t, 0, 16)):
+                pa[t, 1, o, rows, :] = v
+
+    @pl.loop(0, 9)
+    def _(y):
+        rows = pl.ds(pl.multiple_of(y * 16, 16), 16)
+        for t in range(2):
+            for o, v in enumerate(z_group(lambda i, t=t: ec[t, i - 8, rows, :], ct, t, 8, 24)):
+                pc[t, 0, o, rows, :] = v
+            for o, v in enumerate(z_group(lambda i, t=t: ec[t, i, rows, :], ct, t, 0, 16)):
+                pc[t, 1, o, rows, :] = v
+
+
+def outer_kernel(ft, ct, pa, pc, zl, zh, sl, sh, fh, fl, fch, fcl, eh, ech, gn):
     w = x_weights(ft, False)
 
     def strip(ref, i):
@@ -301,47 +337,31 @@
             ech[t, 8 * n : 8 * n + 8, 0:8, :] = r[n, 0, :, :, t * 128 : t * 128 + 128]
             ech[t, 8 * n : 8 * n + 8, 136:144, :] = r[n, 1, :, :, t * 128 : t * 128 + 128]
 
+    def rest(planes, taps, partial, t, n, rows):
+        acc = [partial[t, n, o, rows, :] for o in range(8)]
+        first = 16 * n
+        return z_group(lambda i: planes[t, 8 * n + i - first, rows, :], taps, t, first, first + 8, acc)
+
     @pl.loop(0, 17)
     def _(y):
         rows = pl.ds(pl.multiple_of(y * 16, 16), 16)
         for t in range(2):
-            for zb in range(4):
-
-                def plane(i, t=t, zb=zb):
-                    i = i + 8 * zb
-                    if i < 8:
-                        return eh[t, i, rows, :]
-                    if i < 40:
-                        return e[t, i - 8, rows, :]
-                    return eh[t, i - 32, rows, :]
-
-                for o, v in enumerate(z_group(plane, ft, t, 8)):
-                    z = 8 * zb + o
-                    q, l, r = z // 4, z // 2 % 2, z % 2
-                    hi, lo = split(v)
-                    fh[t, 2 * q + r, rows, l * 128 : l * 128 + 128] = hi
-                    fl[t, 2 * q + r, rows, l * 128 : l * 128 + 128] = lo
+            for n in range(2):
+                put_pair(fh, fl, t, 4 * n, rows, rest(eh, ft, pa, t, n, rows))
 
     @pl.loop(0, 9)
     def _(y):
         rows = pl.ds(pl.multiple_of(y * 16, 16), 16)
         for t in range(2):
-            for zb in range(2):
-
-                def plane(i, t=t, zb=zb):
-                    i = i + 8 * zb
-                    if i < 8:
-                        return ech[t, i, rows, :]
-                    if i < 24:
-                        return ec[t, i - 8, rows, :]
-                    return ech[t, i - 16, rows, :]
-
-                for o, v in enumerate(z_group(plane, ct, t, 8)):
-                    z = 8 * zb + o
+            for n in range(2):
+                for o, v in enumerate(rest(ech, ct, pc, t, n, rows)):
                     hi, lo = split(v)
-                    fch[t, z // 2, rows, (z % 2) * 128 : (z % 2) * 128 + 128] = hi
-                    fcl[t, z // 2, rows, (z % 2) * 128 : (z % 2) * 128 + 128] = lo
-
+                    cols = slice((o % 2) * 128, (o % 2) * 128 + 128)
+                    fch[t, 4 * n + o // 2, rows, cols] = hi
+                    fcl[t, 4 * n + o // 2, rows, cols] = lo
+
+
+def final_kernel(ft, ct, fh, fl, fih, fil, fch, fcl, tp, out):
     wy, wyc = (
         jnp.concatenate([y_weights(taps, t, coarse) for t in range(2)], axis=1)
         for taps, coarse in ((ft, False), (ct, True))
@@ -351,8 +371,7 @@
         rows = slice(first, first + size)
         return jnp.concatenate([stack(h[t, index, rows, :], l[t, index, rows, :]) for t in range(2)], axis=0)
 
-    @pl.loop(0, 8)
-    def _(q):
+    def slab(q, h, l, first):
         for b in range(4):
             top = jnp.concatenate(
                 [jnp.broadcast_to(tp[2 * b + k : 2 * b + k + 1, :], (32, 128)) for k in range(2)], axis=0
@@ -360,9 +379,18 @@
             common = mm(wyc, stacked(fch, fcl, q, 32 * b, 48))
             even, odd = common[:, 0:128] + top, common[:, 128:256] + top
             for r in range(2):
-                res = mm(wy, stacked(fh, fl, 2 * q + r, 64 * b, 80))
+                res = mm(wy, stacked(h, l, first + r, 64 * b, 80))
                 out[4 * q + r, 64 * b : 64 * b + 64, :] = res[:, 0:128] + even
                 out[4 * q + 2 + r, 64 * b : 64 * b + 64, :] = res[:, 128:256] + odd
+
+    @pl.loop(2, 6)
+    def _(q):
+        slab(q, fih, fil, 2 * q - 4)
+
+    @pl.loop(0, 2)
+    def _(n):
+        slab(n, fh, fl, 2 * n)
+        slab(6 + n, fh, fl, 4 + 2 * n)
 
 
 def sds(*shape):
@@ -437,8 +465,8 @@
 
 def p3_kernel(p0, sl, sh, p3):
     p3[0] = p0[...]
-    p3[1] = sl[148]
-    p3[2] = sh[148]
+    p3[1] = sl[...]
+    p3[2] = sh[...]
 
 
 def body(charges, fine_taps, coarse_taps):
@@ -467,42 +495,45 @@
 
     k = call(matrix_kernel, sds(4, 8, 8, 8, 128), 0, (), flops=1 << 24, nbytes=1 << 20)
     q3 = call(q3_kernel, sds(6, 8, 256), 0, (xlo, xl, xr))
+    zlo, zhi = call(
+        zstrip_kernel, (sds(NT, 8, 128), sds(NT, 8, 128)), 0, (g, yl, yh, xl, xr),
+        flops=1 << 20, nbytes=4 << 20,
+    )
+    sl = shift(zhi, "gz", 1)
+    sh = shift(zlo, "gz", -1)
     qm = shift(q3, "gx", 3)
     qp = shift(q3, "gx", -3)
-
-    zlo, zhi, p0 = call(
-        zstrip_kernel, (sds(NT, 8, 128), sds(NT, 8, 128), sds(8, 128)), 0,
-        (g, yl, yh, xl, xr, q3, qm, qp), flops=1 << 20, nbytes=4 << 20,
-    )
-    sl = shift(zhi, "gz", 1)
-    sh = shift(zlo, "gz", -1)
 
     e = call(
         own_fine_kernel, sds(2, 32, 272, 128), 1,
         (ft, charges, yl, yh, xl, xr), flops=5 << 30, nbytes=16 << 20,
     )
-
-    p3 = call(p3_kernel, sds(3, 8, 128), 0, (p0, sl, sh))
+    p0 = call(pack_kernel, sds(8, 128), 0, (q3, qm, qp))
+    pl1 = shift(p0, "gz", 1)
+    pr1 = shift(p0, "gz", -1)
+    half = jax.ShapeDtypeStruct((2, 8, 272, 256), bf16)
+    quarter = jax.ShapeDtypeStruct((2, 8, 144, 256), bf16)
+    fih, fil, pa, pc = call(
+        inner_kernel, (half, half, sds(2, 2, 8, 272, 128), sds(2, 2, 8, 144, 128)), 2,
+        (ft, ct, e, g, yl, yh, xl, xr), scratch=[pltpu.VMEM((2, 16, 144, 128), f32)],
+        flops=5 << 30, nbytes=16 << 20,
+    )
+    p3 = call(p3_kernel, sds(3, 8, 128), 0, (p0, pl1, pr1))
     pm = shift(p3, "gz", 3)
     pp = shift(p3, "gz", -3)
-    ec = call(
-        own_coarse_kernel, sds(2, 16, 144, 128), 1,
-        (ct, g, yl, yh, xl, xr), flops=1 << 30, nbytes=4 << 20,
-    )
-    tp = call(top_kernel, sds(8, 128), 0, (k, p3, pm, pp))
-
-    out = call(
-        final_kernel, sds(32, 256, 128), 2, (ft, ct, e, ec, zl, zh, sl, sh, tp),
+    fh, fl, fch, fcl = call(
+        outer_kernel, (half, half, quarter, quarter), 2, (ft, ct, pa, pc, zl, zh, sl, sh),
         scratch=[
             pltpu.VMEM((2, 16, 272, 128), f32),
             pltpu.VMEM((2, 16, 144, 128), f32),
             pltpu.VMEM((8, 128, 128), f32),
-            pltpu.VMEM((2, 16, 272, 256), bf16),
-            pltpu.VMEM((2, 16, 272, 256), bf16),
-            pltpu.VMEM((2, 8, 144, 256), bf16),
-            pltpu.VMEM((2, 8, 144, 256), bf16),
         ],
-        flops=8 << 30, nbytes=20 << 20, grant=30,
+        flops=4 << 30, nbytes=16 << 20, grant=16,
+    )
+    tp = call(top_kernel, sds(8, 128), 0, (k, p3, pm, pp))
+    out = call(
+        final_kernel, sds(32, 256, 128), 2, (ft, ct, fh, fl, fih, fil, fch, fcl, tp),
+        flops=2 << 30, nbytes=16 << 20,
     )
     return out
 

time: 92 us -> 98.1 us (1.066)
  the two profiles are of different devices: /device:TPU:2 before, /device:TPU:32 now
where the time goes in v3:
time: 98.1 us; the launch traced here: 98 us
  Pallas kernels  36.5 us (37%)
  waiting for transfers between devices  34.3 us (35%)
  starting transfers between devices  24.8 us (25%)
  local copies, waits for them, and re-layouts  2.35 us (2%)
    pallas_call x13, Pallas kernels, call(): pl.pallas_call(kernel, out_shape=outs, in_specs=[SM] * n_smem + [VM] * (l...  36.5 us
    ppermute x15, waiting for transfers between devices, shift(): lax.ppermute(value, axis, [(i, (i + step) % count) for i in range(count)])  34.3 us
    ppermute x15, starting transfers between devices, shift(): lax.ppermute(value, axis, [(i, (i + step) % count) for i in range(count)])  24.8 us
    unnamed x10, local copies, waits for them, and re-layouts  2.2 us
  transfers between devices with their start and end apart: 15, of which 6 were waited for; matrix products, arithmetic and copies ran while one was open for 0% of the time, Pallas kernels for 22%

profile of v3, /device:TPU:32, one launch (start us, length us, event | category | flops | bytes accessed | tf_op | source)
XLA Modules:
  0.0 98.0 jit_solution(14257406743495459301)
XLA Ops:
  0.0 2.2 %copy-done = f32[32,256,128]{2,1,0:T(8,128)S(1)} copy-done((f32[32,256,128]{2,1,0:T(8,128)S(1)}, f32[32,256,128]{2,1,0:T(8,128)}, u32[]{:S(2)}) %copy-start) | copy-done | bytes 4194328
  2.7 1.6 %collective-permute-start = (f32[49,8,128]{2,1,0:T(8,128)S(1)}, f32[49,8,128]{2,1,0:T(8,128)S(1)}, u32[]{:S(2)}, u32[]{:S(2)}) collective-permute-start(f32[49,8,128]{2,1,0:T(8,128)S(1)} %get-tuple-element.23), channel_id=1, source_target_pairs={{0,8},{8,16},{16,24},{24,0},{1,9},{9,17},{17,25},{25,1},{2,10},{10... | collective-permute-start | bytes 602120 | tf_op jit(solution)/shard_map/ppermute | solution.py:22
  4.2 1.7 %collective-permute-start.1 = (f32[49,8,128]{2,1,0:T(8,128)S(1)}, f32[49,8,128]{2,1,0:T(8,128)S(1)}, u32[]{:S(2)}, u32[]{:S(2)}) collective-permute-start(f32[49,8,128]{2,1,0:T(8,128)S(1)} %get-tuple-element.24), channel_id=1, source_target_pairs={{0,24},{8,0},{16,8},{24,16},{1,25},{9,1},{17,9},{25,17},{2,26},{10... | collective-permute-start | bytes 602120 | tf_op jit(solution)/shard_map/ppermute | solution.py:22
  5.9 2.0 %collective-permute-start.2 = (f32[8,128]{1,0:T(8,128)S(1)}, f32[8,128]{1,0:T(8,128)S(1)}, u32[]{:S(2)}, u32[]{:S(2)}) collective-permute-start(f32[8,128]{1,0:T(8,128)S(1)} %get-tuple-element.28.q), channel_id=1, source_target_pairs={{0,16},{8,24},{16,0},{24,8},{1,17},{9,25},{17,1},{25,9},{2,18},{10... | collective-permute-start | bytes 12296 | tf_op jit(solution)/shard_map/ppermute | solution.py:22
  7.9 2.2 %shard_map.38 = (f32[45,8,256]{2,1,0:T(8,128)S(1)}, f32[45,8,256]{2,1,0:T(8,128)S(1)}) custom-call(f32[32,256,128]{2,1,0:T(8,128)S(1)} %copy-done, f32[16,128,128]{2,1,0:T(8,128)S(1)} %get-tuple-element.25.g), custom_call_target="tpu_custom_call" | custom-call | flops 134217728 | bytes 6291456 | tf_op jit(solution)/shard_map/pallas_call | solution.py:401
  10.1 1.8 %collective-permute-done.2.q2 = f32[8,128]{1,0:T(8,128)S(1)} collective-permute-done((f32[8,128]{1,0:T(8,128)S(1)}, f32[8,128]{1,0:T(8,128)S(1)}, u32[]{:S(2)}, u32[]{:S(2)}) %collective-permute-start.2) | collective-permute-done | bytes 4128 | tf_op jit(solution)/shard_map/ppermute | solution.py:22
  12.2 1.1 %collective-permute-start.4 = (f32[45,8,256]{2,1,0:T(8,128)S(1)}, f32[45,8,256]{2,1,0:T(8,128)S(1)}, u32[]{:S(2)}, u32[]{:S(2)}) collective-permute-start(f32[45,8,256]{2,1,0:T(8,128)S(1)} %get-tuple-element.30.xlo), channel_id=1, source_target_pairs={{0,224},{32,0},{64,32},{96,64},{128,96},{160,128},{192,160},{224,1... | collective-permute-start | bytes 1105928 | tf_op jit(solution)/shard_map/ppermute | solution.py:22
  13.3 5.0 %collective-permute-done.4.xr = f32[45,8,256]{2,1,0:T(8,128)S(1)} collective-permute-done((f32[45,8,256]{2,1,0:T(8,128)S(1)}, f32[45,8,256]{2,1,0:T(8,128)S(1)}, u32[]{:S(2)}, u32[]{:S(2)}) %collective-permute-start.4) | collective-permute-done | bytes 368672 | tf_op jit(solution)/shard_map/ppermute | solution.py:22
  18.3 3.1 %collective-permute-done.3.xl = f32[45,8,256]{2,1,0:T(8,128)S(1)} collective-permute-done((f32[45,8,256]{2,1,0:T(8,128)S(1)}, f32[45,8,256]{2,1,0:T(8,128)S(1)}, u32[]{:S(2)}, u32[]{:S(2)}) %collective-permute-start.3) | collective-permute-done | bytes 368672 | tf_op jit(solution)/shard_map/ppermute | solution.py:22
  21.8 1.5 %collective-permute-start.9 = (f32[6,8,256]{2,1,0:T(8,128)S(1)}, f32[6,8,256]{2,1,0:T(8,128)S(1)}, u32[]{:S(2)}, u32[]{:S(2)}) collective-permute-start(f32[6,8,256]{2,1,0:T(8,128)S(1)} %shard_map.45.q3), channel_id=1, source_target_pairs={{0,96},{32,128},{64,160},{96,192},{128,224},{160,0},{192,32},{224,... | collective-permute-start | bytes 147464 | tf_op jit(solution)/shard_map/ppermute | solution.py:22
  23.4 2.0 %collective-permute-start.5 = (f32[8,256,128]{2,1,0:T(8,128)S(1)}, f32[8,256,128]{2,1,0:T(8,128)S(1)}, u32[]{:S(2)}, u32[]{:S(2)}) collective-permute-start(f32[8,256,128]{2,1,0:T(8,128)S(1)} %get-tuple-element.42), channel_id=1, source_target_pairs={{0,1},{1,2},{2,3},{3,4},{4,5},{5,6},{6,7},{7,0},{8,9},{9,10},{10,1... | collective-permute-start | bytes 3145736 | tf_op jit(solution)/shard_map/ppermute | solution.py:22
  25.6 1.3 %collective-permute-done.9.qm = f32[6,8,256]{2,1,0:T(8,128)S(1)} collective-permute-done((f32[6,8,256]{2,1,0:T(8,128)S(1)}, f32[6,8,256]{2,1,0:T(8,128)S(1)}, u32[]{:S(2)}, u32[]{:S(2)}) %collective-permute-start.9) | collective-permute-done | bytes 49184 | tf_op jit(solution)/shard_map/ppermute | solution.py:22
  27.0 2.0 %collective-permute-start.11 = (f32[8,128]{1,0:T(8,128)S(1)}, f32[8,128]{1,0:T(8,128)S(1)}, u32[]{:S(2)}, u32[]{:S(2)}) collective-permute-start(f32[8,128]{1,0:T(8,128)S(1)} %shard_map.46.p0), channel_id=1, source_target_pairs={{0,1},{1,2},{2,3},{3,4},{4,5},{5,6},{6,7},{7,0},{8,9},{9,10},{10,1... | collective-permute-start | bytes 12296 | tf_op jit(solution)/shard_map/ppermute | solution.py:22
  28.9 0.9 collective-permute-start.12
  30.4 1.2 %collective-permute-start.7 = (f32[148,8,128]{2,1,0:T(8,128)S(1)}, f32[148,8,128]{2,1,0:T(8,128)S(1)}, u32[]{:S(2)}, u32[]{:S(2)}) collective-permute-start(f32[148,8,128]{2,1,0:T(8,128)S(1)} %get-tuple-element.33), channel_id=1, source_target_pairs={{0,1},{1,2},{2,3},{3,4},{4,5},{5,6},{6,7},{7,0},{8,9},{9,10},{10,1... | collective-permute-start | bytes 1818632 | tf_op jit(solution)/shard_map/ppermute | solution.py:22
  31.6 18.1 %collective-permute-done.11.sl = f32[8,128]{1,0:T(8,128)S(1)} collective-permute-done((f32[8,128]{1,0:T(8,128)S(1)}, f32[8,128]{1,0:T(8,128)S(1)}, u32[]{:S(2)}, u32[]{:S(2)}) %collective-permute-start.11) | collective-permute-done | bytes 4128 | tf_op jit(solution)/shard_map/ppermute | solution.py:22
  49.6 3.9 %collective-permute-start.8 = (f32[148,8,128]{2,1,0:T(8,128)S(1)}, f32[148,8,128]{2,1,0:T(8,128)S(1)}, u32[]{:S(2)}, u32[]{:S(2)}) collective-permute-start(f32[148,8,128]{2,1,0:T(8,128)S(1)} %get-tuple-element.34), channel_id=1, source_target_pairs={{0,7},{1,0},{2,1},{3,2},{4,3},{5,4},{6,5},{7,6},{8,15},{9,8},{10,9... | collective-permute-start | bytes 1818632 | tf_op jit(solution)/shard_map/ppermute | solution.py:22
  53.6 3.2 %collective-permute-start.13 = (f32[3,8,128]{2,1,0:T(8,128)S(1)}, f32[3,8,128]{2,1,0:T(8,128)S(1)}, u32[]{:S(2)}, u32[]{:S(2)}) collective-permute-start(f32[3,8,128]{2,1,0:T(8,128)S(1)} %shard_map.47.p3), channel_id=1, source_target_pairs={{0,3},{1,4},{2,5},{3,6},{4,7},{5,0},{6,1},{7,2},{8,11},{9,12},{10,... | collective-permute-start | bytes 36872 | tf_op jit(solution)/shard_map/ppermute | solution.py:22
  56.8 4.8 %shard_map.40.e = f32[2,32,272,128]{3,2,1,0:T(8,128)S(1)} custom-call(f32[2,3,17]{2,1,0:T(4,128)S(1)} %copy.11.ft, f32[32,256,128]{2,1,0:T(8,128)S(1)} %copy-done.1, f32[49,8,128]{2,1,0:T(8,128)S(1)} %collective-permute-done.yl, f32[49,8,128]{2,1,0:T(8,128)S(1)} %collective-permute-done.1.yh, f32[45,8,256]{2,1,0:T(8,128)S(1)} %collective-permute-done.3.xl, ...), custom_call_target="tpu_custom_call" | custom-call | flops 5368709120 | bytes 16777216 | tf_op jit(solution)/shard_map/pallas_call | solution.py:401
  61.6 4.9 %collective-permute-done.13.pm = f32[3,8,128]{2,1,0:T(8,128)S(1)} collective-permute-done((f32[3,8,128]{2,1,0:T(8,128)S(1)}, f32[3,8,128]{2,1,0:T(8,128)S(1)}, u32[]{:S(2)}, u32[]{:S(2)}) %collective-permute-start.13) | collective-permute-done | bytes 12320 | tf_op jit(solution)/shard_map/ppermute | solution.py:22
  66.5 3.4 %collective-permute-start.14 = (f32[3,8,128]{2,1,0:T(8,128)S(1)}, f32[3,8,128]{2,1,0:T(8,128)S(1)}, u32[]{:S(2)}, u32[]{:S(2)}) collective-permute-start(f32[3,8,128]{2,1,0:T(8,128)S(1)} %shard_map.47.p3), channel_id=1, source_target_pairs={{0,5},{1,6},{2,7},{3,0},{4,1},{5,2},{6,3},{7,4},{8,13},{9,14},{10,... | collective-permute-start | bytes 36872 | tf_op jit(solution)/shard_map/ppermute | solution.py:22
  69.8 13.6 %shard_map.41 = (bf16[2,8,272,256]{3,2,1,0:T(8,128)(2,1)S(1)}, bf16[2,8,272,256]{3,2,1,0:T(8,128)(2,1)S(1)}, f32[2,2,8,272,128]{4,3,2,1,0:T(8,128)S(1)}, f32[2,2,8,144,128]{4,3,2,1,0:T(8,128)S(1)}) custom-call(f32[2,3,17]{2,1,0:T(4,128)S(1)} %copy.11.ft, f32[2,3,17]{2,1,0:T(4,128)S(1)} %copy.12.ct, f32[2,32,272,128]{3,2,1,0:T(8,128)S(1)} %shard_map.40.e, ...), custom_call_target="tpu_custom_call" | custom-call | flops 5368709120 | bytes 16777216 | tf_op jit(solution)/shard_map/pallas_call | solution.py:401
  83.7 7.2 %shard_map.43 = (bf16[2,8,272,256]{3,2,1,0:T(8,128)(2,1)S(1)}, bf16[2,8,272,256]{3,2,1,0:T(8,128)(2,1)S(1)}, bf16[2,8,144,256]{3,2,1,0:T(8,128)(2,1)S(1)}, bf16[2,8,144,256]{3,2,1,0:T(8,128)(2,1)S(1)}) custom-call(f32[2,3,17]{2,1,0:T(4,128)S(1)} %copy.11.ft, f32[2,3,17]{2,1,0:T(4,128)S(1)} %copy.12.ct, f32[2,2,8,272,128]{4,3,2,1,0:T(8,128)S(1)} %get-tuple-element.31.pa, ...), custom_call_target="tpu_custom_call" | custom-call | flops 4294967296 | bytes 16777216 | tf_op jit(solution)/shard_map/pallas_call | solution.py:401
  90.8 7.2 %shard_map.49 = f32[32,256,128]{2,1,0:T(8,128)} custom-call(f32[2,3,17]{2,1,0:T(4,128)S(1)} %copy.11.ft, f32[2,3,17]{2,1,0:T(4,128)S(1)} %copy.12.ct, bf16[2,8,272,256]{3,2,1,0:T(8,128)(2,1)S(1)} %get-tuple-element.35.fh, bf16[2,8,272,256]{3,2,1,0:T(8,128)(2,1)S(1)} %get-tuple-element.36.fl, bf16[2,8,272,256]{3,2,1,0:T(8,128)(2,1)S(1)} %get-tuple-element.37.fih, ...), custom_call_target="tpu_custom_call" | custom-call | flops 2147483648 | bytes 16777216 | tf_op jit(solution)/shard_map/pallas_call | solution.py:401
  (30 shorter events, 2.2 us)
Async XLA Ops:
  0.0 2.2 %copy-start = (f32[32,256,128]{2,1,0:T(8,128)S(1)}, f32[32,256,128]{2,1,0:T(8,128)}, u32[]{:S(2)}) copy-start(f32[32,256,128]{2,1,0:T(8,128)} %d.5) | copy-start | bytes 12582916
  2.7 9.3 %collective-permute-start = (f32[49,8,128]{2,1,0:T(8,128)S(1)}, f32[49,8,128]{2,1,0:T(8,128)S(1)}, u32[]{:S(2)}, u32[]{:S(2)}) collective-permute-start(f32[49,8,128]{2,1,0:T(8,128)S(1)} %get-tuple-element.23), channel_id=1, source_target_pairs={{0,8},{8,16},{16,24},{24,0},{1,9},{9,17},{17,25},{25,1},{2,10},{10... | collective-permute-start | bytes 602120 | tf_op jit(solution)/shard_map/ppermute | solution.py:22
  4.2 7.7 %collective-permute-start.1 = (f32[49,8,128]{2,1,0:T(8,128)S(1)}, f32[49,8,128]{2,1,0:T(8,128)S(1)}, u32[]{:S(2)}, u32[]{:S(2)}) collective-permute-start(f32[49,8,128]{2,1,0:T(8,128)S(1)} %get-tuple-element.24), channel_id=1, source_target_pairs={{0,24},{8,0},{16,8},{24,16},{1,25},{9,1},{17,9},{25,17},{2,26},{10... | collective-permute-start | bytes 602120 | tf_op jit(solution)/shard_map/ppermute | solution.py:22
  5.9 6.0 %collective-permute-start.2 = (f32[8,128]{1,0:T(8,128)S(1)}, f32[8,128]{1,0:T(8,128)S(1)}, u32[]{:S(2)}, u32[]{:S(2)}) collective-permute-start(f32[8,128]{1,0:T(8,128)S(1)} %get-tuple-element.28.q), channel_id=1, source_target_pairs={{0,16},{8,24},{16,0},{24,8},{1,17},{9,25},{17,1},{25,9},{2,18},{10... | collective-permute-start | bytes 12296 | tf_op jit(solution)/shard_map/ppermute | solution.py:22
  7.9 15.4 %copy-start.1 = (f32[32,256,128]{2,1,0:T(8,128)S(1)}, f32[32,256,128]{2,1,0:T(8,128)}, u32[]{:S(2)}) copy-start(f32[32,256,128]{2,1,0:T(8,128)} %d.5) | copy-start | bytes 12582916
  12.2 6.1 %collective-permute-start.4 = (f32[45,8,256]{2,1,0:T(8,128)S(1)}, f32[45,8,256]{2,1,0:T(8,128)S(1)}, u32[]{:S(2)}, u32[]{:S(2)}) collective-permute-start(f32[45,8,256]{2,1,0:T(8,128)S(1)} %get-tuple-element.30.xlo), channel_id=1, source_target_pairs={{0,224},{32,0},{64,32},{96,64},{128,96},{160,128},{192,160},{224,1... | collective-permute-start | bytes 1105928 | tf_op jit(solution)/shard_map/ppermute | solution.py:22
  13.3 8.1 %collective-permute-start.3 = (f32[45,8,256]{2,1,0:T(8,128)S(1)}, f32[45,8,256]{2,1,0:T(8,128)S(1)}, u32[]{:S(2)}, u32[]{:S(2)}) collective-permute-start(f32[45,8,256]{2,1,0:T(8,128)S(1)} %get-tuple-element.29), channel_id=1, source_target_pairs={{0,32},{32,64},{64,96},{96,128},{128,160},{160,192},{192,224},{224... | collective-permute-start | bytes 1105928 | tf_op jit(solution)/shard_map/ppermute | solution.py:22
  21.5 8.4 %copy-start.2 = (f32[2,3,17]{2,0,1:T(2,128)S(1)}, f32[2,3,17]{2,0,1:T(2,128)}, u32[]{:S(2)}) copy-start(f32[2,3,17]{2,0,1:T(2,128)} %param.4) | copy-start | bytes 1228
  21.5 8.4 %copy-start.3 = (f32[2,3,17]{2,0,1:T(2,128)S(1)}, f32[2,3,17]{2,0,1:T(2,128)}, u32[]{:S(2)}) copy-start(f32[2,3,17]{2,0,1:T(2,128)} %param.5) | copy-start | bytes 1228
  21.5 4.1 %collective-permute-start.10 = (f32[6,8,256]{2,1,0:T(8,128)S(1)}, f32[6,8,256]{2,1,0:T(8,128)S(1)}, u32[]{:S(2)}, u32[]{:S(2)}) collective-permute-start(f32[6,8,256]{2,1,0:T(8,128)S(1)} %shard_map.45.q3), channel_id=1, source_target_pairs={{0,160},{32,192},{64,224},{96,0},{128,32},{160,64},{192,96},{224,1... | collective-permute-start | bytes 147464 | tf_op jit(solution)/shard_map/ppermute | solution.py:22
  21.8 5.0 %collective-permute-start.9 = (f32[6,8,256]{2,1,0:T(8,128)S(1)}, f32[6,8,256]{2,1,0:T(8,128)S(1)}, u32[]{:S(2)}, u32[]{:S(2)}) collective-permute-start(f32[6,8,256]{2,1,0:T(8,128)S(1)} %shard_map.45.q3), channel_id=1, source_target_pairs={{0,96},{32,128},{64,160},{96,192},{128,224},{160,0},{192,32},{224,... | collective-permute-start | bytes 147464 | tf_op jit(solution)/shard_map/ppermute | solution.py:22
  23.4 60.2 %collective-permute-start.5 = (f32[8,256,128]{2,1,0:T(8,128)S(1)}, f32[8,256,128]{2,1,0:T(8,128)S(1)}, u32[]{:S(2)}, u32[]{:S(2)}) collective-permute-start(f32[8,256,128]{2,1,0:T(8,128)S(1)} %get-tuple-element.42), channel_id=1, source_target_pairs={{0,1},{1,2},{2,3},{3,4},{4,5},{5,6},{6,7},{7,0},{8,9},{9,10},{10,1... | collective-permute-start | bytes 3145736 | tf_op jit(solution)/shard_map/ppermute | solution.py:22
  25.4 58.2 %collective-permute-start.6 = (f32[8,256,128]{2,1,0:T(8,128)S(1)}, f32[8,256,128]{2,1,0:T(8,128)S(1)}, u32[]{:S(2)}, u32[]{:S(2)}) collective-permute-start(f32[8,256,128]{2,1,0:T(8,128)S(1)} %get-tuple-element.41), channel_id=1, source_target_pairs={{0,7},{1,0},{2,1},{3,2},{4,3},{5,4},{6,5},{7,6},{8,15},{9,8},{10,9... | collective-permute-start | bytes 3145736 | tf_op jit(solution)/shard_map/ppermute | solution.py:22
  27.0 22.7 %collective-permute-start.11 = (f32[8,128]{1,0:T(8,128)S(1)}, f32[8,128]{1,0:T(8,128)S(1)}, u32[]{:S(2)}, u32[]{:S(2)}) collective-permute-start(f32[8,128]{1,0:T(8,128)S(1)} %shard_map.46.p0), channel_id=1, source_target_pairs={{0,1},{1,2},{2,3},{3,4},{4,5},{5,6},{6,7},{7,0},{8,9},{9,10},{10,1... | collective-permute-start | bytes 12296 | tf_op jit(solution)/shard_map/ppermute | solution.py:22
  28.9 24.6 %collective-permute-start.12 = (f32[8,128]{1,0:T(8,128)S(1)}, f32[8,128]{1,0:T(8,128)S(1)}, u32[]{:S(2)}, u32[]{:S(2)}) collective-permute-start(f32[8,128]{1,0:T(8,128)S(1)} %shard_map.46.p0), channel_id=1, source_target_pairs={{0,7},{1,0},{2,1},{3,2},{4,3},{5,4},{6,5},{7,6},{8,15},{9,8},{10,9... | collective-permute-start | bytes 12296 | tf_op jit(solution)/shard_map/ppermute | solution.py:22
  30.4 53.3 %collective-permute-start.7 = (f32[148,8,128]{2,1,0:T(8,128)S(1)}, f32[148,8,128]{2,1,0:T(8,128)S(1)}, u32[]{:S(2)}, u32[]{:S(2)}) collective-permute-start(f32[148,8,128]{2,1,0:T(8,128)S(1)} %get-tuple-element.33), channel_id=1, source_target_pairs={{0,1},{1,2},{2,3},{3,4},{4,5},{5,6},{6,7},{7,0},{8,9},{9,10},{10,1... | collective-permute-start | bytes 1818632 | tf_op jit(solution)/shard_map/ppermute | solution.py:22
  49.6 34.0 %collective-permute-start.8 = (f32[148,8,128]{2,1,0:T(8,128)S(1)}, f32[148,8,128]{2,1,0:T(8,128)S(1)}, u32[]{:S(2)}, u32[]{:S(2)}) collective-permute-start(f32[148,8,128]{2,1,0:T(8,128)S(1)} %get-tuple-element.34), channel_id=1, source_target_pairs={{0,7},{1,0},{2,1},{3,2},{4,3},{5,4},{6,5},{7,6},{8,15},{9,8},{10,9... | collective-permute-start | bytes 1818632 | tf_op jit(solution)/shard_map/ppermute | solution.py:22
  53.6 12.9 %collective-permute-start.13 = (f32[3,8,128]{2,1,0:T(8,128)S(1)}, f32[3,8,128]{2,1,0:T(8,128)S(1)}, u32[]{:S(2)}, u32[]{:S(2)}) collective-permute-start(f32[3,8,128]{2,1,0:T(8,128)S(1)} %shard_map.47.p3), channel_id=1, source_target_pairs={{0,3},{1,4},{2,5},{3,6},{4,7},{5,0},{6,1},{7,2},{8,11},{9,12},{10,... | collective-permute-start | bytes 36872 | tf_op jit(solution)/shard_map/ppermute | solution.py:22
  66.5 17.0 %collective-permute-start.14 = (f32[3,8,128]{2,1,0:T(8,128)S(1)}, f32[3,8,128]{2,1,0:T(8,128)S(1)}, u32[]{:S(2)}, u32[]{:S(2)}) collective-permute-start(f32[3,8,128]{2,1,0:T(8,128)S(1)} %shard_map.47.p3), channel_id=1, source_target_pairs={{0,5},{1,6},{2,7},{3,0},{4,1},{5,2},{6,3},{7,4},{8,13},{9,14},{10,... | collective-permute-start | bytes 36872 | tf_op jit(solution)/shard_map/ppermute | solution.py:22

commit v4 on v3

--- a/solution.py
+++ b/solution.py
@@ -187,8 +187,8 @@
             )
 
 
-def own_fine_kernel(ft, d, yl, yh, xl, xr, e):
-    w = x_weights(ft, False)
+def own_fine_kernel(wref, d, yl, yh, xl, xr, e):
+    w = wref[...]
 
     def strip(i):
         return jnp.concatenate([xl[i], xr[i]], axis=0)
@@ -205,11 +205,11 @@
             e[t, :, row : row + 8, :] = r[:, :, t * 128 : t * 128 + 128]
 
 
-def own_coarse(ct, g, yl, yh, xl, xr, ec):
+def own_coarse(wcref, g, yl, yh, xl, xr, ec):
     def strip(i):
         return jnp.concatenate([xl[i], xr[i]], axis=0)
 
-    wc = x_weights(ct, True)
+    wc = wcref[...]
 
     @pl.loop(0, 8, unroll=4)
     def _(b):
@@ -247,8 +247,8 @@
         lo_ref[t, first + 2 * q + r, rows, l * 128 : l * 128 + 128] = lo
 
 
-def inner_kernel(ft, ct, e, g, yl, yh, xl, xr, fih, fil, pa, pc, ec):
-    own_coarse(ct, g, yl, yh, xl, xr, ec)
+def inner_kernel(ft, ct, wcref, e, g, yl, yh, xl, xr, fih, fil, pa, pc, ec):
+    own_coarse(wcref, g, yl, yh, xl, xr, ec)
 
     @pl.loop(0, 17)
     def _(y):
@@ -275,8 +275,8 @@
                 pc[t, 1, o, rows, :] = v
 
 
-def outer_kernel(ft, ct, pa, pc, zl, zh, sl, sh, fh, fl, fch, fcl, eh, ech, gn):
-    w = x_weights(ft, False)
+def outer_kernel(ft, ct, wref, wcref, pa, pc, zl, zh, sl, sh, fh, fl, fch, fcl, eh, ech, gn):
+    w = wref[...]
 
     def strip(ref, i):
         return jnp.concatenate(
@@ -316,7 +316,7 @@
             eh[t, 8 * n : 8 * n + 8, 0:8, :] = r[n, 0, :, :, t * 128 : t * 128 + 128]
             eh[t, 8 * n : 8 * n + 8, 264:272, :] = r[n, 1, :, :, t * 128 : t * 128 + 128]
 
-    wc = x_weights(ct, True)
+    wc = wcref[...]
     for n, s in enumerate((sl, sh)):
         for b in range(4):
             near = b >= 2 if n == 0 else b < 2
@@ -361,11 +361,16 @@
                     fcl[t, 4 * n + o // 2, rows, cols] = lo
 
 
-def final_kernel(ft, ct, fh, fl, fih, fil, fch, fcl, tp, out):
-    wy, wyc = (
-        jnp.concatenate([y_weights(taps, t, coarse) for t in range(2)], axis=1)
-        for taps, coarse in ((ft, False), (ct, True))
-    )
+def weights_kernel(ft, ct, w, wc, wy, wyc):
+    w[...] = x_weights(ft, False)
+    wc[...] = x_weights(ct, True)
+    for t in range(2):
+        wy[:, t * 256 : t * 256 + 256] = y_weights(ft, t, False)
+        wyc[:, t * 256 : t * 256 + 256] = y_weights(ct, t, True)
+
+
+def final_kernel(wyref, wycref, fh, fl, fih, fil, fch, fcl, tp, out_hbm, out, sems):
+    wy, wyc = wyref[...], wycref[...]
 
     def stacked(h, l, index, first, size):
         rows = slice(first, first + size)
@@ -383,26 +388,36 @@
                 out[4 * q + r, 64 * b : 64 * b + 64, :] = res[:, 0:128] + even
                 out[4 * q + 2 + r, 64 * b : 64 * b + 64, :] = res[:, 128:256] + odd
 
+    def leave(q):
+        planes = pl.ds(4 * q, 4)
+        return pltpu.make_async_copy(out.at[planes], out_hbm.at[planes], sems.at[q])
+
     @pl.loop(2, 6)
     def _(q):
         slab(q, fih, fil, 2 * q - 4)
+        leave(q).start()
 
     @pl.loop(0, 2)
     def _(n):
         slab(n, fh, fl, 2 * n)
+        leave(n).start()
         slab(6 + n, fh, fl, 4 + 2 * n)
+        leave(6 + n).start()
+
+    for q in range(8):
+        leave(q).wait()
 
 
 def sds(*shape):
     return jax.ShapeDtypeStruct(shape, f32)
 
 
-def call(kernel, outs, n_smem, args, scratch=(), flops=0, nbytes=0, grant=12, alias=None):
+def call(kernel, outs, n_smem, args, scratch=(), flops=0, nbytes=0, grant=12, alias=None, space=VM):
     return pl.pallas_call(
         kernel,
         out_shape=outs,
         in_specs=[SM] * n_smem + [VM] * (len(args) - n_smem),
-        out_specs=jax.tree.map(lambda _: VM, outs),
+        out_specs=jax.tree.map(lambda _: space, outs),
         scratch_shapes=scratch,
         compiler_params=pltpu.CompilerParams(vmem_limit_bytes=grant * 1024 * 1024),
         input_output_aliases=alias or {},
@@ -494,6 +509,8 @@
     xr = shift(xlo, "gx", -1)
 
     k = call(matrix_kernel, sds(4, 8, 8, 8, 128), 0, (), flops=1 << 24, nbytes=1 << 20)
+    wide, tall = (jax.ShapeDtypeStruct(v, bf16) for v in ((64, 512), (512, 256)))
+    w, wc, wy, wyc = call(weights_kernel, (tall, tall, wide, wide), 2, (ft, ct), flops=1 << 24, nbytes=1 << 20)
     q3 = call(q3_kernel, sds(6, 8, 256), 0, (xlo, xl, xr))
     zlo, zhi = call(
         zstrip_kernel, (sds(NT, 8, 128), sds(NT, 8, 128)), 0, (g, yl, yh, xl, xr),
@@ -505,8 +522,8 @@
     qp = shift(q3, "gx", -3)
 
     e = call(
-        own_fine_kernel, sds(2, 32, 272, 128), 1,
-        (ft, charges, yl, yh, xl, xr), flops=5 << 30, nbytes=16 << 20,
+        own_fine_kernel, sds(2, 32, 272, 128), 0,
+        (w, charges, yl, yh, xl, xr), flops=5 << 30, nbytes=16 << 20,
     )
     p0 = call(pack_kernel, sds(8, 128), 0, (q3, qm, qp))
     pl1 = shift(p0, "gz", 1)
@@ -515,14 +532,14 @@
     quarter = jax.ShapeDtypeStruct((2, 8, 144, 256), bf16)
     fih, fil, pa, pc = call(
         inner_kernel, (half, half, sds(2, 2, 8, 272, 128), sds(2, 2, 8, 144, 128)), 2,
-        (ft, ct, e, g, yl, yh, xl, xr), scratch=[pltpu.VMEM((2, 16, 144, 128), f32)],
+        (ft, ct, wc, e, g, yl, yh, xl, xr), scratch=[pltpu.VMEM((2, 16, 144, 128), f32)],
         flops=5 << 30, nbytes=16 << 20,
     )
     p3 = call(p3_kernel, sds(3, 8, 128), 0, (p0, pl1, pr1))
     pm = shift(p3, "gz", 3)
     pp = shift(p3, "gz", -3)
     fh, fl, fch, fcl = call(
-        outer_kernel, (half, half, quarter, quarter), 2, (ft, ct, pa, pc, zl, zh, sl, sh),
+        outer_kernel, (half, half, quarter, quarter), 2, (ft, ct, w, wc, pa, pc, zl, zh, sl, sh),
         scratch=[
             pltpu.VMEM((2, 16, 272, 128), f32),
             pltpu.VMEM((2, 16, 144, 128), f32),
@@ -532,8 +549,9 @@
     )
     tp = call(top_kernel, sds(8, 128), 0, (k, p3, pm, pp))
     out = call(
-        final_kernel, sds(32, 256, 128), 2, (ft, ct, fh, fl, fih, fil, fch, fcl, tp),
-        flops=2 << 30, nbytes=16 << 20,
+        final_kernel, sds(32, 256, 128), 0, (wy, wyc, fh, fl, fih, fil, fch, fcl, tp),
+        scratch=[pltpu.VMEM((32, 256, 128), f32), pltpu.SemaphoreType.DMA((8,))],
+        flops=2 << 30, nbytes=16 << 20, grant=16, space=pl.BlockSpec(memory_space=pl.ANY),
     )
     return out
 

time: 98.1 us -> 95.6 us (0.975)
  Pallas kernels: 36.5 us -> 34.4 us
    pallas_call x13 -> x14, Pallas kernels: 36.5 us -> 34.4 us  [call(): pl.pallas_call(kernel, out_shape=outs, in_specs=[SM] * n_smem + [VM] * (l...]
  transfers between devices with their start and end apart: 15 -> 15, of which waited for: 6 -> 6; matrix products, arithmetic and copies ran while one was open for 0% -> 0% of each run, Pallas kernels for 22% -> 23%
where the time goes in v4:
time: 95.6 us; the launch traced here: 95.5 us
  Pallas kernels  34.4 us (36%)
  waiting for transfers between devices  33.5 us (35%)
  starting transfers between devices  25 us (26%)
  local copies, waits for them, and re-layouts  2.34 us (2%)
    pallas_call x14, Pallas kernels, call(): pl.pallas_call(kernel, out_shape=outs, in_specs=[SM] * n_smem + [VM] * (l...  34.4 us
    ppermute x15, waiting for transfers between devices, shift(): lax.ppermute(value, axis, [(i, (i + step) % count) for i in range(count)])  33.5 us
    ppermute x15, starting transfers between devices, shift(): lax.ppermute(value, axis, [(i, (i + step) % count) for i in range(count)])  25 us
    unnamed x10, local copies, waits for them, and re-layouts  2.2 us
  transfers between devices with their start and end apart: 15, of which 6 were waited for; matrix products, arithmetic and copies ran while one was open for 0% of the time, Pallas kernels for 23%

profile of v4, /device:TPU:32, one launch (start us, length us, event | category | flops | bytes accessed | tf_op | source)
XLA Modules:
  0.0 95.5 jit_solution(3628366840339180290)
XLA Ops:
  0.0 2.2 %copy-done = f32[32,256,128]{2,1,0:T(8,128)S(1)} copy-done((f32[32,256,128]{2,1,0:T(8,128)S(1)}, f32[32,256,128]{2,1,0:T(8,128)}, u32[]{:S(2)}) %copy-start) | copy-done | bytes 4194328
  2.7 1.6 %collective-permute-start = (f32[49,8,128]{2,1,0:T(8,128)S(1)}, f32[49,8,128]{2,1,0:T(8,128)S(1)}, u32[]{:S(2)}, u32[]{:S(2)}) collective-permute-start(f32[49,8,128]{2,1,0:T(8,128)S(1)} %get-tuple-element.31), channel_id=1, source_target_pairs={{0,8},{8,16},{16,24},{24,0},{1,9},{9,17},{17,25},{25,1},{2,10},{10... | collective-permute-start | bytes 602120 | tf_op jit(solution)/shard_map/ppermute | solution.py:22
  4.2 1.7 %collective-permute-start.1 = (f32[49,8,128]{2,1,0:T(8,128)S(1)}, f32[49,8,128]{2,1,0:T(8,128)S(1)}, u32[]{:S(2)}, u32[]{:S(2)}) collective-permute-start(f32[49,8,128]{2,1,0:T(8,128)S(1)} %get-tuple-element.32), channel_id=1, source_target_pairs={{0,24},{8,0},{16,8},{24,16},{1,25},{9,1},{17,9},{25,17},{2,26},{10... | collective-permute-start | bytes 602120 | tf_op jit(solution)/shard_map/ppermute | solution.py:22
  5.9 2.0 %collective-permute-start.2 = (f32[8,128]{1,0:T(8,128)S(1)}, f32[8,128]{1,0:T(8,128)S(1)}, u32[]{:S(2)}, u32[]{:S(2)}) collective-permute-start(f32[8,128]{1,0:T(8,128)S(1)} %get-tuple-element.36.q), channel_id=1, source_target_pairs={{0,16},{8,24},{16,0},{24,8},{1,17},{9,25},{17,1},{25,9},{2,18},{10... | collective-permute-start | bytes 12296 | tf_op jit(solution)/shard_map/ppermute | solution.py:22
  7.9 2.2 %shard_map.39 = (f32[45,8,256]{2,1,0:T(8,128)S(1)}, f32[45,8,256]{2,1,0:T(8,128)S(1)}) custom-call(f32[32,256,128]{2,1,0:T(8,128)S(1)} %copy-done, f32[16,128,128]{2,1,0:T(8,128)S(1)} %get-tuple-element.33.g), custom_call_target="tpu_custom_call" | custom-call | flops 134217728 | bytes 6291456 | tf_op jit(solution)/shard_map/pallas_call | solution.py:416
  10.1 1.8 %collective-permute-done.2.q2 = f32[8,128]{1,0:T(8,128)S(1)} collective-permute-done((f32[8,128]{1,0:T(8,128)S(1)}, f32[8,128]{1,0:T(8,128)S(1)}, u32[]{:S(2)}, u32[]{:S(2)}) %collective-permute-start.2) | collective-permute-done | bytes 4128 | tf_op jit(solution)/shard_map/ppermute | solution.py:22
  12.2 1.1 %collective-permute-start.4 = (f32[45,8,256]{2,1,0:T(8,128)S(1)}, f32[45,8,256]{2,1,0:T(8,128)S(1)}, u32[]{:S(2)}, u32[]{:S(2)}) collective-permute-start(f32[45,8,256]{2,1,0:T(8,128)S(1)} %get-tuple-element.38.xlo), channel_id=1, source_target_pairs={{0,224},{32,0},{64,32},{96,64},{128,96},{160,128},{192,160},{224,1... | collective-permute-start | bytes 1105928 | tf_op jit(solution)/shard_map/ppermute | solution.py:22
  13.3 5.0 %collective-permute-done.4.xr = f32[45,8,256]{2,1,0:T(8,128)S(1)} collective-permute-done((f32[45,8,256]{2,1,0:T(8,128)S(1)}, f32[45,8,256]{2,1,0:T(8,128)S(1)}, u32[]{:S(2)}, u32[]{:S(2)}) %collective-permute-start.4) | collective-permute-done | bytes 368672 | tf_op jit(solution)/shard_map/ppermute | solution.py:22
  18.3 3.1 %collective-permute-done.3.xl = f32[45,8,256]{2,1,0:T(8,128)S(1)} collective-permute-done((f32[45,8,256]{2,1,0:T(8,128)S(1)}, f32[45,8,256]{2,1,0:T(8,128)S(1)}, u32[]{:S(2)}, u32[]{:S(2)}) %collective-permute-start.3) | collective-permute-done | bytes 368672 | tf_op jit(solution)/shard_map/ppermute | solution.py:22
  21.8 1.5 %collective-permute-start.9 = (f32[6,8,256]{2,1,0:T(8,128)S(1)}, f32[6,8,256]{2,1,0:T(8,128)S(1)}, u32[]{:S(2)}, u32[]{:S(2)}) collective-permute-start(f32[6,8,256]{2,1,0:T(8,128)S(1)} %shard_map.46.q3), channel_id=1, source_target_pairs={{0,96},{32,128},{64,160},{96,192},{128,224},{160,0},{192,32},{224,... | collective-permute-start | bytes 147464 | tf_op jit(solution)/shard_map/ppermute | solution.py:22
  23.4 2.0 %collective-permute-start.5 = (f32[8,256,128]{2,1,0:T(8,128)S(1)}, f32[8,256,128]{2,1,0:T(8,128)S(1)}, u32[]{:S(2)}, u32[]{:S(2)}) collective-permute-start(f32[8,256,128]{2,1,0:T(8,128)S(1)} %get-tuple-element.50), channel_id=1, source_target_pairs={{0,1},{1,2},{2,3},{3,4},{4,5},{5,6},{6,7},{7,0},{8,9},{9,10},{10,1... | collective-permute-start | bytes 3145736 | tf_op jit(solution)/shard_map/ppermute | solution.py:22
  25.5 1.3 %collective-permute-done.9.qm = f32[6,8,256]{2,1,0:T(8,128)S(1)} collective-permute-done((f32[6,8,256]{2,1,0:T(8,128)S(1)}, f32[6,8,256]{2,1,0:T(8,128)S(1)}, u32[]{:S(2)}, u32[]{:S(2)}) %collective-permute-start.9) | collective-permute-done | bytes 49184 | tf_op jit(solution)/shard_map/ppermute | solution.py:22
  27.0 2.0 %collective-permute-start.11 = (f32[8,128]{1,0:T(8,128)S(1)}, f32[8,128]{1,0:T(8,128)S(1)}, u32[]{:S(2)}, u32[]{:S(2)}) collective-permute-start(f32[8,128]{1,0:T(8,128)S(1)} %shard_map.47.p0), channel_id=1, source_target_pairs={{0,1},{1,2},{2,3},{3,4},{4,5},{5,6},{6,7},{7,0},{8,9},{9,10},{10,1... | collective-permute-start | bytes 12296 | tf_op jit(solution)/shard_map/ppermute | solution.py:22
  30.3 1.3 %shard_map.37 = (bf16[512,256]{1,0:T(8,128)(2,1)S(1)}, bf16[512,256]{1,0:T(8,128)(2,1)S(1)}, bf16[64,512]{1,0:T(8,128)(2,1)S(1)}, bf16[64,512]{1,0:T(8,128)(2,1)S(1)}) custom-call(f32[2,3,17]{2,1,0:T(4,128)S(1)} %copy.6.ft, f32[2,3,17]{2,1,0:T(4,128)S(1)} %copy.7.ct), custom_call_target="tpu_custom_call" | custom-call | flops 16777216 | bytes 1048576 | tf_op jit(solution)/shard_map/pallas_call | solution.py:416
  31.7 1.2 %collective-permute-start.7 = (f32[148,8,128]{2,1,0:T(8,128)S(1)}, f32[148,8,128]{2,1,0:T(8,128)S(1)}, u32[]{:S(2)}, u32[]{:S(2)}) collective-permute-start(f32[148,8,128]{2,1,0:T(8,128)S(1)} %get-tuple-element.41), channel_id=1, source_target_pairs={{0,1},{1,2},{2,3},{3,4},{4,5},{5,6},{6,7},{7,0},{8,9},{9,10},{10,1... | collective-permute-start | bytes 1818632 | tf_op jit(solution)/shard_map/ppermute | solution.py:22
  32.9 16.7 %collective-permute-done.11.sl = f32[8,128]{1,0:T(8,128)S(1)} collective-permute-done((f32[8,128]{1,0:T(8,128)S(1)}, f32[8,128]{1,0:T(8,128)S(1)}, u32[]{:S(2)}, u32[]{:S(2)}) %collective-permute-start.11) | collective-permute-done | bytes 4128 | tf_op jit(solution)/shard_map/ppermute | solution.py:22
  49.6 3.9 %collective-permute-start.8 = (f32[148,8,128]{2,1,0:T(8,128)S(1)}, f32[148,8,128]{2,1,0:T(8,128)S(1)}, u32[]{:S(2)}, u32[]{:S(2)}) collective-permute-start(f32[148,8,128]{2,1,0:T(8,128)S(1)} %get-tuple-element.42), channel_id=1, source_target_pairs={{0,7},{1,0},{2,1},{3,2},{4,3},{5,4},{6,5},{7,6},{8,15},{9,8},{10,9... | collective-permute-start | bytes 1818632 | tf_op jit(solution)/shard_map/ppermute | solution.py:22
  53.6 3.4 %collective-permute-start.13 = (f32[3,8,128]{2,1,0:T(8,128)S(1)}, f32[3,8,128]{2,1,0:T(8,128)S(1)}, u32[]{:S(2)}, u32[]{:S(2)}) collective-permute-start(f32[3,8,128]{2,1,0:T(8,128)S(1)} %shard_map.48.p3), channel_id=1, source_target_pairs={{0,3},{1,4},{2,5},{3,6},{4,7},{5,0},{6,1},{7,2},{8,11},{9,12},{10,... | collective-permute-start | bytes 36872 | tf_op jit(solution)/shard_map/ppermute | solution.py:22
  57.0 4.0 %shard_map.41.e = f32[2,32,272,128]{3,2,1,0:T(8,128)S(1)} custom-call(bf16[512,256]{1,0:T(8,128)(2,1)S(1)} %get-tuple-element.29.wref, f32[32,256,128]{2,1,0:T(8,128)S(1)} %copy-done.1, f32[49,8,128]{2,1,0:T(8,128)S(1)} %collective-permute-done.yl, f32[49,8,128]{2,1,0:T(8,128)S(1)} %collective-permute-done.1.yh, ...), custom_call_target="tpu_custom_call" | custom-call | flops 5368709120 | bytes 16777216 | tf_op jit(solution)/shard_map/pallas_call | solution.py:416
  61.0 5.5 %collective-permute-done.13.pm = f32[3,8,128]{2,1,0:T(8,128)S(1)} collective-permute-done((f32[3,8,128]{2,1,0:T(8,128)S(1)}, f32[3,8,128]{2,1,0:T(8,128)S(1)}, u32[]{:S(2)}, u32[]{:S(2)}) %collective-permute-start.13) | collective-permute-done | bytes 12320 | tf_op jit(solution)/shard_map/ppermute | solution.py:22
  66.4 3.4 %collective-permute-start.14 = (f32[3,8,128]{2,1,0:T(8,128)S(1)}, f32[3,8,128]{2,1,0:T(8,128)S(1)}, u32[]{:S(2)}, u32[]{:S(2)}) collective-permute-start(f32[3,8,128]{2,1,0:T(8,128)S(1)} %shard_map.48.p3), channel_id=1, source_target_pairs={{0,5},{1,6},{2,7},{3,0},{4,1},{5,2},{6,3},{7,4},{8,13},{9,14},{10,... | collective-permute-start | bytes 36872 | tf_op jit(solution)/shard_map/ppermute | solution.py:22
  69.8 13.4 %shard_map.42 = (bf16[2,8,272,256]{3,2,1,0:T(8,128)(2,1)S(1)}, bf16[2,8,272,256]{3,2,1,0:T(8,128)(2,1)S(1)}, f32[2,2,8,272,128]{4,3,2,1,0:T(8,128)S(1)}, f32[2,2,8,144,128]{4,3,2,1,0:T(8,128)S(1)}) custom-call(f32[2,3,17]{2,1,0:T(4,128)S(1)} %copy.6.ft, f32[2,3,17]{2,1,0:T(4,128)S(1)} %copy.7.ct, bf16[512,256]{1,0:T(8,128)(2,1)S(1)} %get-tuple-element.30.wcref, ...), custom_call_target="tpu_custom_call" | custom-call | flops 5368709120 | bytes 16777216 | tf_op jit(solution)/shard_map/pallas_call | solution.py:416
  83.5 6.8 %shard_map.44 = (bf16[2,8,272,256]{3,2,1,0:T(8,128)(2,1)S(1)}, bf16[2,8,272,256]{3,2,1,0:T(8,128)(2,1)S(1)}, bf16[2,8,144,256]{3,2,1,0:T(8,128)(2,1)S(1)}, bf16[2,8,144,256]{3,2,1,0:T(8,128)(2,1)S(1)}) custom-call(f32[2,3,17]{2,1,0:T(4,128)S(1)} %copy.6.ft, f32[2,3,17]{2,1,0:T(4,128)S(1)} %copy.7.ct, bf16[512,256]{1,0:T(8,128)(2,1)S(1)} %get-tuple-element.29.wref, ...), custom_call_target="tpu_custom_call" | custom-call | flops 4294967296 | bytes 16777216 | tf_op jit(solution)/shard_map/pallas_call | solution.py:416
  90.3 5.1 %shard_map.50 = f32[32,256,128]{2,1,0:T(8,128)} custom-call(bf16[64,512]{1,0:T(8,128)(2,1)S(1)} %get-tuple-element.27.wyref, bf16[64,512]{1,0:T(8,128)(2,1)S(1)} %get-tuple-element.28.wycref, bf16[2,8,272,256]{3,2,1,0:T(8,128)(2,1)S(1)} %get-tuple-element.43.fh, bf16[2,8,272,256]{3,2,1,0:T(8,128)(2,1)S(1)} %get-tuple-element.44.fl, ...), custom_call_target="tpu_custom_call" | custom-call | flops 2147483648 | bytes 16777216 | tf_op jit(solution)/shard_map/pallas_call | solution.py:416
  (31 shorter events, 3.1 us)
Async XLA Ops:
  0.0 2.2 %copy-start = (f32[32,256,128]{2,1,0:T(8,128)S(1)}, f32[32,256,128]{2,1,0:T(8,128)}, u32[]{:S(2)}) copy-start(f32[32,256,128]{2,1,0:T(8,128)} %d.5) | copy-start | bytes 12582916
  2.7 9.3 %collective-permute-start = (f32[49,8,128]{2,1,0:T(8,128)S(1)}, f32[49,8,128]{2,1,0:T(8,128)S(1)}, u32[]{:S(2)}, u32[]{:S(2)}) collective-permute-start(f32[49,8,128]{2,1,0:T(8,128)S(1)} %get-tuple-element.31), channel_id=1, source_target_pairs={{0,8},{8,16},{16,24},{24,0},{1,9},{9,17},{17,25},{25,1},{2,10},{10... | collective-permute-start | bytes 602120 | tf_op jit(solution)/shard_map/ppermute | solution.py:22
  4.2 7.7 %collective-permute-start.1 = (f32[49,8,128]{2,1,0:T(8,128)S(1)}, f32[49,8,128]{2,1,0:T(8,128)S(1)}, u32[]{:S(2)}, u32[]{:S(2)}) collective-permute-start(f32[49,8,128]{2,1,0:T(8,128)S(1)} %get-tuple-element.32), channel_id=1, source_target_pairs={{0,24},{8,0},{16,8},{24,16},{1,25},{9,1},{17,9},{25,17},{2,26},{10... | collective-permute-start | bytes 602120 | tf_op jit(solution)/shard_map/ppermute | solution.py:22
  5.9 6.0 %collective-permute-start.2 = (f32[8,128]{1,0:T(8,128)S(1)}, f32[8,128]{1,0:T(8,128)S(1)}, u32[]{:S(2)}, u32[]{:S(2)}) collective-permute-start(f32[8,128]{1,0:T(8,128)S(1)} %get-tuple-element.36.q), channel_id=1, source_target_pairs={{0,16},{8,24},{16,0},{24,8},{1,17},{9,25},{17,1},{25,9},{2,18},{10... | collective-permute-start | bytes 12296 | tf_op jit(solution)/shard_map/ppermute | solution.py:22
  7.9 15.4 %copy-start.1 = (f32[32,256,128]{2,1,0:T(8,128)S(1)}, f32[32,256,128]{2,1,0:T(8,128)}, u32[]{:S(2)}) copy-start(f32[32,256,128]{2,1,0:T(8,128)} %d.5) | copy-start | bytes 12582916
  12.2 6.1 %collective-permute-start.4 = (f32[45,8,256]{2,1,0:T(8,128)S(1)}, f32[45,8,256]{2,1,0:T(8,128)S(1)}, u32[]{:S(2)}, u32[]{:S(2)}) collective-permute-start(f32[45,8,256]{2,1,0:T(8,128)S(1)} %get-tuple-element.38.xlo), channel_id=1, source_target_pairs={{0,224},{32,0},{64,32},{96,64},{128,96},{160,128},{192,160},{224,1... | collective-permute-start | bytes 1105928 | tf_op jit(solution)/shard_map/ppermute | solution.py:22
  13.3 8.1 %collective-permute-start.3 = (f32[45,8,256]{2,1,0:T(8,128)S(1)}, f32[45,8,256]{2,1,0:T(8,128)S(1)}, u32[]{:S(2)}, u32[]{:S(2)}) collective-permute-start(f32[45,8,256]{2,1,0:T(8,128)S(1)} %get-tuple-element.37), channel_id=1, source_target_pairs={{0,32},{32,64},{64,96},{96,128},{128,160},{160,192},{192,224},{224... | collective-permute-start | bytes 1105928 | tf_op jit(solution)/shard_map/ppermute | solution.py:22
  21.5 8.4 %copy-start.2 = (f32[2,3,17]{2,0,1:T(2,128)S(1)}, f32[2,3,17]{2,0,1:T(2,128)}, u32[]{:S(2)}) copy-start(f32[2,3,17]{2,0,1:T(2,128)} %param.4) | copy-start | bytes 1228
  21.5 8.4 %copy-start.3 = (f32[2,3,17]{2,0,1:T(2,128)S(1)}, f32[2,3,17]{2,0,1:T(2,128)}, u32[]{:S(2)}) copy-start(f32[2,3,17]{2,0,1:T(2,128)} %param.5) | copy-start | bytes 1228
  21.5 4.1 %collective-permute-start.10 = (f32[6,8,256]{2,1,0:T(8,128)S(1)}, f32[6,8,256]{2,1,0:T(8,128)S(1)}, u32[]{:S(2)}, u32[]{:S(2)}) collective-permute-start(f32[6,8,256]{2,1,0:T(8,128)S(1)} %shard_map.46.q3), channel_id=1, source_target_pairs={{0,160},{32,192},{64,224},{96,0},{128,32},{160,64},{192,96},{224,1... | collective-permute-start | bytes 147464 | tf_op jit(solution)/shard_map/ppermute | solution.py:22
  21.8 5.0 %collective-permute-start.9 = (f32[6,8,256]{2,1,0:T(8,128)S(1)}, f32[6,8,256]{2,1,0:T(8,128)S(1)}, u32[]{:S(2)}, u32[]{:S(2)}) collective-permute-start(f32[6,8,256]{2,1,0:T(8,128)S(1)} %shard_map.46.q3), channel_id=1, source_target_pairs={{0,96},{32,128},{64,160},{96,192},{128,224},{160,0},{192,32},{224,... | collective-permute-start | bytes 147464 | tf_op jit(solution)/shard_map/ppermute | solution.py:22
  23.4 60.0 %collective-permute-start.5 = (f32[8,256,128]{2,1,0:T(8,128)S(1)}, f32[8,256,128]{2,1,0:T(8,128)S(1)}, u32[]{:S(2)}, u32[]{:S(2)}) collective-permute-start(f32[8,256,128]{2,1,0:T(8,128)S(1)} %get-tuple-element.50), channel_id=1, source_target_pairs={{0,1},{1,2},{2,3},{3,4},{4,5},{5,6},{6,7},{7,0},{8,9},{9,10},{10,1... | collective-permute-start | bytes 3145736 | tf_op jit(solution)/shard_map/ppermute | solution.py:22
  25.4 58.0 %collective-permute-start.6 = (f32[8,256,128]{2,1,0:T(8,128)S(1)}, f32[8,256,128]{2,1,0:T(8,128)S(1)}, u32[]{:S(2)}, u32[]{:S(2)}) collective-permute-start(f32[8,256,128]{2,1,0:T(8,128)S(1)} %get-tuple-element.49), channel_id=1, source_target_pairs={{0,7},{1,0},{2,1},{3,2},{4,3},{5,4},{6,5},{7,6},{8,15},{9,8},{10,9... | collective-permute-start | bytes 3145736 | tf_op jit(solution)/shard_map/ppermute | solution.py:22
  27.0 22.7 %collective-permute-start.11 = (f32[8,128]{1,0:T(8,128)S(1)}, f32[8,128]{1,0:T(8,128)S(1)}, u32[]{:S(2)}, u32[]{:S(2)}) collective-permute-start(f32[8,128]{1,0:T(8,128)S(1)} %shard_map.47.p0), channel_id=1, source_target_pairs={{0,1},{1,2},{2,3},{3,4},{4,5},{5,6},{6,7},{7,0},{8,9},{9,10},{10,1... | collective-permute-start | bytes 12296 | tf_op jit(solution)/shard_map/ppermute | solution.py:22
  28.9 24.6 %collective-permute-start.12 = (f32[8,128]{1,0:T(8,128)S(1)}, f32[8,128]{1,0:T(8,128)S(1)}, u32[]{:S(2)}, u32[]{:S(2)}) collective-permute-start(f32[8,128]{1,0:T(8,128)S(1)} %shard_map.47.p0), channel_id=1, source_target_pairs={{0,7},{1,0},{2,1},{3,2},{4,3},{5,4},{6,5},{7,6},{8,15},{9,8},{10,9... | collective-permute-start | bytes 12296 | tf_op jit(solution)/shard_map/ppermute | solution.py:22
  31.7 51.7 %collective-permute-start.7 = (f32[148,8,128]{2,1,0:T(8,128)S(1)}, f32[148,8,128]{2,1,0:T(8,128)S(1)}, u32[]{:S(2)}, u32[]{:S(2)}) collective-permute-start(f32[148,8,128]{2,1,0:T(8,128)S(1)} %get-tuple-element.41), channel_id=1, source_target_pairs={{0,1},{1,2},{2,3},{3,4},{4,5},{5,6},{6,7},{7,0},{8,9},{9,10},{10,1... | collective-permute-start | bytes 1818632 | tf_op jit(solution)/shard_map/ppermute | solution.py:22
  49.6 33.8 %collective-permute-start.8 = (f32[148,8,128]{2,1,0:T(8,128)S(1)}, f32[148,8,128]{2,1,0:T(8,128)S(1)}, u32[]{:S(2)}, u32[]{:S(2)}) collective-permute-start(f32[148,8,128]{2,1,0:T(8,128)S(1)} %get-tuple-element.42), channel_id=1, source_target_pairs={{0,7},{1,0},{2,1},{3,2},{4,3},{5,4},{6,5},{7,6},{8,15},{9,8},{10,9... | collective-permute-start | bytes 1818632 | tf_op jit(solution)/shard_map/ppermute | solution.py:22
  53.6 12.9 %collective-permute-start.13 = (f32[3,8,128]{2,1,0:T(8,128)S(1)}, f32[3,8,128]{2,1,0:T(8,128)S(1)}, u32[]{:S(2)}, u32[]{:S(2)}) collective-permute-start(f32[3,8,128]{2,1,0:T(8,128)S(1)} %shard_map.48.p3), channel_id=1, source_target_pairs={{0,3},{1,4},{2,5},{3,6},{4,7},{5,0},{6,1},{7,2},{8,11},{9,12},{10,... | collective-permute-start | bytes 36872 | tf_op jit(solution)/shard_map/ppermute | solution.py:22
  66.4 16.8 %collective-permute-start.14 = (f32[3,8,128]{2,1,0:T(8,128)S(1)}, f32[3,8,128]{2,1,0:T(8,128)S(1)}, u32[]{:S(2)}, u32[]{:S(2)}) collective-permute-start(f32[3,8,128]{2,1,0:T(8,128)S(1)} %shard_map.48.p3), channel_id=1, source_target_pairs={{0,5},{1,6},{2,7},{3,0},{4,1},{5,2},{6,3},{7,4},{8,13},{9,14},{10,... | collective-permute-start | bytes 36872 | tf_op jit(solution)/shard_map/ppermute | solution.py:22

commit v5 on v4

--- a/solution.py
+++ b/solution.py
@@ -8,7 +8,7 @@
 
 f32 = jnp.float32
 bf16 = jnp.bfloat16
-NB = 45
+NB = 40
 NT = 148
 R = 8
 TAPS = 17
@@ -133,19 +133,19 @@
         put(xlo, xhi, 8 * k, [d[8 * k + p] for p in range(8)], False)
     for k in range(2):
         sources = [g[8 * k + 2 * p : 8 * k + 2 * p + 2].reshape(256, 128) for p in range(4)]
-        put(xlo, xhi, 34 + 4 * k, sources, True)
-
-
-def strip_y_kernel(xlo_in, xhi_in, yl, yh, q, q2, xlo, xhi):
-    put(xlo, xhi, 32, [yl[0:32].reshape(256, 128), yh[0:32].reshape(256, 128)], False)
+        put(xlo, xhi, 32 + 4 * k, sources, True)
+
+
+def strip_y_kernel(yl, yh, q, q2, xlo, xhi):
+    put(xlo, xhi, 0, [yl[0:32].reshape(256, 128), yh[0:32].reshape(256, 128)], False)
     coarse = jnp.concatenate([yl[32:48].reshape(128, 128), yh[32:48].reshape(128, 128)], axis=0)
-    put(xlo, xhi, 42, [coarse], True)
+    put(xlo, xhi, 2, [coarse], True)
     sides = jnp.concatenate([yl[48], yh[48]], axis=1)
     rest = jnp.concatenate([q[...], q2[...]], axis=1)
-    xlo[43] = sides
-    xlo[44] = rest
-    xhi[43] = sides
-    xhi[44] = rest
+    xlo[3] = sides
+    xlo[4] = rest
+    xhi[3] = sides
+    xhi[4] = rest
 
 
 def pack_kernel(q3, qm, qp, own):
@@ -160,7 +160,7 @@
     )
 
 
-def zstrip_kernel(g, yl, yh, xl, xr, zlo, zhi):
+def zstrip_kernel(g, yl, yh, xl, xr, cl, cr, zlo, zhi):
     for out, p0, far in ((zlo, 0, 4), (zhi, 24, 8)):
         for p in range(8):
             for s, src in ((0, xl), (1, xr)):
@@ -168,8 +168,8 @@
                     out[p * 4 + s * 2 + half] = src[p0 + p, :, half * 128 : half * 128 + 128]
         out[32:40] = yl[p0 : p0 + 8]
         out[40:48] = yh[p0 : p0 + 8]
-        for s, src in ((0, xl), (1, xr)):
-            a, b = src[32], src[33]
+        for s, src in ((0, cl), (1, cr)):
+            a, b = src[0], src[1]
             out[48 + s] = jnp.concatenate([a[:, p0 * 8 : p0 * 8 + 64], b[:, p0 * 8 : p0 * 8 + 64]], axis=1)
         for i in range(4):
             out[50 + 16 * i : 66 + 16 * i] = g[far + i].reshape(16, 8, 128)
@@ -179,47 +179,48 @@
         for b in range(4):
             for s, src in ((0, xl), (1, xr)):
                 for half in range(2):
-                    out[130 + b * 4 + s * 2 + half] = src[34 + c0 // 2 + b, :, half * 128 : half * 128 + 128]
-        for s, src in ((0, xl), (1, xr)):
-            a = src[42]
+                    out[130 + b * 4 + s * 2 + half] = src[32 + c0 // 2 + b, :, half * 128 : half * 128 + 128]
+        for s, src in ((0, cl), (1, cr)):
+            a = src[2]
             out[146 + s] = jnp.concatenate(
                 [a[:, c0 * 8 : c0 * 8 + 64], a[:, 128 + c0 * 8 : 128 + c0 * 8 + 64]], axis=1
             )
 
 
-def own_fine_kernel(wref, d, yl, yh, xl, xr, e):
+def own_fine_kernel(wref, d, xl, xr, e):
     w = wref[...]
 
+    @pl.loop(0, 32, unroll=4)
+    def _(z):
+        r = x_block(d[z], jnp.concatenate([xl[z], xr[z]], axis=0), w)
+        for t in range(2):
+            e[t, z, 8:264, :] = r[:, t * 128 : t * 128 + 128]
+
+
+def own_y_kernel(e_in, wref, yl, yh, cl, cr, e):
+    w = wref[...]
+    for i, src, row in ((0, yl, 0), (1, yh, 264)):
+        strip = jnp.concatenate([cl[i], cr[i]], axis=0)
+        r = x_block(src[0:32].reshape(256, 128), strip, w).reshape(32, 8, 256)
+        for t in range(2):
+            e[t, :, row : row + 8, :] = r[:, :, t * 128 : t * 128 + 128]
+
+
+def own_coarse(wcref, g, yl, yh, xl, xr, cl, cr, ec):
     def strip(i):
         return jnp.concatenate([xl[i], xr[i]], axis=0)
 
-    @pl.loop(0, 32, unroll=4)
-    def _(z):
-        r = x_block(d[z], strip(z), w)
-        for t in range(2):
-            e[t, z, 8:264, :] = r[:, t * 128 : t * 128 + 128]
-
-    for i, src, row in ((32, yl, 0), (33, yh, 264)):
-        r = x_block(src[0:32].reshape(256, 128), strip(i), w).reshape(32, 8, 256)
-        for t in range(2):
-            e[t, :, row : row + 8, :] = r[:, :, t * 128 : t * 128 + 128]
-
-
-def own_coarse(wcref, g, yl, yh, xl, xr, ec):
-    def strip(i):
-        return jnp.concatenate([xl[i], xr[i]], axis=0)
-
     wc = wcref[...]
 
     @pl.loop(0, 8, unroll=4)
     def _(b):
-        r = x_block(g[pl.ds(2 * b, 2)].reshape(256, 128), strip(34 + b), wc).reshape(2, 128, 256)
+        r = x_block(g[pl.ds(2 * b, 2)].reshape(256, 128), strip(32 + b), wc).reshape(2, 128, 256)
         for t in range(2):
             ec[t, pl.ds(2 * b, 2), 8:136, :] = r[:, :, t * 128 : t * 128 + 128]
 
     r = x_block(
         jnp.concatenate([yl[32:48].reshape(128, 128), yh[32:48].reshape(128, 128)], axis=0),
-        strip(42), wc,
+        jnp.concatenate([cl[2], cr[2]], axis=0), wc,
     ).reshape(2, 16, 8, 256)
     for t in range(2):
         ec[t, :, 0:8, :] = r[0, :, :, t * 128 : t * 128 + 128]
@@ -247,9 +248,7 @@
         lo_ref[t, first + 2 * q + r, rows, l * 128 : l * 128 + 128] = lo
 
 
-def inner_kernel(ft, ct, wcref, e, g, yl, yh, xl, xr, fih, fil, pa, pc, ec):
-    own_coarse(wcref, g, yl, yh, xl, xr, ec)
-
+def inner_kernel(ft, e, fih, fil):
     @pl.loop(0, 17)
     def _(y):
         rows = pl.ds(pl.multiple_of(y * 16, 16), 16)
@@ -260,6 +259,15 @@
                     return e[t, i + 8 * n, rows, :]
 
                 put_pair(fih, fil, t, 4 * n, rows, z_group(plane, ft, t, 0, 24))
+
+
+def partial_kernel(ft, ct, wcref, e, g, yl, yh, xl, xr, cl, cr, pa, pc, ec):
+    own_coarse(wcref, g, yl, yh, xl, xr, cl, cr, ec)
+
+    @pl.loop(0, 17)
+    def _(y):
+        rows = pl.ds(pl.multiple_of(y * 16, 16), 16)
+        for t in range(2):
             for o, v in enumerate(z_group(lambda i, t=t: e[t, i - 8, rows, :], ft, t, 8, 24)):
                 pa[t, 0, o, rows, :] = v
             for o, v in enumerate(z_group(lambda i, t=t: e[t, i + 16, rows, :], ft, t, 0, 16)):
@@ -473,9 +481,9 @@
 
 
 def q3_kernel(xlo, xl, xr, q3):
-    q3[0:2] = xlo[43:45]
-    q3[2:4] = xl[43:45]
-    q3[4:6] = xr[43:45]
+    q3[0:2] = xlo[3:5]
+    q3[2:4] = xl[3:5]
+    q3[4:6] = xr[3:5]
 
 
 def p3_kernel(p0, sl, sh, p3):
@@ -501,19 +509,20 @@
         strip_kernel, (sds(NB, 8, 256), sds(NB, 8, 256)), 0, (charges, g),
         flops=1 << 27, nbytes=6 << 20,
     )
-    xlo, xhi = call(
-        strip_y_kernel, (sds(NB, 8, 256), sds(NB, 8, 256)), 0, (xlo, xhi, yl, yh, q, q2),
-        flops=1 << 24, nbytes=1 << 20, alias={0: 0, 1: 1},
-    )
     xl = shift(xhi, "gx", 1)
     xr = shift(xlo, "gx", -1)
-
+    clo, chi = call(
+        strip_y_kernel, (sds(5, 8, 256), sds(5, 8, 256)), 0, (yl, yh, q, q2),
+        flops=1 << 24, nbytes=1 << 20,
+    )
+    cl = shift(chi, "gx", 1)
+    cr = shift(clo, "gx", -1)
     k = call(matrix_kernel, sds(4, 8, 8, 8, 128), 0, (), flops=1 << 24, nbytes=1 << 20)
     wide, tall = (jax.ShapeDtypeStruct(v, bf16) for v in ((64, 512), (512, 256)))
     w, wc, wy, wyc = call(weights_kernel, (tall, tall, wide, wide), 2, (ft, ct), flops=1 << 24, nbytes=1 << 20)
-    q3 = call(q3_kernel, sds(6, 8, 256), 0, (xlo, xl, xr))
+    q3 = call(q3_kernel, sds(6, 8, 256), 0, (clo, cl, cr))
     zlo, zhi = call(
-        zstrip_kernel, (sds(NT, 8, 128), sds(NT, 8, 128)), 0, (g, yl, yh, xl, xr),
+        zstrip_kernel, (sds(NT, 8, 128), sds(NT, 8, 128)), 0, (g, yl, yh, xl, xr, cl, cr),
         flops=1 << 20, nbytes=4 << 20,
     )
     sl = shift(zhi, "gz", 1)
@@ -523,17 +532,22 @@
 
     e = call(
         own_fine_kernel, sds(2, 32, 272, 128), 0,
-        (w, charges, yl, yh, xl, xr), flops=5 << 30, nbytes=16 << 20,
-    )
+        (w, charges, xl, xr), flops=5 << 30, nbytes=16 << 20,
+    )
+    e = call(
+        own_y_kernel, sds(2, 32, 272, 128), 0,
+        (e, w, yl, yh, cl, cr), flops=1 << 28, nbytes=1 << 20, alias={0: 0},
+    )
+    half = jax.ShapeDtypeStruct((2, 8, 272, 256), bf16)
+    quarter = jax.ShapeDtypeStruct((2, 8, 144, 256), bf16)
+    fih, fil = call(inner_kernel, (half, half), 1, (ft, e), flops=3 << 30, nbytes=16 << 20)
     p0 = call(pack_kernel, sds(8, 128), 0, (q3, qm, qp))
     pl1 = shift(p0, "gz", 1)
     pr1 = shift(p0, "gz", -1)
-    half = jax.ShapeDtypeStruct((2, 8, 272, 256), bf16)
-    quarter = jax.ShapeDtypeStruct((2, 8, 144, 256), bf16)
-    fih, fil, pa, pc = call(
-        inner_kernel, (half, half, sds(2, 2, 8, 272, 128), sds(2, 2, 8, 144, 128)), 2,
-        (ft, ct, wc, e, g, yl, yh, xl, xr), scratch=[pltpu.VMEM((2, 16, 144, 128), f32)],
-        flops=5 << 30, nbytes=16 << 20,
+    pa, pc = call(
+        partial_kernel, (sds(2, 2, 8, 272, 128), sds(2, 2, 8, 144, 128)), 2,
+        (ft, ct, wc, e, g, yl, yh, xl, xr, cl, cr), scratch=[pltpu.VMEM((2, 16, 144, 128), f32)],
+        flops=3 << 30, nbytes=16 << 20,
     )
     p3 = call(p3_kernel, sds(3, 8, 128), 0, (p0, pl1, pr1))
     pm = shift(p3, "gz", 3)

time: 95.6 us -> 90.9 us (0.951)
  the two profiles are of different devices: /device:TPU:32 before, /device:TPU:6 now
where the time goes in v5:
time: 90.9 us; the launch traced here: 90.8 us
  Pallas kernels  34.8 us (38%)
  starting transfers between devices  27.6 us (30%)
  waiting for transfers between devices  25.8 us (28%)
  local copies, waits for them, and re-layouts  2.38 us (3%)
    pallas_call x16, Pallas kernels, call(): pl.pallas_call(kernel, out_shape=outs, in_specs=[SM] * n_smem + [VM] * (l...  34.8 us
    ppermute x17, starting transfers between devices, shift(): lax.ppermute(value, axis, [(i, (i + step) % count) for i in range(count)])  27.6 us
    ppermute x17, waiting for transfers between devices, shift(): lax.ppermute(value, axis, [(i, (i + step) % count) for i in range(count)])  25.8 us
    unnamed x10, local copies, waits for them, and re-layouts  2.21 us
  transfers between devices with their start and end apart: 17, of which 5 were waited for; matrix products, arithmetic and copies ran while one was open for 0% of the time, Pallas kernels for 24%

profile of v5, /device:TPU:6, one launch (start us, length us, event | category | flops | bytes accessed | tf_op | source)
XLA Modules:
  0.0 90.8 jit_solution(6506438792912683457)
XLA Ops:
  0.0 2.2 %copy-done = f32[32,256,128]{2,1,0:T(8,128)S(1)} copy-done((f32[32,256,128]{2,1,0:T(8,128)S(1)}, f32[32,256,128]{2,1,0:T(8,128)}, u32[]{:S(2)}) %copy-start) | copy-done | bytes 4194328
  2.7 1.6 %collective-permute-start.2 = (f32[49,8,128]{2,1,0:T(8,128)S(1)}, f32[49,8,128]{2,1,0:T(8,128)S(1)}, u32[]{:S(2)}, u32[]{:S(2)}) collective-permute-start(f32[49,8,128]{2,1,0:T(8,128)S(1)} %get-tuple-element.34), channel_id=1, source_target_pairs={{0,8},{8,16},{16,24},{24,0},{1,9},{9,17},{17,25},{25,1},{2,10},{10... | collective-permute-start | bytes 602120 | tf_op jit(solution)/shard_map/ppermute | solution.py:22
  4.2 1.7 %collective-permute-start.3 = (f32[49,8,128]{2,1,0:T(8,128)S(1)}, f32[49,8,128]{2,1,0:T(8,128)S(1)}, u32[]{:S(2)}, u32[]{:S(2)}) collective-permute-start(f32[49,8,128]{2,1,0:T(8,128)S(1)} %get-tuple-element.35), channel_id=1, source_target_pairs={{0,24},{8,0},{16,8},{24,16},{1,25},{9,1},{17,9},{25,17},{2,26},{10... | collective-permute-start | bytes 602120 | tf_op jit(solution)/shard_map/ppermute | solution.py:22
  5.9 2.0 %collective-permute-start.4 = (f32[8,128]{1,0:T(8,128)S(1)}, f32[8,128]{1,0:T(8,128)S(1)}, u32[]{:S(2)}, u32[]{:S(2)}) collective-permute-start(f32[8,128]{1,0:T(8,128)S(1)} %get-tuple-element.36.q), channel_id=1, source_target_pairs={{0,16},{8,24},{16,0},{24,8},{1,17},{9,25},{17,1},{25,9},{2,18},{10... | collective-permute-start | bytes 12296 | tf_op jit(solution)/shard_map/ppermute | solution.py:22
  7.9 4.0 %collective-permute-done.4.q2 = f32[8,128]{1,0:T(8,128)S(1)} collective-permute-done((f32[8,128]{1,0:T(8,128)S(1)}, f32[8,128]{1,0:T(8,128)S(1)}, u32[]{:S(2)}, u32[]{:S(2)}) %collective-permute-start.4) | collective-permute-done | bytes 4128 | tf_op jit(solution)/shard_map/ppermute | solution.py:22
  12.3 1.7 %collective-permute-start.6 = (f32[5,8,256]{2,1,0:T(8,128)S(1)}, f32[5,8,256]{2,1,0:T(8,128)S(1)}, u32[]{:S(2)}, u32[]{:S(2)}) collective-permute-start(f32[5,8,256]{2,1,0:T(8,128)S(1)} %get-tuple-element.38.xlo), channel_id=1, source_target_pairs={{0,224},{32,0},{64,32},{96,64},{128,96},{160,128},{192,160},{224,1... | collective-permute-start | bytes 122888 | tf_op jit(solution)/shard_map/ppermute | solution.py:22
  14.0 1.7 %collective-permute-done.5.cl.xl = f32[5,8,256]{2,1,0:T(8,128)S(1)} collective-permute-done((f32[5,8,256]{2,1,0:T(8,128)S(1)}, f32[5,8,256]{2,1,0:T(8,128)S(1)}, u32[]{:S(2)}, u32[]{:S(2)}) %collective-permute-start.5) | collective-permute-done | bytes 40992 | tf_op jit(solution)/shard_map/ppermute | solution.py:22
  15.7 2.6 %collective-permute-start.12 = (f32[6,8,256]{2,1,0:T(8,128)S(1)}, f32[6,8,256]{2,1,0:T(8,128)S(1)}, u32[]{:S(2)}, u32[]{:S(2)}) collective-permute-start(f32[6,8,256]{2,1,0:T(8,128)S(1)} %shard_map.48.q3), channel_id=1, source_target_pairs={{0,160},{32,192},{64,224},{96,0},{128,32},{160,64},{192,96},{224,1... | collective-permute-start | bytes 147464 | tf_op jit(solution)/shard_map/ppermute | solution.py:22
  18.7 2.2 %shard_map.39 = (f32[40,8,256]{2,1,0:T(8,128)S(1)}, f32[40,8,256]{2,1,0:T(8,128)S(1)}) custom-call(f32[32,256,128]{2,1,0:T(8,128)S(1)} %copy-done.1, f32[16,128,128]{2,1,0:T(8,128)S(1)} %get-tuple-element.31.g), custom_call_target="tpu_custom_call" | custom-call | flops 134217728 | bytes 6291456 | tf_op jit(solution)/shard_map/pallas_call | solution.py:424
  21.0 2.8 %collective-permute-start = (f32[40,8,256]{2,1,0:T(8,128)S(1)}, f32[40,8,256]{2,1,0:T(8,128)S(1)}, u32[]{:S(2)}, u32[]{:S(2)}) collective-permute-start(f32[40,8,256]{2,1,0:T(8,128)S(1)} %get-tuple-element.32), channel_id=1, source_target_pairs={{0,32},{32,64},{64,96},{96,128},{128,160},{160,192},{192,224},{224... | collective-permute-start | bytes 983048 | tf_op jit(solution)/shard_map/ppermute | solution.py:22
  23.9 5.4 %collective-permute-start.14 = (f32[8,128]{1,0:T(8,128)S(1)}, f32[8,128]{1,0:T(8,128)S(1)}, u32[]{:S(2)}, u32[]{:S(2)}) collective-permute-start(f32[8,128]{1,0:T(8,128)S(1)} %shard_map.49.p0), channel_id=1, source_target_pairs={{0,7},{1,0},{2,1},{3,2},{4,3},{5,4},{6,5},{7,6},{8,15},{9,8},{10,9... | collective-permute-start | bytes 12296 | tf_op jit(solution)/shard_map/ppermute | solution.py:22
  29.4 1.3 %collective-permute-done.14.sh = f32[8,128]{1,0:T(8,128)S(1)} collective-permute-done((f32[8,128]{1,0:T(8,128)S(1)}, f32[8,128]{1,0:T(8,128)S(1)}, u32[]{:S(2)}, u32[]{:S(2)}) %collective-permute-start.14) | collective-permute-done | bytes 4128 | tf_op jit(solution)/shard_map/ppermute | solution.py:22
  30.7 3.5 %collective-permute-done.13.sl = f32[8,128]{1,0:T(8,128)S(1)} collective-permute-done((f32[8,128]{1,0:T(8,128)S(1)}, f32[8,128]{1,0:T(8,128)S(1)}, u32[]{:S(2)}, u32[]{:S(2)}) %collective-permute-start.13) | collective-permute-done | bytes 4128 | tf_op jit(solution)/shard_map/ppermute | solution.py:22
  34.9 3.1 %collective-permute-start.15 = (f32[3,8,128]{2,1,0:T(8,128)S(1)}, f32[3,8,128]{2,1,0:T(8,128)S(1)}, u32[]{:S(2)}, u32[]{:S(2)}) collective-permute-start(f32[3,8,128]{2,1,0:T(8,128)S(1)} %shard_map.50.p3), channel_id=1, source_target_pairs={{0,3},{1,4},{2,5},{3,6},{4,7},{5,0},{6,1},{7,2},{8,11},{9,12},{10,... | collective-permute-start | bytes 36872 | tf_op jit(solution)/shard_map/ppermute | solution.py:22
  38.2 1.3 %collective-permute-start.8 = (f32[8,256,128]{2,1,0:T(8,128)S(1)}, f32[8,256,128]{2,1,0:T(8,128)S(1)}, u32[]{:S(2)}, u32[]{:S(2)}) collective-permute-start(f32[8,256,128]{2,1,0:T(8,128)S(1)} %get-tuple-element.49), channel_id=1, source_target_pairs={{0,7},{1,0},{2,1},{3,2},{4,3},{5,4},{6,5},{7,6},{8,15},{9,8},{10,9... | collective-permute-start | bytes 3145736 | tf_op jit(solution)/shard_map/ppermute | solution.py:22
  39.9 1.3 %shard_map.37 = (bf16[512,256]{1,0:T(8,128)(2,1)S(1)}, bf16[512,256]{1,0:T(8,128)(2,1)S(1)}, bf16[64,512]{1,0:T(8,128)(2,1)S(1)}, bf16[64,512]{1,0:T(8,128)(2,1)S(1)}) custom-call(f32[2,3,17]{2,1,0:T(4,128)S(1)} %copy.5.ft, f32[2,3,17]{2,1,0:T(4,128)S(1)} %copy.6.ct), custom_call_target="tpu_custom_call" | custom-call | flops 16777216 | bytes 1048576 | tf_op jit(solution)/shard_map/pallas_call | solution.py:424
  41.2 0.9 collective-permute-start.7
  43.1 2.7 %collective-permute-start.10 = (f32[148,8,128]{2,1,0:T(8,128)S(1)}, f32[148,8,128]{2,1,0:T(8,128)S(1)}, u32[]{:S(2)}, u32[]{:S(2)}) collective-permute-start(f32[148,8,128]{2,1,0:T(8,128)S(1)} %get-tuple-element.42), channel_id=1, source_target_pairs={{0,7},{1,0},{2,1},{3,2},{4,3},{5,4},{6,5},{7,6},{8,15},{9,8},{10,9... | collective-permute-start | bytes 1818632 | tf_op jit(solution)/shard_map/ppermute | solution.py:22
  45.7 3.7 %shard_map.40.e_in = f32[2,32,272,128]{3,2,1,0:T(8,128)S(1)} custom-call(bf16[512,256]{1,0:T(8,128)(2,1)S(1)} %get-tuple-element.29.wref, f32[32,256,128]{2,1,0:T(8,128)S(1)} %copy-done.1, f32[40,8,256]{2,1,0:T(8,128)S(1)} %collective-permute-done.xl, f32[40,8,256]{2,1,0:T(8,128)S(1)} %collective-permute-done.1.xr), custom_call_target="tpu_custom_call" | custom-call | flops 5368709120 | bytes 16777216 | tf_op jit(solution)/shard_map/pallas_call | solution.py:424
  49.7 6.5 %shard_map.46 = (bf16[2,8,272,256]{3,2,1,0:T(8,128)(2,1)S(1)}, bf16[2,8,272,256]{3,2,1,0:T(8,128)(2,1)S(1)}) custom-call(f32[2,3,17]{2,1,0:T(4,128)S(1)} %copy.5.ft, f32[2,32,272,128]{3,2,1,0:T(8,128)S(1)} %shard_map.42.e), custom_call_target="tpu_custom_call" | custom-call | flops 3221225472 | bytes 16777216 | tf_op jit(solution)/shard_map/pallas_call | solution.py:424
  56.2 7.4 %shard_map.43 = (f32[2,2,8,272,128]{4,3,2,1,0:T(8,128)S(1)}, f32[2,2,8,144,128]{4,3,2,1,0:T(8,128)S(1)}) custom-call(f32[2,3,17]{2,1,0:T(4,128)S(1)} %copy.5.ft, f32[2,3,17]{2,1,0:T(4,128)S(1)} %copy.6.ct, bf16[512,256]{1,0:T(8,128)(2,1)S(1)} %get-tuple-element.30.wcref, f32[2,32,272,128]{3,2,1,0:T(8,128)S(1)} %shard_map.42.e, ...), custom_call_target="tpu_custom_call" | custom-call | flops 3221225472 | bytes 16777216 | tf_op jit(solution)/shard_map/pallas_call | solution.py:424
  63.6 15.2 %collective-permute-done.9.sl = f32[148,8,128]{2,1,0:T(8,128)S(1)} collective-permute-done((f32[148,8,128]{2,1,0:T(8,128)S(1)}, f32[148,8,128]{2,1,0:T(8,128)S(1)}, u32[]{:S(2)}, u32[]{:S(2)}) %collective-permute-start.9) | collective-permute-done | bytes 606240 | tf_op jit(solution)/shard_map/ppermute | solution.py:22
  78.8 6.8 %shard_map.45 = (bf16[2,8,272,256]{3,2,1,0:T(8,128)(2,1)S(1)}, bf16[2,8,272,256]{3,2,1,0:T(8,128)(2,1)S(1)}, bf16[2,8,144,256]{3,2,1,0:T(8,128)(2,1)S(1)}, bf16[2,8,144,256]{3,2,1,0:T(8,128)(2,1)S(1)}) custom-call(f32[2,3,17]{2,1,0:T(4,128)S(1)} %copy.5.ft, f32[2,3,17]{2,1,0:T(4,128)S(1)} %copy.6.ct, bf16[512,256]{1,0:T(8,128)(2,1)S(1)} %get-tuple-element.29.wref, ...), custom_call_target="tpu_custom_call" | custom-call | flops 4294967296 | bytes 16777216 | tf_op jit(solution)/shard_map/pallas_call | solution.py:424
  85.6 5.1 %shard_map.52 = f32[32,256,128]{2,1,0:T(8,128)} custom-call(bf16[64,512]{1,0:T(8,128)(2,1)S(1)} %get-tuple-element.27.wyref, bf16[64,512]{1,0:T(8,128)(2,1)S(1)} %get-tuple-element.28.wycref, bf16[2,8,272,256]{3,2,1,0:T(8,128)(2,1)S(1)} %get-tuple-element.43.fh, bf16[2,8,272,256]{3,2,1,0:T(8,128)(2,1)S(1)} %get-tuple-element.44.fl, ...), custom_call_target="tpu_custom_call" | custom-call | flops 2147483648 | bytes 16777216 | tf_op jit(solution)/shard_map/pallas_call | solution.py:424
  (37 shorter events, 3.8 us)
Async XLA Ops:
  0.0 2.2 %copy-start = (f32[32,256,128]{2,1,0:T(8,128)S(1)}, f32[32,256,128]{2,1,0:T(8,128)}, u32[]{:S(2)}) copy-start(f32[32,256,128]{2,1,0:T(8,128)} %d.5) | copy-start | bytes 12582916
  2.2 16.5 %copy-start.1 = (f32[32,256,128]{2,1,0:T(8,128)S(1)}, f32[32,256,128]{2,1,0:T(8,128)}, u32[]{:S(2)}) copy-start(f32[32,256,128]{2,1,0:T(8,128)} %d.5) | copy-start | bytes 12582916
  2.7 9.3 %collective-permute-start.2 = (f32[49,8,128]{2,1,0:T(8,128)S(1)}, f32[49,8,128]{2,1,0:T(8,128)S(1)}, u32[]{:S(2)}, u32[]{:S(2)}) collective-permute-start(f32[49,8,128]{2,1,0:T(8,128)S(1)} %get-tuple-element.34), channel_id=1, source_target_pairs={{0,8},{8,16},{16,24},{24,0},{1,9},{9,17},{17,25},{25,1},{2,10},{10... | collective-permute-start | bytes 602120 | tf_op jit(solution)/shard_map/ppermute | solution.py:22
  4.2 7.7 %collective-permute-start.3 = (f32[49,8,128]{2,1,0:T(8,128)S(1)}, f32[49,8,128]{2,1,0:T(8,128)S(1)}, u32[]{:S(2)}, u32[]{:S(2)}) collective-permute-start(f32[49,8,128]{2,1,0:T(8,128)S(1)} %get-tuple-element.35), channel_id=1, source_target_pairs={{0,24},{8,0},{16,8},{24,16},{1,25},{9,1},{17,9},{25,17},{2,26},{10... | collective-permute-start | bytes 602120 | tf_op jit(solution)/shard_map/ppermute | solution.py:22
  5.9 6.0 %collective-permute-start.4 = (f32[8,128]{1,0:T(8,128)S(1)}, f32[8,128]{1,0:T(8,128)S(1)}, u32[]{:S(2)}, u32[]{:S(2)}) collective-permute-start(f32[8,128]{1,0:T(8,128)S(1)} %get-tuple-element.36.q), channel_id=1, source_target_pairs={{0,16},{8,24},{16,0},{24,8},{1,17},{9,25},{17,1},{25,9},{2,18},{10... | collective-permute-start | bytes 12296 | tf_op jit(solution)/shard_map/ppermute | solution.py:22
  12.2 3.4 %collective-permute-start.5 = (f32[5,8,256]{2,1,0:T(8,128)S(1)}, f32[5,8,256]{2,1,0:T(8,128)S(1)}, u32[]{:S(2)}, u32[]{:S(2)}) collective-permute-start(f32[5,8,256]{2,1,0:T(8,128)S(1)} %get-tuple-element.37), channel_id=1, source_target_pairs={{0,32},{32,64},{64,96},{96,128},{128,160},{160,192},{192,224},{224... | collective-permute-start | bytes 122888 | tf_op jit(solution)/shard_map/ppermute | solution.py:22
  12.3 3.4 %collective-permute-start.6 = (f32[5,8,256]{2,1,0:T(8,128)S(1)}, f32[5,8,256]{2,1,0:T(8,128)S(1)}, u32[]{:S(2)}, u32[]{:S(2)}) collective-permute-start(f32[5,8,256]{2,1,0:T(8,128)S(1)} %get-tuple-element.38.xlo), channel_id=1, source_target_pairs={{0,224},{32,0},{64,32},{96,64},{128,96},{160,128},{192,160},{224,1... | collective-permute-start | bytes 122888 | tf_op jit(solution)/shard_map/ppermute | solution.py:22
  15.7 8.1 %collective-permute-start.12 = (f32[6,8,256]{2,1,0:T(8,128)S(1)}, f32[6,8,256]{2,1,0:T(8,128)S(1)}, u32[]{:S(2)}, u32[]{:S(2)}) collective-permute-start(f32[6,8,256]{2,1,0:T(8,128)S(1)} %shard_map.48.q3), channel_id=1, source_target_pairs={{0,160},{32,192},{64,224},{96,0},{128,32},{160,64},{192,96},{224,1... | collective-permute-start | bytes 147464 | tf_op jit(solution)/shard_map/ppermute | solution.py:22
  18.3 5.5 %collective-permute-start.11 = (f32[6,8,256]{2,1,0:T(8,128)S(1)}, f32[6,8,256]{2,1,0:T(8,128)S(1)}, u32[]{:S(2)}, u32[]{:S(2)}) collective-permute-start(f32[6,8,256]{2,1,0:T(8,128)S(1)} %shard_map.48.q3), channel_id=1, source_target_pairs={{0,96},{32,128},{64,160},{96,192},{128,224},{160,0},{192,32},{224,... | collective-permute-start | bytes 147464 | tf_op jit(solution)/shard_map/ppermute | solution.py:22
  21.0 18.5 %copy-start.2 = (f32[2,3,17]{2,0,1:T(2,128)S(1)}, f32[2,3,17]{2,0,1:T(2,128)}, u32[]{:S(2)}) copy-start(f32[2,3,17]{2,0,1:T(2,128)} %param.4) | copy-start | bytes 1228
  21.0 18.5 %copy-start.3 = (f32[2,3,17]{2,0,1:T(2,128)S(1)}, f32[2,3,17]{2,0,1:T(2,128)}, u32[]{:S(2)}) copy-start(f32[2,3,17]{2,0,1:T(2,128)} %param.5) | copy-start | bytes 1228
  21.0 21.3 %collective-permute-start = (f32[40,8,256]{2,1,0:T(8,128)S(1)}, f32[40,8,256]{2,1,0:T(8,128)S(1)}, u32[]{:S(2)}, u32[]{:S(2)}) collective-permute-start(f32[40,8,256]{2,1,0:T(8,128)S(1)} %get-tuple-element.32), channel_id=1, source_target_pairs={{0,32},{32,64},{64,96},{96,128},{128,160},{160,192},{192,224},{224... | collective-permute-start | bytes 983048 | tf_op jit(solution)/shard_map/ppermute | solution.py:22
  23.8 18.5 %collective-permute-start.1 = (f32[40,8,256]{2,1,0:T(8,128)S(1)}, f32[40,8,256]{2,1,0:T(8,128)S(1)}, u32[]{:S(2)}, u32[]{:S(2)}) collective-permute-start(f32[40,8,256]{2,1,0:T(8,128)S(1)} %get-tuple-element.33), channel_id=1, source_target_pairs={{0,224},{32,0},{64,32},{96,64},{128,96},{160,128},{192,160},{224,1... | collective-permute-start | bytes 983048 | tf_op jit(solution)/shard_map/ppermute | solution.py:22
  23.9 6.8 %collective-permute-start.14 = (f32[8,128]{1,0:T(8,128)S(1)}, f32[8,128]{1,0:T(8,128)S(1)}, u32[]{:S(2)}, u32[]{:S(2)}) collective-permute-start(f32[8,128]{1,0:T(8,128)S(1)} %shard_map.49.p0), channel_id=1, source_target_pairs={{0,7},{1,0},{2,1},{3,2},{4,3},{5,4},{6,5},{7,6},{8,15},{9,8},{10,9... | collective-permute-start | bytes 12296 | tf_op jit(solution)/shard_map/ppermute | solution.py:22
  29.4 4.8 %collective-permute-start.13 = (f32[8,128]{1,0:T(8,128)S(1)}, f32[8,128]{1,0:T(8,128)S(1)}, u32[]{:S(2)}, u32[]{:S(2)}) collective-permute-start(f32[8,128]{1,0:T(8,128)S(1)} %shard_map.49.p0), channel_id=1, source_target_pairs={{0,1},{1,2},{2,3},{3,4},{4,5},{5,6},{6,7},{7,0},{8,9},{9,10},{10,1... | collective-permute-start | bytes 12296 | tf_op jit(solution)/shard_map/ppermute | solution.py:22
  34.2 7.1 %collective-permute-start.16 = (f32[3,8,128]{2,1,0:T(8,128)S(1)}, f32[3,8,128]{2,1,0:T(8,128)S(1)}, u32[]{:S(2)}, u32[]{:S(2)}) collective-permute-start(f32[3,8,128]{2,1,0:T(8,128)S(1)} %shard_map.50.p3), channel_id=1, source_target_pairs={{0,5},{1,6},{2,7},{3,0},{4,1},{5,2},{6,3},{7,4},{8,13},{9,14},{10,... | collective-permute-start | bytes 36872 | tf_op jit(solution)/shard_map/ppermute | solution.py:22
  34.9 7.3 %collective-permute-start.15 = (f32[3,8,128]{2,1,0:T(8,128)S(1)}, f32[3,8,128]{2,1,0:T(8,128)S(1)}, u32[]{:S(2)}, u32[]{:S(2)}) collective-permute-start(f32[3,8,128]{2,1,0:T(8,128)S(1)} %shard_map.50.p3), channel_id=1, source_target_pairs={{0,3},{1,4},{2,5},{3,6},{4,7},{5,0},{6,1},{7,2},{8,11},{9,12},{10,... | collective-permute-start | bytes 36872 | tf_op jit(solution)/shard_map/ppermute | solution.py:22
  38.2 40.6 %collective-permute-start.8 = (f32[8,256,128]{2,1,0:T(8,128)S(1)}, f32[8,256,128]{2,1,0:T(8,128)S(1)}, u32[]{:S(2)}, u32[]{:S(2)}) collective-permute-start(f32[8,256,128]{2,1,0:T(8,128)S(1)} %get-tuple-element.49), channel_id=1, source_target_pairs={{0,7},{1,0},{2,1},{3,2},{4,3},{5,4},{6,5},{7,6},{8,15},{9,8},{10,9... | collective-permute-start | bytes 3145736 | tf_op jit(solution)/shard_map/ppermute | solution.py:22
  41.2 37.6 %collective-permute-start.7 = (f32[8,256,128]{2,1,0:T(8,128)S(1)}, f32[8,256,128]{2,1,0:T(8,128)S(1)}, u32[]{:S(2)}, u32[]{:S(2)}) collective-permute-start(f32[8,256,128]{2,1,0:T(8,128)S(1)} %get-tuple-element.50), channel_id=1, source_target_pairs={{0,1},{1,2},{2,3},{3,4},{4,5},{5,6},{6,7},{7,0},{8,9},{9,10},{10,1... | collective-permute-start | bytes 3145736 | tf_op jit(solution)/shard_map/ppermute | solution.py:22
  42.4 36.4 %collective-permute-start.9 = (f32[148,8,128]{2,1,0:T(8,128)S(1)}, f32[148,8,128]{2,1,0:T(8,128)S(1)}, u32[]{:S(2)}, u32[]{:S(2)}) collective-permute-start(f32[148,8,128]{2,1,0:T(8,128)S(1)} %get-tuple-element.41), channel_id=1, source_target_pairs={{0,1},{1,2},{2,3},{3,4},{4,5},{5,6},{6,7},{7,0},{8,9},{9,10},{10,1... | collective-permute-start | bytes 1818632 | tf_op jit(solution)/shard_map/ppermute | solution.py:22
  43.1 35.7 %collective-permute-start.10 = (f32[148,8,128]{2,1,0:T(8,128)S(1)}, f32[148,8,128]{2,1,0:T(8,128)S(1)}, u32[]{:S(2)}, u32[]{:S(2)}) collective-permute-start(f32[148,8,128]{2,1,0:T(8,128)S(1)} %get-tuple-element.42), channel_id=1, source_target_pairs={{0,7},{1,0},{2,1},{3,2},{4,3},{5,4},{6,5},{7,6},{8,15},{9,8},{10,9... | collective-permute-start | bytes 1818632 | tf_op jit(solution)/shard_map/ppermute | solution.py:22

commit v6 on v5

--- a/solution.py
+++ b/solution.py
@@ -155,7 +155,7 @@
 
     own[...] = jnp.concatenate(
         sum((quarters(q3, i) for i in range(3)), [])
-        + quarters(qm, 1) + quarters(qm, 0) + quarters(qm, 2) + quarters(qp, 1) + quarters(qp, 0),
+        + quarters(qm, 1) + quarters(qm, 0) + quarters(qm, 2) + quarters(qp, 0) + quarters(qp, 2),
         axis=1,
     )
 
@@ -465,7 +465,7 @@
 
 
 def top_kernel(k, p3, pm, pp, tp):
-    tiles = [p3[0], p3[1], p3[2], pm[1], pm[0], pm[2], pp[1], pp[0]]
+    tiles = [p3[0], p3[1], p3[2], pm[1], pm[0], pm[2], pp[0], pp[2]]
     lane = iota((8, 128), 1) >> 5
     out = jnp.zeros((8, 128), f32)
     for x in range(4):
@@ -528,7 +528,7 @@
     sl = shift(zhi, "gz", 1)
     sh = shift(zlo, "gz", -1)
     qm = shift(q3, "gx", 3)
-    qp = shift(q3, "gx", -3)
+    qp = shift(q3, "gx", -2)
 
     e = call(
         own_fine_kernel, sds(2, 32, 272, 128), 0,
@@ -551,7 +551,7 @@
     )
     p3 = call(p3_kernel, sds(3, 8, 128), 0, (p0, pl1, pr1))
     pm = shift(p3, "gz", 3)
-    pp = shift(p3, "gz", -3)
+    pp = shift(p3, "gz", -2)
     fh, fl, fch, fcl = call(
         outer_kernel, (half, half, quarter, quarter), 2, (ft, ct, w, wc, pa, pc, zl, zh, sl, sh),
         scratch=[

time: 90.9 us -> 92 us (1.012)
  the two profiles are of different devices: /device:TPU:6 before, /device:TPU:1 now
where the time goes in v6:
time: 92 us; the launch traced here: 90.9 us
  Pallas kernels  34.8 us (38%)
  waiting for transfers between devices  28.7 us (31%)
  starting transfers between devices  24.6 us (27%)
  local copies, waits for them, and re-layouts  2.38 us (3%)
    pallas_call x16, Pallas kernels, call(): pl.pallas_call(kernel, out_shape=outs, in_specs=[SM] * n_smem + [VM] * (l...  34.8 us
    ppermute x17, waiting for transfers between devices, shift(): lax.ppermute(value, axis, [(i, (i + step) % count) for i in range(count)])  28.7 us
    ppermute x17, starting transfers between devices, shift(): lax.ppermute(value, axis, [(i, (i + step) % count) for i in range(count)])  24.6 us
    unnamed x10, local copies, waits for them, and re-layouts  2.21 us
  transfers between devices with their start and end apart: 17, of which 7 were waited for; matrix products, arithmetic and copies ran while one was open for 0% of the time, Pallas kernels for 24%

profile of v6, /device:TPU:1, one launch (start us, length us, event | category | flops | bytes accessed | tf_op | source)
XLA Modules:
  0.0 90.9 jit_solution(4867046003764023419)
XLA Ops:
  0.0 2.2 %copy-done = f32[32,256,128]{2,1,0:T(8,128)S(1)} copy-done((f32[32,256,128]{2,1,0:T(8,128)S(1)}, f32[32,256,128]{2,1,0:T(8,128)}, u32[]{:S(2)}) %copy-start) | copy-done | bytes 4194328
  2.7 2.1 %collective-permute-start.2 = (f32[49,8,128]{2,1,0:T(8,128)S(1)}, f32[49,8,128]{2,1,0:T(8,128)S(1)}, u32[]{:S(2)}, u32[]{:S(2)}) collective-permute-start(f32[49,8,128]{2,1,0:T(8,128)S(1)} %get-tuple-element.34), channel_id=1, source_target_pairs={{0,8},{8,16},{16,24},{24,0},{1,9},{9,17},{17,25},{25,1},{2,10},{10... | collective-permute-start | bytes 602120 | tf_op jit(solution)/shard_map/ppermute | solution.py:22
  4.8 1.5 %collective-permute-start.3 = (f32[49,8,128]{2,1,0:T(8,128)S(1)}, f32[49,8,128]{2,1,0:T(8,128)S(1)}, u32[]{:S(2)}, u32[]{:S(2)}) collective-permute-start(f32[49,8,128]{2,1,0:T(8,128)S(1)} %get-tuple-element.35), channel_id=1, source_target_pairs={{0,24},{8,0},{16,8},{24,16},{1,25},{9,1},{17,9},{25,17},{2,26},{10... | collective-permute-start | bytes 602120 | tf_op jit(solution)/shard_map/ppermute | solution.py:22
  6.3 1.6 %collective-permute-start.4 = (f32[8,128]{1,0:T(8,128)S(1)}, f32[8,128]{1,0:T(8,128)S(1)}, u32[]{:S(2)}, u32[]{:S(2)}) collective-permute-start(f32[8,128]{1,0:T(8,128)S(1)} %get-tuple-element.36.q), channel_id=1, source_target_pairs={{0,16},{8,24},{16,0},{24,8},{1,17},{9,25},{17,1},{25,9},{2,18},{10... | collective-permute-start | bytes 12296 | tf_op jit(solution)/shard_map/ppermute | solution.py:22
  7.9 3.7 %collective-permute-done.4.q2 = f32[8,128]{1,0:T(8,128)S(1)} collective-permute-done((f32[8,128]{1,0:T(8,128)S(1)}, f32[8,128]{1,0:T(8,128)S(1)}, u32[]{:S(2)}, u32[]{:S(2)}) %collective-permute-start.4) | collective-permute-done | bytes 4128 | tf_op jit(solution)/shard_map/ppermute | solution.py:22
  11.9 2.9 %collective-permute-start.5 = (f32[5,8,256]{2,1,0:T(8,128)S(1)}, f32[5,8,256]{2,1,0:T(8,128)S(1)}, u32[]{:S(2)}, u32[]{:S(2)}) collective-permute-start(f32[5,8,256]{2,1,0:T(8,128)S(1)} %get-tuple-element.37), channel_id=1, source_target_pairs={{0,32},{32,64},{64,96},{96,128},{128,160},{160,192},{192,224},{224... | collective-permute-start | bytes 122888 | tf_op jit(solution)/shard_map/ppermute | solution.py:22
  14.9 1.1 %collective-permute-done.5.cl.xl = f32[5,8,256]{2,1,0:T(8,128)S(1)} collective-permute-done((f32[5,8,256]{2,1,0:T(8,128)S(1)}, f32[5,8,256]{2,1,0:T(8,128)S(1)}, u32[]{:S(2)}, u32[]{:S(2)}) %collective-permute-start.5) | collective-permute-done | bytes 40992 | tf_op jit(solution)/shard_map/ppermute | solution.py:22
  16.0 2.6 %collective-permute-done.6.cr.xr = f32[5,8,256]{2,1,0:T(8,128)S(1)} collective-permute-done((f32[5,8,256]{2,1,0:T(8,128)S(1)}, f32[5,8,256]{2,1,0:T(8,128)S(1)}, u32[]{:S(2)}, u32[]{:S(2)}) %collective-permute-start.6) | collective-permute-done | bytes 40992 | tf_op jit(solution)/shard_map/ppermute | solution.py:22
  18.6 3.2 %collective-permute-start.12 = (f32[6,8,256]{2,1,0:T(8,128)S(1)}, f32[6,8,256]{2,1,0:T(8,128)S(1)}, u32[]{:S(2)}, u32[]{:S(2)}) collective-permute-start(f32[6,8,256]{2,1,0:T(8,128)S(1)} %shard_map.48.q3), channel_id=1, source_target_pairs={{0,192},{32,224},{64,0},{96,32},{128,64},{160,96},{192,128},{224,1... | collective-permute-start | bytes 147464 | tf_op jit(solution)/shard_map/ppermute | solution.py:22
  21.8 2.2 %shard_map.39 = (f32[40,8,256]{2,1,0:T(8,128)S(1)}, f32[40,8,256]{2,1,0:T(8,128)S(1)}) custom-call(f32[32,256,128]{2,1,0:T(8,128)S(1)} %copy-done.1, f32[16,128,128]{2,1,0:T(8,128)S(1)} %get-tuple-element.31.g), custom_call_target="tpu_custom_call" | custom-call | flops 134217728 | bytes 6291456 | tf_op jit(solution)/shard_map/pallas_call | solution.py:424
  24.5 1.9 %collective-permute-done.11.qm = f32[6,8,256]{2,1,0:T(8,128)S(1)} collective-permute-done((f32[6,8,256]{2,1,0:T(8,128)S(1)}, f32[6,8,256]{2,1,0:T(8,128)S(1)}, u32[]{:S(2)}, u32[]{:S(2)}) %collective-permute-start.11) | collective-permute-done | bytes 49184 | tf_op jit(solution)/shard_map/ppermute | solution.py:22
  26.6 4.9 %collective-permute-start.14 = (f32[8,128]{1,0:T(8,128)S(1)}, f32[8,128]{1,0:T(8,128)S(1)}, u32[]{:S(2)}, u32[]{:S(2)}) collective-permute-start(f32[8,128]{1,0:T(8,128)S(1)} %shard_map.49.p0), channel_id=1, source_target_pairs={{0,7},{1,0},{2,1},{3,2},{4,3},{5,4},{6,5},{7,6},{8,15},{9,8},{10,9... | collective-permute-start | bytes 12296 | tf_op jit(solution)/shard_map/ppermute | solution.py:22
  31.4 0.8 collective-permute-done.14.sh
  32.2 2.9 %collective-permute-done.13.sl = f32[8,128]{1,0:T(8,128)S(1)} collective-permute-done((f32[8,128]{1,0:T(8,128)S(1)}, f32[8,128]{1,0:T(8,128)S(1)}, u32[]{:S(2)}, u32[]{:S(2)}) %collective-permute-start.13) | collective-permute-done | bytes 4128 | tf_op jit(solution)/shard_map/ppermute | solution.py:22
  35.4 0.6 collective-permute-start.15
  36.2 4.0 %collective-permute-start.8 = (f32[8,256,128]{2,1,0:T(8,128)S(1)}, f32[8,256,128]{2,1,0:T(8,128)S(1)}, u32[]{:S(2)}, u32[]{:S(2)}) collective-permute-start(f32[8,256,128]{2,1,0:T(8,128)S(1)} %get-tuple-element.49), channel_id=1, source_target_pairs={{0,7},{1,0},{2,1},{3,2},{4,3},{5,4},{6,5},{7,6},{8,15},{9,8},{10,9... | collective-permute-start | bytes 3145736 | tf_op jit(solution)/shard_map/ppermute | solution.py:22
  40.5 1.3 %shard_map.37 = (bf16[512,256]{1,0:T(8,128)(2,1)S(1)}, bf16[512,256]{1,0:T(8,128)(2,1)S(1)}, bf16[64,512]{1,0:T(8,128)(2,1)S(1)}, bf16[64,512]{1,0:T(8,128)(2,1)S(1)}) custom-call(f32[2,3,17]{2,1,0:T(4,128)S(1)} %copy.5.ft, f32[2,3,17]{2,1,0:T(4,128)S(1)} %copy.6.ct), custom_call_target="tpu_custom_call" | custom-call | flops 16777216 | bytes 1048576 | tf_op jit(solution)/shard_map/pallas_call | solution.py:424
  42.4 2.9 %collective-permute-start.10 = (f32[148,8,128]{2,1,0:T(8,128)S(1)}, f32[148,8,128]{2,1,0:T(8,128)S(1)}, u32[]{:S(2)}, u32[]{:S(2)}) collective-permute-start(f32[148,8,128]{2,1,0:T(8,128)S(1)} %get-tuple-element.42), channel_id=1, source_target_pairs={{0,7},{1,0},{2,1},{3,2},{4,3},{5,4},{6,5},{7,6},{8,15},{9,8},{10,9... | collective-permute-start | bytes 1818632 | tf_op jit(solution)/shard_map/ppermute | solution.py:22
  45.3 3.7 %shard_map.40.e_in = f32[2,32,272,128]{3,2,1,0:T(8,128)S(1)} custom-call(bf16[512,256]{1,0:T(8,128)(2,1)S(1)} %get-tuple-element.29.wref, f32[32,256,128]{2,1,0:T(8,128)S(1)} %copy-done.1, f32[40,8,256]{2,1,0:T(8,128)S(1)} %collective-permute-done.xl, f32[40,8,256]{2,1,0:T(8,128)S(1)} %collective-permute-done.1.xr), custom_call_target="tpu_custom_call" | custom-call | flops 5368709120 | bytes 16777216 | tf_op jit(solution)/shard_map/pallas_call | solution.py:424
  49.2 6.5 %shard_map.46 = (bf16[2,8,272,256]{3,2,1,0:T(8,128)(2,1)S(1)}, bf16[2,8,272,256]{3,2,1,0:T(8,128)(2,1)S(1)}) custom-call(f32[2,3,17]{2,1,0:T(4,128)S(1)} %copy.5.ft, f32[2,32,272,128]{3,2,1,0:T(8,128)S(1)} %shard_map.42.e), custom_call_target="tpu_custom_call" | custom-call | flops 3221225472 | bytes 16777216 | tf_op jit(solution)/shard_map/pallas_call | solution.py:424
  55.7 7.4 %shard_map.43 = (f32[2,2,8,272,128]{4,3,2,1,0:T(8,128)S(1)}, f32[2,2,8,144,128]{4,3,2,1,0:T(8,128)S(1)}) custom-call(f32[2,3,17]{2,1,0:T(4,128)S(1)} %copy.5.ft, f32[2,3,17]{2,1,0:T(4,128)S(1)} %copy.6.ct, bf16[512,256]{1,0:T(8,128)(2,1)S(1)} %get-tuple-element.30.wcref, f32[2,32,272,128]{3,2,1,0:T(8,128)S(1)} %shard_map.42.e, ...), custom_call_target="tpu_custom_call" | custom-call | flops 3221225472 | bytes 16777216 | tf_op jit(solution)/shard_map/pallas_call | solution.py:424
  63.2 15.7 %collective-permute-done.9.sl = f32[148,8,128]{2,1,0:T(8,128)S(1)} collective-permute-done((f32[148,8,128]{2,1,0:T(8,128)S(1)}, f32[148,8,128]{2,1,0:T(8,128)S(1)}, u32[]{:S(2)}, u32[]{:S(2)}) %collective-permute-start.9) | collective-permute-done | bytes 606240 | tf_op jit(solution)/shard_map/ppermute | solution.py:22
  78.8 6.8 %shard_map.45 = (bf16[2,8,272,256]{3,2,1,0:T(8,128)(2,1)S(1)}, bf16[2,8,272,256]{3,2,1,0:T(8,128)(2,1)S(1)}, bf16[2,8,144,256]{3,2,1,0:T(8,128)(2,1)S(1)}, bf16[2,8,144,256]{3,2,1,0:T(8,128)(2,1)S(1)}) custom-call(f32[2,3,17]{2,1,0:T(4,128)S(1)} %copy.5.ft, f32[2,3,17]{2,1,0:T(4,128)S(1)} %copy.6.ct, bf16[512,256]{1,0:T(8,128)(2,1)S(1)} %get-tuple-element.29.wref, ...), custom_call_target="tpu_custom_call" | custom-call | flops 4294967296 | bytes 16777216 | tf_op jit(solution)/shard_map/pallas_call | solution.py:424
  85.6 5.1 %shard_map.52 = f32[32,256,128]{2,1,0:T(8,128)} custom-call(bf16[64,512]{1,0:T(8,128)(2,1)S(1)} %get-tuple-element.27.wyref, bf16[64,512]{1,0:T(8,128)(2,1)S(1)} %get-tuple-element.28.wycref, bf16[2,8,272,256]{3,2,1,0:T(8,128)(2,1)S(1)} %get-tuple-element.43.fh, bf16[2,8,272,256]{3,2,1,0:T(8,128)(2,1)S(1)} %get-tuple-element.44.fl, ...), custom_call_target="tpu_custom_call" | custom-call | flops 2147483648 | bytes 16777216 | tf_op jit(solution)/shard_map/pallas_call | solution.py:424
  (37 shorter events, 3.1 us)
Async XLA Ops:
  0.0 2.2 %copy-start = (f32[32,256,128]{2,1,0:T(8,128)S(1)}, f32[32,256,128]{2,1,0:T(8,128)}, u32[]{:S(2)}) copy-start(f32[32,256,128]{2,1,0:T(8,128)} %d.5) | copy-start | bytes 12582916
  2.2 19.6 %copy-start.1 = (f32[32,256,128]{2,1,0:T(8,128)S(1)}, f32[32,256,128]{2,1,0:T(8,128)}, u32[]{:S(2)}) copy-start(f32[32,256,128]{2,1,0:T(8,128)} %d.5) | copy-start | bytes 12582916
  2.7 8.9 %collective-permute-start.2 = (f32[49,8,128]{2,1,0:T(8,128)S(1)}, f32[49,8,128]{2,1,0:T(8,128)S(1)}, u32[]{:S(2)}, u32[]{:S(2)}) collective-permute-start(f32[49,8,128]{2,1,0:T(8,128)S(1)} %get-tuple-element.34), channel_id=1, source_target_pairs={{0,8},{8,16},{16,24},{24,0},{1,9},{9,17},{17,25},{25,1},{2,10},{10... | collective-permute-start | bytes 602120 | tf_op jit(solution)/shard_map/ppermute | solution.py:22
  4.8 6.8 %collective-permute-start.3 = (f32[49,8,128]{2,1,0:T(8,128)S(1)}, f32[49,8,128]{2,1,0:T(8,128)S(1)}, u32[]{:S(2)}, u32[]{:S(2)}) collective-permute-start(f32[49,8,128]{2,1,0:T(8,128)S(1)} %get-tuple-element.35), channel_id=1, source_target_pairs={{0,24},{8,0},{16,8},{24,16},{1,25},{9,1},{17,9},{25,17},{2,26},{10... | collective-permute-start | bytes 602120 | tf_op jit(solution)/shard_map/ppermute | solution.py:22
  6.3 5.3 %collective-permute-start.4 = (f32[8,128]{1,0:T(8,128)S(1)}, f32[8,128]{1,0:T(8,128)S(1)}, u32[]{:S(2)}, u32[]{:S(2)}) collective-permute-start(f32[8,128]{1,0:T(8,128)S(1)} %get-tuple-element.36.q), channel_id=1, source_target_pairs={{0,16},{8,24},{16,0},{24,8},{1,17},{9,25},{17,1},{25,9},{2,18},{10... | collective-permute-start | bytes 12296 | tf_op jit(solution)/shard_map/ppermute | solution.py:22
  11.9 4.0 %collective-permute-start.5 = (f32[5,8,256]{2,1,0:T(8,128)S(1)}, f32[5,8,256]{2,1,0:T(8,128)S(1)}, u32[]{:S(2)}, u32[]{:S(2)}) collective-permute-start(f32[5,8,256]{2,1,0:T(8,128)S(1)} %get-tuple-element.37), channel_id=1, source_target_pairs={{0,32},{32,64},{64,96},{96,128},{128,160},{160,192},{192,224},{224... | collective-permute-start | bytes 122888 | tf_op jit(solution)/shard_map/ppermute | solution.py:22
  14.8 3.7 %collective-permute-start.6 = (f32[5,8,256]{2,1,0:T(8,128)S(1)}, f32[5,8,256]{2,1,0:T(8,128)S(1)}, u32[]{:S(2)}, u32[]{:S(2)}) collective-permute-start(f32[5,8,256]{2,1,0:T(8,128)S(1)} %get-tuple-element.38.xlo), channel_id=1, source_target_pairs={{0,224},{32,0},{64,32},{96,64},{128,96},{160,128},{192,160},{224,1... | collective-permute-start | bytes 122888 | tf_op jit(solution)/shard_map/ppermute | solution.py:22
  18.6 6.0 %collective-permute-start.12 = (f32[6,8,256]{2,1,0:T(8,128)S(1)}, f32[6,8,256]{2,1,0:T(8,128)S(1)}, u32[]{:S(2)}, u32[]{:S(2)}) collective-permute-start(f32[6,8,256]{2,1,0:T(8,128)S(1)} %shard_map.48.q3), channel_id=1, source_target_pairs={{0,192},{32,224},{64,0},{96,32},{128,64},{160,96},{192,128},{224,1... | collective-permute-start | bytes 147464 | tf_op jit(solution)/shard_map/ppermute | solution.py:22
  21.7 4.7 %collective-permute-start.11 = (f32[6,8,256]{2,1,0:T(8,128)S(1)}, f32[6,8,256]{2,1,0:T(8,128)S(1)}, u32[]{:S(2)}, u32[]{:S(2)}) collective-permute-start(f32[6,8,256]{2,1,0:T(8,128)S(1)} %shard_map.48.q3), channel_id=1, source_target_pairs={{0,96},{32,128},{64,160},{96,192},{128,224},{160,0},{192,32},{224,... | collective-permute-start | bytes 147464 | tf_op jit(solution)/shard_map/ppermute | solution.py:22
  24.0 16.1 %copy-start.2 = (f32[2,3,17]{2,0,1:T(2,128)S(1)}, f32[2,3,17]{2,0,1:T(2,128)}, u32[]{:S(2)}) copy-start(f32[2,3,17]{2,0,1:T(2,128)} %param.4) | copy-start | bytes 1228
  24.0 16.1 %copy-start.3 = (f32[2,3,17]{2,0,1:T(2,128)S(1)}, f32[2,3,17]{2,0,1:T(2,128)}, u32[]{:S(2)}) copy-start(f32[2,3,17]{2,0,1:T(2,128)} %param.5) | copy-start | bytes 1228
  24.0 18.2 %collective-permute-start = (f32[40,8,256]{2,1,0:T(8,128)S(1)}, f32[40,8,256]{2,1,0:T(8,128)S(1)}, u32[]{:S(2)}, u32[]{:S(2)}) collective-permute-start(f32[40,8,256]{2,1,0:T(8,128)S(1)} %get-tuple-element.32), channel_id=1, source_target_pairs={{0,32},{32,64},{64,96},{96,128},{128,160},{160,192},{192,224},{224... | collective-permute-start | bytes 983048 | tf_op jit(solution)/shard_map/ppermute | solution.py:22
  24.0 18.1 %collective-permute-start.1 = (f32[40,8,256]{2,1,0:T(8,128)S(1)}, f32[40,8,256]{2,1,0:T(8,128)S(1)}, u32[]{:S(2)}, u32[]{:S(2)}) collective-permute-start(f32[40,8,256]{2,1,0:T(8,128)S(1)} %get-tuple-element.33), channel_id=1, source_target_pairs={{0,224},{32,0},{64,32},{96,64},{128,96},{160,128},{192,160},{224,1... | collective-permute-start | bytes 983048 | tf_op jit(solution)/shard_map/ppermute | solution.py:22
  26.6 5.6 %collective-permute-start.14 = (f32[8,128]{1,0:T(8,128)S(1)}, f32[8,128]{1,0:T(8,128)S(1)}, u32[]{:S(2)}, u32[]{:S(2)}) collective-permute-start(f32[8,128]{1,0:T(8,128)S(1)} %shard_map.49.p0), channel_id=1, source_target_pairs={{0,7},{1,0},{2,1},{3,2},{4,3},{5,4},{6,5},{7,6},{8,15},{9,8},{10,9... | collective-permute-start | bytes 12296 | tf_op jit(solution)/shard_map/ppermute | solution.py:22
  31.4 3.7 %collective-permute-start.13 = (f32[8,128]{1,0:T(8,128)S(1)}, f32[8,128]{1,0:T(8,128)S(1)}, u32[]{:S(2)}, u32[]{:S(2)}) collective-permute-start(f32[8,128]{1,0:T(8,128)S(1)} %shard_map.49.p0), channel_id=1, source_target_pairs={{0,1},{1,2},{2,3},{3,4},{4,5},{5,6},{6,7},{7,0},{8,9},{9,10},{10,1... | collective-permute-start | bytes 12296 | tf_op jit(solution)/shard_map/ppermute | solution.py:22
  35.1 6.8 %collective-permute-start.16 = (f32[3,8,128]{2,1,0:T(8,128)S(1)}, f32[3,8,128]{2,1,0:T(8,128)S(1)}, u32[]{:S(2)}, u32[]{:S(2)}) collective-permute-start(f32[3,8,128]{2,1,0:T(8,128)S(1)} %shard_map.50.p3), channel_id=1, source_target_pairs={{0,6},{1,7},{2,0},{3,1},{4,2},{5,3},{6,4},{7,5},{8,14},{9,15},{10,... | collective-permute-start | bytes 36872 | tf_op jit(solution)/shard_map/ppermute | solution.py:22
  35.4 6.6 %collective-permute-start.15 = (f32[3,8,128]{2,1,0:T(8,128)S(1)}, f32[3,8,128]{2,1,0:T(8,128)S(1)}, u32[]{:S(2)}, u32[]{:S(2)}) collective-permute-start(f32[3,8,128]{2,1,0:T(8,128)S(1)} %shard_map.50.p3), channel_id=1, source_target_pairs={{0,3},{1,4},{2,5},{3,6},{4,7},{5,0},{6,1},{7,2},{8,11},{9,12},{10,... | collective-permute-start | bytes 36872 | tf_op jit(solution)/shard_map/ppermute | solution.py:22
  36.2 42.7 %collective-permute-start.8 = (f32[8,256,128]{2,1,0:T(8,128)S(1)}, f32[8,256,128]{2,1,0:T(8,128)S(1)}, u32[]{:S(2)}, u32[]{:S(2)}) collective-permute-start(f32[8,256,128]{2,1,0:T(8,128)S(1)} %get-tuple-element.49), channel_id=1, source_target_pairs={{0,7},{1,0},{2,1},{3,2},{4,3},{5,4},{6,5},{7,6},{8,15},{9,8},{10,9... | collective-permute-start | bytes 3145736 | tf_op jit(solution)/shard_map/ppermute | solution.py:22
  41.9 36.9 %collective-permute-start.7 = (f32[8,256,128]{2,1,0:T(8,128)S(1)}, f32[8,256,128]{2,1,0:T(8,128)S(1)}, u32[]{:S(2)}, u32[]{:S(2)}) collective-permute-start(f32[8,256,128]{2,1,0:T(8,128)S(1)} %get-tuple-element.50), channel_id=1, source_target_pairs={{0,1},{1,2},{2,3},{3,4},{4,5},{5,6},{6,7},{7,0},{8,9},{9,10},{10,1... | collective-permute-start | bytes 3145736 | tf_op jit(solution)/shard_map/ppermute | solution.py:22
  42.3 36.5 %collective-permute-start.9 = (f32[148,8,128]{2,1,0:T(8,128)S(1)}, f32[148,8,128]{2,1,0:T(8,128)S(1)}, u32[]{:S(2)}, u32[]{:S(2)}) collective-permute-start(f32[148,8,128]{2,1,0:T(8,128)S(1)} %get-tuple-element.41), channel_id=1, source_target_pairs={{0,1},{1,2},{2,3},{3,4},{4,5},{5,6},{6,7},{7,0},{8,9},{9,10},{10,1... | collective-permute-start | bytes 1818632 | tf_op jit(solution)/shard_map/ppermute | solution.py:22
  42.4 36.4 %collective-permute-start.10 = (f32[148,8,128]{2,1,0:T(8,128)S(1)}, f32[148,8,128]{2,1,0:T(8,128)S(1)}, u32[]{:S(2)}, u32[]{:S(2)}) collective-permute-start(f32[148,8,128]{2,1,0:T(8,128)S(1)} %get-tuple-element.42), channel_id=1, source_target_pairs={{0,7},{1,0},{2,1},{3,2},{4,3},{5,4},{6,5},{7,6},{8,15},{9,8},{10,9... | collective-permute-start | bytes 1818632 | tf_op jit(solution)/shard_map/ppermute | solution.py:22
